TPU v7x, 32 devices: a whole 2x2x4 slice. The times are simulated.
32 devices in a mesh: ctx: 16 (over z, y, core), fsdp: 2 (over x).
Axes of the slice: x: 2, y: 2, z: 4, core: 2. Of those that a mesh axis runs over, the one named last changes fastest.
Arguments:
- tokens: bfloat16 [8192, 768], P(('ctx', 'fsdp')), may hold values from -6 to 6
- cotangent: bfloat16 [8192, 768], P(('ctx', 'fsdp')), may hold values from -6 to 6
- doc_lengths: int32 [4], replicated, may hold values from 1 to 4096, 8192 in all
- deal: int32 [64], replicated, may hold values from 0 to 63, each once
- first_gain: bfloat16 [768], P('fsdp'), may hold values from 0.5 to 1.5
- first_shift: bfloat16 [768], P('fsdp'), may hold values from -4 to 4
- query_weight: bfloat16 [768, 768], P('fsdp'), may hold values from -0.21875 to 0.21875
- query_bias: bfloat16 [768], P('fsdp'), may hold values from -6 to 6
- key_weight: bfloat16 [768, 768], P('fsdp'), may hold values from -0.21875 to 0.21875
- value_weight: bfloat16 [768, 768], P('fsdp'), may hold values from -0.21875 to 0.21875
- value_bias: bfloat16 [768], P('fsdp'), may hold values from -0.75 to 0.75
- output_weight: bfloat16 [768, 768], P('fsdp'), may hold values from -3.5 to 3.5
- output_bias: bfloat16 [768], P('fsdp'), may hold values from -4 to 4
- second_gain: bfloat16 [768], P('fsdp'), may hold values from 0.5 to 1.5
- second_shift: bfloat16 [768], P('fsdp'), may hold values from -4 to 4
- up_weight: bfloat16 [768, 3072], P('fsdp'), may hold values from -0.21875 to 0.21875
- up_bias: bfloat16 [3072], P('fsdp'), may hold values from -4 to 4
- down_weight: bfloat16 [3072, 768], P('fsdp'), may hold values from -0.109375 to 0.109375
- down_bias: bfloat16 [768], P('fsdp'), may hold values from -4 to 4
Outputs:
- result: bfloat16 [8192, 768], P(('ctx', 'fsdp'))
- grad_tokens: float32 [8192, 768], P(('ctx', 'fsdp'))
- grad_first_gain: float32 [768], P('fsdp')
- grad_first_shift: float32 [768], P('fsdp')
- grad_query_weight: float32 [768, 768], P('fsdp')
- grad_query_bias: float32 [768], P('fsdp')
- grad_key_weight: float32 [768, 768], P('fsdp')
- grad_value_weight: float32 [768, 768], P('fsdp')
- grad_value_bias: float32 [768], P('fsdp')
- grad_output_weight: float32 [768, 768], P('fsdp')
- grad_output_bias: float32 [768], P('fsdp')
- grad_second_gain: float32 [768], P('fsdp')
- grad_second_shift: float32 [768], P('fsdp')
- grad_up_weight: float32 [768, 3072], P('fsdp')
- grad_up_bias: float32 [3072], P('fsdp')
- grad_down_weight: float32 [3072, 768], P('fsdp')
- grad_down_bias: float32 [768], P('fsdp')
Inputs may be any that keep to these rules, and one draw needn't show every extreme that they name: Slot j of the 64 slots holds text block deal[j]; every block stands in exactly one slot. `doc_lengths`: the documents in text order; their lengths sum to 8192.
All inputs are finite; a program needn't handle non-finite values.
Results may differ from a plain program's by a relative error of at most 0.014.
Values may be sent and summed in bfloat16 or wider, within the bound.
A program may use at most 384 MiB of HBM per device.

v0:
```python
import jax
import jax.numpy as jnp
from jax import lax
from jax.experimental import pallas as pl
from jax.experimental.pallas import tpu as pltpu
from jax.sharding import Mesh
from jax.sharding import PartitionSpec as P

HEADS = 12
DH = 64
NSUM = 50
SEG = 2048
BLK = 128
GROUPS = 4
PER = HEADS // GROUPS
HW = PER * DH
WIDE = PER * BLK
CHUNK = 2 * BLK
EPS = 1e-05
SCALE = 0.125
MASKED = -1e30
ROOT_HALF = 0.7071067811865476
PDF_SCALE = 0.3989422804014327
VMEM_LIMIT = 56 << 20
bf16 = jnp.bfloat16
f32 = jnp.float32


def layer_norm(values, gain, shift):
    mean = jnp.mean(values, axis=-1, keepdims=True)
    centred = values - mean
    spread = jnp.mean(centred * centred, axis=-1, keepdims=True)
    return centred * lax.rsqrt(spread + EPS) * gain + shift


def outer(left, right):
    return lax.dot_general(left, right, (((0,), (0,)), ((), ())), preferred_element_type=f32)


def inner(left, right):
    return lax.dot_general(left, right, (((1,), (1,)), ((), ())), preferred_element_type=f32)


def dot(left, right):
    return jnp.dot(left, right, preferred_element_type=f32)


def survey(deal_ref, lengths_ref, where_ref, text_ref, low_ref, high_ref, first_ref):
    blocks = deal_ref.shape[0]
    per_group = blocks // (2 * GROUPS)
    rest = lax.axis_index(ROWS)

    def note(j, kept):
        pair = j // 2
        group = pair // per_group
        where_ref[deal_ref[j]] = ((pair - group * per_group) * GROUPS + group) * 2 + j % 2
        return kept

    lax.fori_loop(0, blocks, note, 0)
    starts = [jnp.int32(0)]
    for doc in range(lengths_ref.shape[0] - 1):
        starts.append(starts[-1] + lengths_ref[doc])

    def first_of(at):
        begin = jnp.zeros_like(at)
        for start in starts:
            begin = jnp.where(start <= at, jnp.maximum(begin, start), begin)
        return jnp.where(at - begin >= SEG + NSUM, begin + SEG, begin)

    for slot in range(2 * GROUPS):
        text = deal_ref[2 * ((slot // 2) * per_group + rest) + slot % 2]
        text_ref[slot] = text
        low_ref[slot] = first_of(text * BLK) // CHUNK
        high_ref[slot] = text // 2
        first_ref[slot] = first_of(text * BLK + lax.broadcasted_iota(jnp.int32, (1, BLK), 1))


def survey_scratch(blocks):
    slots = 2 * GROUPS
    return [
        pltpu.SMEM((blocks,), jnp.int32),
        pltpu.SMEM((slots,), jnp.int32),
        pltpu.SMEM((slots,), jnp.int32),
        pltpu.SMEM((slots,), jnp.int32),
        pltpu.VMEM((slots, 1, BLK), jnp.int32),
    ]


def spread_heads_t(part_t, order):
    rows = []
    zero = jnp.zeros((DH, BLK), part_t.dtype)
    for head in order:
        if head is None:
            rows.append(jnp.zeros((DH, WIDE), part_t.dtype))
        else:
            piece = part_t[DH * head : DH * head + DH]
            rows.append(
                jnp.concatenate([piece if h == head else zero for h in range(PER)], axis=1)
            )
    return jnp.concatenate(rows, axis=0)


K_ORDER = (0, 1, 2, None)
V_ORDER = (None, 2, 0, 1)


def visible(chunk, first, own):
    at = chunk * CHUNK + lax.broadcasted_iota(jnp.int32, (CHUNK, BLK), 0)
    allowed = (at >= first) & (at <= own)
    return jnp.concatenate([allowed] * PER, axis=1)


def load_chunk(kv_ref, where_ref, chunk):
    return jnp.concatenate(
        [kv_ref[where_ref[2 * chunk]], kv_ref[where_ref[2 * chunk + 1]]], axis=0
    )


def forward_kernel(
    deal_ref, lengths_ref, q_ref, kv_ref,
    out_ref, wide_ref, lse_ref,
    where_ref, text_ref, low_ref, high_ref, first_ref, vt_ref, acc_ref,
):
    survey(deal_ref, lengths_ref, where_ref, text_ref, low_ref, high_ref, first_ref)
    chunks = kv_ref.shape[0] // 2

    def turn(chunk, _):
        vt_ref[chunk] = load_chunk(kv_ref, where_ref, chunk)[:, BLK : 3 * BLK].T[DH:]
        return _

    lax.fori_loop(0, chunks, turn, 0)

    def one_slot(slot, _):
        wide_q = spread_heads_t(q_ref[slot].T[:HW], K_ORDER)
        first = first_ref[slot]
        own = text_ref[slot] * BLK + lax.broadcasted_iota(jnp.int32, (1, BLK), 1)
        acc_ref[...] = jnp.zeros_like(acc_ref)

        def step(chunk, carry):
            top, total = carry
            part = load_chunk(kv_ref, where_ref, chunk)
            scores = dot(part[:, : 2 * BLK], wide_q)
            scores = jnp.where(visible(chunk, first, own), scores, MASKED)
            fresh = jnp.maximum(top, jnp.max(scores, axis=0, keepdims=True))
            expo = jnp.exp(scores - fresh)
            shrink = jnp.exp(top - fresh)
            total = total * shrink + jnp.sum(expo, axis=0, keepdims=True)
            acc_ref[...] = acc_ref[...] * shrink + dot(vt_ref[chunk], expo.astype(bf16))
            return fresh, total

        top, total = lax.fori_loop(
            low_ref[slot],
            high_ref[slot] + 1,
            step,
            (jnp.full((1, WIDE), MASKED, f32), jnp.zeros((1, WIDE), f32)),
        )
        lse_ref[slot] = top + jnp.log(total)
        scaled = acc_ref[...] / total
        pieces = []
        for head in range(PER):
            row = DH * V_ORDER.index(head) - DH
            pieces.append(scaled[row : row + DH, BLK * head : BLK * head + BLK])
        kept = jnp.concatenate(pieces, axis=0)
        wide_ref[slot] = kept
        out_ref[slot] = kept.astype(bf16)
        return _

    lax.fori_loop(0, q_ref.shape[0], one_slot, 0)


def whole_vmem():
    return pl.BlockSpec(memory_space=pltpu.VMEM)


def whole_smem():
    return pl.BlockSpec(memory_space=pltpu.SMEM)


def attend_forward(deal, lengths, q, kv):
    slots = q.shape[0]
    blocks = kv.shape[0]
    return pl.pallas_call(
        forward_kernel,
        out_shape=(
            jax.ShapeDtypeStruct((slots, HW, BLK), bf16),
            jax.ShapeDtypeStruct((slots, HW, BLK), f32),
            jax.ShapeDtypeStruct((slots, 1, WIDE), f32),
        ),
        in_specs=[whole_smem()] * 2 + [whole_vmem()] * 2,
        out_specs=(whole_vmem(),) * 3,
        scratch_shapes=[
            *survey_scratch(blocks),
            pltpu.VMEM((blocks // 2, HW, CHUNK), bf16),
            pltpu.VMEM((HW, WIDE), f32),
        ],
        compiler_params=pltpu.CompilerParams(vmem_limit_bytes=(6 << 20) + kv.size // 5 * 16),
        name="attend_forward",
    )(deal, lengths, q, kv)


def backward_kernel(
    deal_ref, lengths_ref, q_ref, kv_ref, lse_ref, do_ref, wide_ref,
    dq_ref, dkv_ref, where_ref, text_ref, low_ref, high_ref, first_ref, qt_ref, qm_ref, dot_ref, dom_ref, delta_ref, acc_ref, dk_acc, dv_acc,
):
    survey(deal_ref, lengths_ref, where_ref, text_ref, low_ref, high_ref, first_ref)
    slots = q_ref.shape[0]
    chunks = kv_ref.shape[0] // 2

    def ready(slot, _):
        q = q_ref[slot]
        qt_ref[slot] = spread_heads_t(q.T[:HW], K_ORDER)
        lane = lax.broadcasted_iota(jnp.int32, (BLK, 2 * BLK), 1) // DH
        zero = jnp.zeros_like(q)
        qm_ref[slot] = jnp.concatenate(
            [jnp.where(lane == K_ORDER.index(h), q, zero) for h in range(PER)], axis=0
        )
        grad_t = do_ref[slot]
        dot_ref[slot] = spread_heads_t(grad_t, V_ORDER)
        ordered = jnp.concatenate(
            [
                jnp.zeros((DH, BLK), bf16) if h is None else grad_t[DH * h : DH * h + DH]
                for h in V_ORDER
            ],
            axis=0,
        ).T
        dom_ref[slot] = jnp.concatenate(
            [jnp.where(lane == V_ORDER.index(h), ordered, zero) for h in range(PER)], axis=0
        )
        both = grad_t.astype(f32) * wide_ref[slot]
        delta_ref[slot] = jnp.concatenate(
            [jnp.sum(both[DH * h : DH * h + DH], axis=0, keepdims=True) for h in range(PER)],
            axis=1,
        )
        acc_ref[slot] = jnp.zeros((HW, WIDE), f32)
        return _

    lax.fori_loop(0, slots, ready, 0)

    def one_chunk(chunk, _):
        part = load_chunk(kv_ref, where_ref, chunk)
        keys = part[:, : 2 * BLK]
        vals = part[:, BLK:]
        keys_t = keys.T[:HW]
        dk_acc[...] = jnp.zeros_like(dk_acc)
        dv_acc[...] = jnp.zeros_like(dv_acc)

        def one_slot(slot, kept):
            @pl.when((low_ref[slot] <= chunk) & (chunk <= high_ref[slot]))
            def _():
                own = text_ref[slot] * BLK + lax.broadcasted_iota(jnp.int32, (1, BLK), 1)
                scores = dot(keys, qt_ref[slot])
                probs = jnp.where(
                    visible(chunk, first_ref[slot], own), jnp.exp(scores - lse_ref[slot]), 0.0
                )
                dprobs = dot(vals, dot_ref[slot])
                dscores = (probs * (dprobs - delta_ref[slot])).astype(bf16)
                dv_acc[...] += dot(probs.astype(bf16), dom_ref[slot])
                dk_acc[...] += dot(dscores, qm_ref[slot])
                acc_ref[slot] += dot(keys_t, dscores)

            return kept

        lax.fori_loop(0, slots, one_slot, 0)
        packed = jnp.concatenate(
            [
                dk_acc[:, :BLK],
                dk_acc[:, BLK:] + dv_acc[:, :BLK],
                dv_acc[:, BLK:],
            ],
            axis=1,
        ).astype(bf16)
        dkv_ref[where_ref[2 * chunk]] = packed[:BLK]
        dkv_ref[where_ref[2 * chunk + 1]] = packed[BLK:]
        return _

    lax.fori_loop(0, chunks, one_chunk, 0)

    def finish(slot, _):
        total = acc_ref[slot]
        kept = jnp.concatenate(
            [total[DH * h : DH * h + DH, BLK * h : BLK * h + BLK] for h in range(PER)]
            + [jnp.zeros((DH, BLK), f32)],
            axis=0,
        )
        dq_ref[slot] = kept.T.astype(bf16)
        return _

    lax.fori_loop(0, slots, finish, 0)


def attend_backward(deal, lengths, q, kv, lse, grad_t, wide):
    slots = q.shape[0]
    return pl.pallas_call(
        backward_kernel,
        out_shape=(
            jax.ShapeDtypeStruct((slots, BLK, 2 * BLK), bf16),
            jax.ShapeDtypeStruct(kv.shape, bf16),
        ),
        in_specs=[whole_smem()] * 2 + [whole_vmem()] * 5,
        out_specs=(whole_vmem(),) * 2,
        scratch_shapes=[
            *survey_scratch(kv.shape[0]),
            pltpu.VMEM((slots, 2 * BLK, WIDE), bf16),
            pltpu.VMEM((slots, WIDE, 2 * BLK), bf16),
            pltpu.VMEM((slots, 2 * BLK, WIDE), bf16),
            pltpu.VMEM((slots, WIDE, 2 * BLK), bf16),
            pltpu.VMEM((slots, 1, WIDE), f32),
            pltpu.VMEM((slots, HW, WIDE), f32),
            pltpu.VMEM((CHUNK, 2 * BLK), f32),
            pltpu.VMEM((CHUNK, 2 * BLK), f32),
        ],
        compiler_params=pltpu.CompilerParams(
            vmem_limit_bytes=min((17 << 20) + kv.size // 5 * 21, VMEM_LIMIT + (4 << 20))
        ),
        name="attend_backward",
    )(deal, lengths, q, kv, lse, grad_t, wide)


MESH = pl.DeviceIdType.MESH


def send(src, dst, out_sem, in_sem, **device):
    return pltpu.make_async_remote_copy(
        src_ref=src, dst_ref=dst, send_sem=out_sem, recv_sem=in_sem, device_id=device, device_id_type=MESH
    )


def place():
    return tuple(lax.axis_index(name) for name in ("g", "r", "core", "x"))


def seat(r, core, x):
    return (r * 2 + core) * 2 + x


def greet(g, r, core, x, line):
    barrier = pltpu.get_barrier_semaphore()

    def hello(**device):
        pl.semaphore_signal(barrier, inc=1, device_id=device, device_id_type=MESH)

    hello(core=1 - core)
    hello(x=1 - x)
    hello(r=1 - r)
    if line:
        for away in range(1, GROUPS):
            hello(g=lax.rem(g + away, GROUPS))
        pl.semaphore_wait(barrier, 3 + GROUPS - 1)
    else:
        pl.when(g > 0)(lambda: hello(g=g - 1))
        pl.when(g < GROUPS - 1)(lambda: hello(g=g + 1))
        pl.semaphore_wait(barrier, 5 - jnp.where(g == 0, 1, 0) - jnp.where(g == GROUPS - 1, 1, 0))


NEAREST = tuple(tuple(sorted(range(GROUPS), key=lambda s: (abs(s - z), s))) for z in range(GROUPS))


def nearest(g, step):
    picked = NEAREST[0][step]
    for z in range(1, GROUPS):
        picked = jnp.where(g == z, NEAREST[z][step], picked)
    return picked


def prepare(g, x, query_ref, key_ref, value_ref, lines_ref, narrow_ref, small_ref):
    half = lines_ref.shape[1]
    odd = lax.rem(g, 2) == 1

    def columns(ref):
        low = pl.multiple_of(3 * g // 2 * BLK, BLK)
        window = ref[:, pl.ds(low, 2 * BLK)]
        moved = jnp.concatenate([window[:, DH:], window[:, :DH]], axis=1)
        return jnp.where(odd, moved, window)

    lane = lax.broadcasted_iota(jnp.int32, (half, 2 * BLK), 1)
    query = columns(query_ref)
    narrow_ref[:, : 2 * BLK] = jnp.where(lane < HW, query, jnp.zeros_like(query))
    narrow_ref[:, 2 * BLK :] = pack_kv(columns(key_ref)[:, :HW], columns(value_ref)[:, :HW])

    lines = lines_ref[...].astype(f32)
    zero = jnp.zeros((1, half), f32)
    small_ref[...] = jnp.zeros_like(small_ref)
    for row in range(6):
        line = lines[row : row + 1]
        small_ref[row : row + 1] = jnp.where(
            x == 0, jnp.concatenate([line, zero], axis=1), jnp.concatenate([zero, line], axis=1)
        )
    for i in range(2):
        small_ref[pl.ds(8 + 2 * x + i, 1)] = jnp.concatenate(
            [lines[8 + 2 * i : 9 + 2 * i], lines[9 + 2 * i : 10 + 2 * i]], axis=1
        )

    def part(row):
        line = lines[row : row + 1]
        mine = jnp.where(odd, line[:, HW:], line[:, :HW])
        return jnp.where(g // 2 == x, mine, jnp.zeros_like(mine))

    value = part(7)
    small_ref[12:13] = jnp.concatenate(
        [part(6), jnp.zeros((1, 2 * BLK), f32), value[:, 2 * DH :], value[:, : 2 * DH], jnp.zeros((1, BLK), f32)], axis=1
    )


def gather_kernel(
    tokens_ref, query_ref, key_ref, value_ref, lines_ref, up_ref, wo_ref,
    kv_ref, q_ref, normed_ref, small_out, wfull, up_out, wo_out,
    lined, narrow_ref, small_ref, small_in, kvs,
    z_own, z_send, z_recv, s_sem, n_send, n_recv, kv_send, kv_recv, kv_local, w_send, w_recv, w_local,
):
    g, r, core, x = place()
    other = 1 - x
    rows, width = tokens_ref.shape
    half = width // 2
    fourth = half // 2
    eighth = half // 4
    greet(g, r, core, x, False)

    def along(source, away, sem):
        return send(lined.at[source], lined.at[source], sem, z_recv.at[source], g=g + away)

    lined[g] = tokens_ref[...]
    pl.when(g > 0)(lambda: along(g, -1, z_own.at[0]).start())
    pl.when(g < GROUPS - 1)(lambda: along(g, 1, z_own.at[1]).start())

    prepare(g, x, query_ref, key_ref, value_ref, lines_ref, narrow_ref, small_ref)
    small_move = send(small_ref, small_in, s_sem.at[0], s_sem.at[1], x=other)
    small_move.start()
    mine = pl.ds(x * half + core * fourth, fourth)
    narrow_x = send(narrow_ref.at[pl.ds(core * fourth, fourth)], wfull.at[mine], n_send.at[0], n_recv.at[0], x=other)
    narrow_x.start()

    def wo_rows(owner, part):
        return wo_out.at[pl.ds(owner * half + core * fourth + part * eighth, eighth)]

    def up_rows(owner, part):
        return up_out.at[pl.ds(owner * half + part * fourth, fourth)]

    def up_columns(owner):
        return pl.ds(pl.multiple_of((2 * owner + core) * width, width), width)

    wo_x = send(wo_ref.at[pl.ds(core * fourth + r * eighth, eighth)], wo_rows(x, r), w_send.at[0], w_recv.at[0], x=other)
    up_x = send(
        up_ref.at[pl.ds(r * fourth, fourth), up_columns(other)], up_rows(x, r), w_send.at[1], w_recv.at[1], x=other
    )
    wo_y = send(wo_rows(other, r), wo_rows(other, r), w_send.at[3], w_recv.at[3], r=1 - r)
    up_y = send(up_rows(other, r), up_rows(other, r), w_send.at[4], w_recv.at[4], r=1 - r)
    wo_s = [
        send(wo_rows(other, part), wo_rows(other, part), w_send.at[6 + i], w_recv.at[6 + i], core=1 - core)
        for i, part in enumerate((r, 1 - r))
    ]
    wo_x.start()
    locals_ = [
        pltpu.make_async_copy(wo_ref, wo_out.at[pl.ds(x * half, half)], w_local.at[0]),
        pltpu.make_async_copy(up_ref.at[:, up_columns(x)], up_out.at[pl.ds(x * half, half)], w_local.at[1]),
    ]
    for item in locals_:
        item.start()

    wfull[pl.ds(x * half, half)] = narrow_ref[...]
    narrow_x.wait_recv()
    theirs = wfull.at[pl.ds(other * half + core * fourth, fourth)]
    narrow_s = send(theirs, theirs, n_send.at[1], n_recv.at[1], core=1 - core)
    narrow_s.start()
    small_move.wait_recv()
    small_out[...] = small_ref[...] + small_in[...]
    narrow_s.wait_recv()

    own = seat(r, core, x)

    def block(owner, source):
        return kv_ref.at[owner, source]

    def push(step, kind, what, **device):
        copy = send(what[0], what[1], kv_send.at[kind, step], kv_recv.at[kind, step], **device)
        copy.start()

    def settle(step, kind, owner, source):
        send(block(owner, source), block(owner, source), kv_send.at[kind, step], kv_recv.at[kind, step], x=other).wait_recv()

    def forward(step):
        source = nearest(g, step)
        by_x = block(seat(r, core, other), source)
        settle(step, 0, seat(r, core, other), source)
        if step % 2 == 0:
            push(step, 3, (by_x, by_x), r=1 - r)
        push(step, 4, (by_x, by_x), core=1 - core)
        by_y = block(seat(1 - r, core, x), source)
        settle(step, 1, seat(1 - r, core, x), source)
        if step % 2 == 1:
            push(step, 3, (by_y, by_y), x=other)
        push(step, 5, (by_y, by_y), core=1 - core)

    def forward_far(step):
        source = nearest(g, step)
        far = block(seat(1 - r, core, other), source)
        settle(step, 3, seat(1 - r, core, other), source)
        push(step, 6, (far, far), core=1 - core)

    for step in range(GROUPS):
        source = nearest(g, step)
        if step > 0:
            send(lined.at[source], lined.at[source], z_send.at[source], z_recv.at[source], x=other).wait_recv()
            pl.when((source < g) & (g < GROUPS - 1))(lambda: along(source, 1, z_send.at[source]).start())
            pl.when((source > g) & (g > 0))(lambda: along(source, -1, z_send.at[source]).start())
        values = lined[source].astype(f32)
        normed = layer_norm(values, small_out[0:1], small_out[1:2]).astype(bf16)
        normed_ref[source] = normed
        both = dot(normed, wfull[...]) + small_out[12:13, : wfull.shape[1]]
        q_ref[source] = (both[:, : 2 * BLK] * SCALE).astype(bf16)
        kvs[step] = both[:, 2 * BLK :].astype(bf16)
        here = (kvs.at[step], block(own, source))
        push(step, 0, here, x=other)
        push(step, 1, here, r=1 - r)
        push(step, 2, here, core=1 - core)
        pltpu.make_async_copy(kvs.at[step], block(own, source), kv_local.at[step]).start()
        if step == 0:
            up_x.start()
        if step > 0:
            forward(step - 1)
        if step > 1:
            forward_far(step - 2)
    wo_x.wait_recv()
    wo_y.start()
    wo_s[0].start()
    forward(GROUPS - 1)
    forward_far(GROUPS - 2)
    up_x.wait_recv()
    up_y.start()
    send(wo_rows(other, 1 - r), wo_rows(other, 1 - r), w_send.at[3], w_recv.at[3], r=1 - r).wait_recv()
    wo_s[1].start()
    forward_far(GROUPS - 1)

    for step in range(GROUPS):
        source = nearest(g, step)
        pltpu.make_async_copy(kvs.at[step], block(own, source), kv_local.at[step]).wait()
        settle(step, 2, seat(r, 1 - core, x), source)
        settle(step, 4, seat(r, 1 - core, other), source)
        settle(step, 5, seat(1 - r, 1 - core, x), source)
        settle(step, 6, seat(1 - r, 1 - core, other), source)
        for kind in range(7):
            send(kvs.at[step], block(own, source), kv_send.at[kind, step], kv_recv.at[kind, step], x=other).wait_send()
    pl.when(g > 0)(lambda: along(g, -1, z_own.at[0]).wait_send())
    pl.when(g < GROUPS - 1)(lambda: along(g, 1, z_own.at[1]).wait_send())
    for step in range(1, GROUPS):
        source = nearest(g, step)
        passed = ((source < g) & (g < GROUPS - 1)) | ((source > g) & (g > 0))
        pl.when(passed)(lambda: send(lined.at[source], lined.at[source], z_send.at[source], z_recv.at[source], x=other).wait_send())
    small_move.wait_send()
    narrow_x.wait_send()
    narrow_s.wait_send()
    for item in locals_:
        item.wait()
    for item in (wo_x, up_x, wo_y, up_y, *wo_s):
        item.wait_send()
    send(up_rows(other, 1 - r), up_rows(other, 1 - r), w_send.at[4], w_recv.at[4], r=1 - r).wait_recv()
    for i, part in enumerate((r, 1 - r)):
        there = wo_out.at[pl.ds(other * half + (1 - core) * fourth + part * eighth, eighth)]
        send(there, there, w_send.at[6 + i], w_recv.at[6 + i], core=1 - core).wait_recv()


def anywhere():
    return pl.BlockSpec(memory_space=pl.ANY)


def gather(tokens, query, key, value, lines, up, wo):
    rows, width = tokens.shape
    wide = 2 * BLK + 2 * HW
    small = (16, width)
    dma = pltpu.SemaphoreType.DMA
    return pl.pallas_call(
        gather_kernel,
        out_shape=(
            jax.ShapeDtypeStruct((8, GROUPS, rows, 2 * HW), bf16),
            jax.ShapeDtypeStruct((GROUPS, rows, 2 * BLK), bf16),
            jax.ShapeDtypeStruct((GROUPS, rows, width), bf16),
            jax.ShapeDtypeStruct(small, f32),
            jax.ShapeDtypeStruct((width, wide), bf16),
            jax.ShapeDtypeStruct((width, width), bf16),
            jax.ShapeDtypeStruct((width, width), bf16),
        ),
        in_specs=[whole_vmem()] * 5 + [anywhere()] * 2,
        out_specs=(anywhere(), *(whole_vmem(),) * 4, anywhere(), anywhere()),
        scratch_shapes=[
            pltpu.VMEM((GROUPS, rows, width), bf16),
            pltpu.VMEM((width // 2, wide), bf16),
            pltpu.VMEM(small, f32),
            pltpu.VMEM(small, f32),
            pltpu.VMEM((GROUPS, rows, 2 * HW), bf16),
            dma((2,)), dma((GROUPS,)), dma((GROUPS,)), dma((2,)), dma((2,)), dma((2,)),
            dma((7, GROUPS)), dma((7, GROUPS)), dma((GROUPS,)), dma((8,)), dma((8,)), dma((2,)),
        ],
        compiler_params=pltpu.CompilerParams(
            collective_id=0, has_side_effects=True, vmem_limit_bytes=14 << 20
        ),
        name="gather",
    )(tokens, query, key, value, lines, up, wo)


def erf_parts(values):
    below = 0.5 * (1.0 + lax.erf(values * ROOT_HALF))
    return below, PDF_SCALE * jnp.exp(-0.5 * values * values)


PARTS = 8
UNIT = 216


def dense_kernel(
    out_t_ref, tokens_ref, cot_ref, small_ref, up_ref, wo_ref, down_any,
    result_ref, middle_grad_ref, grad_t_ref, bundle_ref, sums_ref,
    down_ref, attn_in, attn_t, cots, h2s, mid_ref, n2_ref, part_y, part_d, in_y, in_d, pass_y, pass_d, x_y, x_d,
    hids, dus, grad_out, wo_keep, wo_give, wo_in, wo_pass, wo_x,
    down_sem, a_send, a_recv, c_send, c_recv, h_send, h_recv, y_send, y_recv, d_send, d_recv, o_send, o_recv,
    w_send, w_recv,
):
    g, r, core, x = place()
    other = 1 - x
    rows, width = tokens_ref.shape
    half = width // 2
    fourth = half // 2
    load = pltpu.make_async_copy(
        down_any.at[pl.ds(pl.multiple_of(core * width, width), width)], down_ref, down_sem
    )
    load.start()
    greet(g, r, core, x, True)
    cots[0] = cot_ref[...]

    def share(rows_ref, out_sem, in_sem):
        moves = (
            send(rows_ref.at[0], rows_ref.at[2], out_sem.at[1], in_sem.at[1], x=other),
            send(rows_ref.at[0], rows_ref.at[1], out_sem.at[0], in_sem.at[0], core=1 - core),
        )
        for move in moves:
            move.start()
        return moves

    def pass_on(rows_ref, moves, out_sem, in_sem):
        moves[0].wait_recv()
        move = send(rows_ref.at[2], rows_ref.at[3], out_sem.at[2], in_sem.at[2], core=1 - core)
        move.start()
        return move

    def other_group(away):
        return lax.rem(g + away, GROUPS)

    attn_moves = []
    for away in range(1, GROUPS):
        to = other_group(away)
        attn_moves.append(
            send(out_t_ref.at[pl.ds(2 * to, 2)], attn_in.at[g], a_send.at[away], a_recv.at[g], g=to)
        )
        attn_moves[-1].start()
    cot_moves = share(cots, c_send, c_recv)
    attn_in[g] = out_t_ref[pl.ds(2 * g, 2)]
    sums_ref[...] = jnp.zeros_like(sums_ref)
    sums_ref[5:6] = jnp.sum(cot_ref[...].astype(f32), axis=0, keepdims=True)
    for away in range(1, GROUPS):
        source = other_group(away)
        send(attn_in.at[source], attn_in.at[source], a_send.at[away], a_recv.at[source], g=source).wait_recv()
    for source in range(GROUPS):
        attn_t[HW * source : HW * source + HW] = jnp.concatenate(
            [attn_in[source, 0], attn_in[source, 1]], axis=1
        )
    middle = tokens_ref[...].astype(f32) + outer(attn_t[...], wo_ref[...]) + small_ref[2:3]
    mid_ref[...] = middle
    mean = jnp.mean(middle, axis=-1, keepdims=True)
    centred = middle - mean
    spread = jnp.mean(centred * centred, axis=-1, keepdims=True)
    scale = lax.rsqrt(spread + EPS)
    n2_ref[...] = centred * scale
    h2s[0] = (n2_ref[...] * small_ref[3:4] + small_ref[4:5]).astype(bf16)
    h2_moves = share(h2s, h_send, h_recv)
    cot_pass = pass_on(cots, cot_moves, c_send, c_recv)
    load.wait()
    bias_row = 8 + 2 * x + core
    bias = small_ref[pl.ds(bias_row, 1)]
    sums_ref[pl.ds(bias_row, 1)] = jnp.zeros((1, width), f32)

    def one_part(part):
        expanded = dot(h2s[part], up_ref[...]) + bias
        below, density = erf_parts(expanded)
        hidden = (expanded * below).astype(bf16)
        hids[part] = hidden
        slope = below + expanded * density
        grad_hidden = inner(cots[part], down_ref[...]).astype(bf16).astype(f32)
        grad_expand = (grad_hidden * slope).astype(bf16)
        dus[part] = grad_expand
        part_d[part] = inner(grad_expand, up_ref[...])
        part_y[part] = dot(hidden, down_ref[...])
        sums_ref[pl.ds(bias_row, 1)] += jnp.sum(grad_expand.astype(f32), axis=0, keepdims=True)

    one_part(0)
    cot_moves[1].wait_recv()
    h2_moves[1].wait_recv()
    h2_pass = pass_on(h2s, h2_moves, h_send, h_recv)
    one_part(1)
    d_sib = send(part_d.at[1], in_d, d_send.at[0], d_recv.at[0], core=1 - core)
    d_sib.start()
    cot_pass.wait_recv()
    h2_pass.wait_recv()
    one_part(3)
    x_d[0] = part_d[3].astype(bf16)
    x_y[0] = part_y[3].astype(bf16)
    d_pass = send(x_d.at[0], pass_d, d_send.at[1], d_recv.at[1], core=1 - core)
    y_pass = send(x_y.at[0], pass_y, y_send.at[1], y_recv.at[1], core=1 - core)
    d_pass.start()
    y_pass.start()
    one_part(2)
    d_pass.wait_recv()
    x_d[1] = (part_d[2] + pass_d[...].astype(f32)).astype(bf16)
    d_x = send(x_d.at[1], x_d.at[2], d_send.at[2], d_recv.at[2], x=other)
    d_x.start()
    y_pass.wait_recv()
    x_y[1] = (part_y[2] + pass_y[...].astype(f32)).astype(bf16)
    y_x = send(x_y.at[1], x_y.at[2], y_send.at[2], y_recv.at[2], x=other)
    y_x.start()
    y_sib = send(part_y.at[1], in_y, y_send.at[0], y_recv.at[0], core=1 - core)
    y_sib.start()

    def over_rows(left, right):
        total = outer(left[0], right[0])
        for part in range(1, 4):
            total += outer(left[part], right[part])
        return total.astype(bf16)

    down_grad = over_rows(hids, cots)
    up_grad = over_rows(h2s, dus)
    for p in range(PARTS):
        bundle_ref[p // GROUPS, p % GROUPS, 0:96] = down_grad[96 * p : 96 * p + 96]
        bundle_ref[p // GROUPS, p % GROUPS, 96:144] = up_grad[48 * p : 48 * p + 48]
        bundle_ref[p // GROUPS, p % GROUPS, 144:192] = up_grad[half + 48 * p : half + 48 * p + 48]

    d_sib.wait_recv()
    d_x.wait_recv()
    grad_second = part_d[0] + in_d[...] + x_d[2].astype(f32)
    n2 = n2_ref[...]
    sums_ref[3:4] = jnp.sum(grad_second * n2, axis=0, keepdims=True)
    sums_ref[4:5] = jnp.sum(grad_second, axis=0, keepdims=True)
    pulled = grad_second * small_ref[3:4]
    inward = pulled - jnp.mean(pulled, axis=-1, keepdims=True) - n2 * jnp.mean(pulled * n2, axis=-1, keepdims=True)
    grad_middle = cot_ref[...].astype(f32) + inward * scale
    middle_grad_ref[...] = grad_middle
    branch = grad_middle.astype(bf16)
    sums_ref[2:3] = jnp.sum(branch.astype(f32), axis=0, keepdims=True)
    grad_out_t = inner(wo_ref[...], branch).astype(bf16)
    for group in range(GROUPS):
        for b in range(2):
            grad_out[group, b] = grad_out_t[HW * group : HW * group + HW, BLK * b : BLK * b + BLK]
    grad_moves = []
    for away in range(1, GROUPS):
        to = other_group(away)
        grad_moves.append(
            send(grad_out.at[to], grad_t_ref.at[pl.ds(2 * g, 2)], o_send.at[away], o_recv.at[g], g=to)
        )
        grad_moves[-1].start()
    grad_t_ref[pl.ds(2 * g, 2)] = grad_out[g]

    for owner in range(2):
        for c in range(2):
            piece = dot(attn_t[half * owner + fourth * c : half * owner + fourth * c + fourth], branch)

            @pl.when(core == c)
            def _():
                wo_keep[owner] = piece

            @pl.when(core != c)
            def _():
                wo_give[owner] = piece.astype(bf16)

    w_sib = send(wo_give, wo_in, w_send.at[0], w_recv.at[0], core=1 - core)
    w_sib.start()
    y_x.wait_recv()
    y_sib.wait_recv()
    result_ref[...] = (
        mid_ref[...] + part_y[0] + in_y[...] + x_y[2].astype(f32) + small_ref[5:6]
    ).astype(bf16)
    w_sib.wait_recv()
    wo_pass[...] = (wo_keep[other] + wo_in[other].astype(f32)).astype(bf16)
    w_x = send(wo_pass, wo_x, w_send.at[1], w_recv.at[1], x=other)
    w_x.start()
    mine = wo_keep[x] + wo_in[x].astype(f32)
    w_x.wait_recv()
    wo_sum = (mine + wo_x[...].astype(f32)).astype(bf16)
    for p in range(PARTS):
        bundle_ref[p // GROUPS, p % GROUPS, 192:UNIT] = wo_sum[24 * p : 24 * p + 24]
    for away in range(1, GROUPS):
        source = other_group(away)
        send(
            grad_t_ref.at[pl.ds(2 * source, 2)], grad_t_ref.at[pl.ds(2 * source, 2)],
            o_send.at[away], o_recv.at[source], g=source,
        ).wait_recv()
    for item in (
        *cot_moves, cot_pass, *h2_moves, h2_pass, d_sib, d_pass, d_x, y_sib, y_pass, y_x, w_sib, w_x, *attn_moves, *grad_moves,
    ):
        item.wait_send()


def dense(out_t, tokens, cot, small, up, wo, down):
    rows, width = tokens.shape
    dma = pltpu.SemaphoreType.DMA
    full = (rows, width)
    fourth = (width // 4, width)
    return pl.pallas_call(
        dense_kernel,
        out_shape=(
            jax.ShapeDtypeStruct(full, bf16),
            jax.ShapeDtypeStruct(full, f32),
            jax.ShapeDtypeStruct(out_t.shape, bf16),
            jax.ShapeDtypeStruct((2, GROUPS, UNIT, width), bf16),
            jax.ShapeDtypeStruct(small.shape, f32),
        ),
        in_specs=[whole_vmem()] * 6 + [anywhere()],
        out_specs=(whole_vmem(),) * 5,
        scratch_shapes=[
            pltpu.VMEM((width, width), bf16),
            pltpu.VMEM((GROUPS, 2, HW, BLK), bf16),
            pltpu.VMEM((width, rows), bf16),
            pltpu.VMEM((4, *full), bf16),
            pltpu.VMEM((4, *full), bf16),
            pltpu.VMEM(full, f32),
            pltpu.VMEM(full, f32),
            pltpu.VMEM((4, *full), f32),
            pltpu.VMEM((4, *full), f32),
            pltpu.VMEM(full, f32),
            pltpu.VMEM(full, f32),
            pltpu.VMEM(full, bf16),
            pltpu.VMEM(full, bf16),
            pltpu.VMEM((3, *full), bf16),
            pltpu.VMEM((3, *full), bf16),
            pltpu.VMEM((4, *full), bf16),
            pltpu.VMEM((4, *full), bf16),
            pltpu.VMEM((GROUPS, 2, HW, BLK), bf16),
            pltpu.VMEM((2, *fourth), f32),
            pltpu.VMEM((2, *fourth), bf16),
            pltpu.VMEM((2, *fourth), bf16),
            pltpu.VMEM(fourth, bf16),
            pltpu.VMEM(fourth, bf16),
            dma(()), dma((GROUPS,)), dma((GROUPS,)), dma((3,)), dma((3,)), dma((3,)), dma((3,)),
            dma((3,)), dma((3,)), dma((3,)), dma((3,)), dma((GROUPS,)), dma((GROUPS,)), dma((2,)), dma((2,)),
        ],
        compiler_params=pltpu.CompilerParams(
            collective_id=1, has_side_effects=True, vmem_limit_bytes=40 << 20
        ),
        name="dense",
    )(out_t, tokens, cot, small, up, wo, down)


FARTHEST = ((3, 2, 1, 0), (3, 0, 2, 1), (0, 3, 1, 2), (0, 1, 2, 3))


def farthest(g, step):
    picked = FARTHEST[0][step]
    for z in range(1, GROUPS):
        picked = jnp.where(g == z, FARTHEST[z][step], picked)
    return picked


class Chain:
    def __init__(self, g, x, total, parts, inward, outward, out_sem, in_sem):
        self.g, self.x, self.total, self.parts = g, x, total, parts
        self.inward, self.outward, self.out_sem, self.in_sem = inward, outward, out_sem, in_sem

    def move(self, to, way):
        return send(
            self.outward.at[to], self.inward.at[way, to], self.out_sem.at[to], self.in_sem.at[way, to],
            g=jnp.clip(self.g + (1 if way == 0 else -1), 0, GROUPS - 1),
        )

    def step(self, to):
        g = self.g
        self.total[...] = self.parts[to].astype(f32)

        def take(way):
            arrived(self.inward.at[way, to], self.out_sem.at[to], self.in_sem.at[way, to], self.x)
            self.total[...] += self.inward[way, to].astype(f32)

        pl.when((to >= g) & (g > 0))(lambda: take(0))
        pl.when((to <= g) & (g < GROUPS - 1))(lambda: take(1))

        @pl.when(to != g)
        def _():
            self.outward[to] = self.total[...].astype(bf16)

        pl.when(to > g)(lambda: self.move(to, 0).start())
        pl.when(to < g)(lambda: self.move(to, 1).start())

    def finish(self):
        for step in range(GROUPS - 1):
            to = farthest(self.g, step)
            left(self.outward.at[to], self.out_sem.at[to], self.in_sem.at[0, to], self.x)


class Ring:
    def __init__(self, g, x, slot, own_sem, out_sem, in_sem):
        self.g, self.x, self.slot = g, x, slot
        self.own_sem, self.out_sem, self.in_sem = own_sem, out_sem, in_sem

    def move(self, source, way, sem):
        return send(
            self.slot(source), self.slot(source), sem, self.in_sem.at[source],
            g=jnp.clip(self.g + way, 0, GROUPS - 1),
        )

    def start(self):
        g = self.g
        pl.when(g > 0)(lambda: self.move(g, -1, self.own_sem.at[0]).start())
        pl.when(g < GROUPS - 1)(lambda: self.move(g, 1, self.own_sem.at[1]).start())

    def step(self, step):
        g, source = self.g, nearest(self.g, step)
        arrived(self.slot(source), self.out_sem.at[source], self.in_sem.at[source], self.x)
        pl.when((source < g) & (g < GROUPS - 1))(lambda: self.move(source, 1, self.out_sem.at[source]).start())
        pl.when((source > g) & (g > 0))(lambda: self.move(source, -1, self.out_sem.at[source]).start())
        return source

    def finish(self):
        g = self.g
        for i, there in enumerate((g > 0, g < GROUPS - 1)):
            pl.when(there)(lambda: left(self.slot(g), self.own_sem.at[i], self.in_sem.at[g], self.x))
        for step in range(1, GROUPS):
            source = nearest(g, step)
            passed = ((source < g) & (g < GROUPS - 1)) | ((source > g) & (g > 0))
            pl.when(passed)(
                lambda: left(self.slot(source), self.out_sem.at[source], self.in_sem.at[source], self.x)
            )


def arrived(what, out_sem, in_sem, x):
    send(what, what, out_sem, in_sem, x=1 - x).wait_recv()


def left(what, out_sem, in_sem, x):
    send(what, what, out_sem, in_sem, x=1 - x).wait_send()


def scatter_kernel(
    dkv_ref, dq_ref, normed_ref, wfull_ref, tokens_ref, mgrad_ref, small_ref, bundle_ref, sums_in,
    tokens_grad_ref, big_ref, qout_ref, kvout_ref, sums_ref,
    own_kv, sib_kv, keep_x, give_x, in_x, give_y, in_y, part_a, total_a, inward_a, outward_a, wg_kv,
    by_in, by_sum, total_b, inward_b, outward_b, unit,
    q_keep, q_give, q_in, q_pass, q_x, q_y, q_sum, v_keep, v_give, v_in, v_pass, v_x, v_y, v_sum,
    sums_got,
    own_sem, k_send, k_recv, x_send, x_recv, y_send, y_recv, ca_send, ca_recv,
    b_send, b_recv, cb_send, cb_recv, u_send, u_recv, rb_own, rb_send, rb_recv,
    fy_send, fy_recv, fs_send, fs_recv,
    q_send, q_recv, rq_own, rq_send, rq_recv, qs_send, qs_recv,
    v_send, v_recv, rv_own, rv_send, rv_recv, vs_send, vs_recv,
    s_send, s_recv, l_sem,
):
    g, r, core, x = place()
    other, sib, far_r = 1 - x, 1 - core, 1 - r
    rows, width = tokens_ref.shape
    half = width // 2
    fourth = half // 2
    wide_q = 2 * BLK
    greet(g, r, core, x, True)
    pending = []

    def begin(src, dst, out_sem, in_sem, **device):
        move = send(src, dst, out_sem, in_sem, **device)
        move.start()
        pending.append(move)
        return move

    def settled(move):
        move.wait_recv()
        move.wait_send()
        pending[:] = [item for item in pending if item is not move]

    kv_moves = []
    for i in range(GROUPS):
        c = farthest(g, i)
        for spot in range(4):
            own = pltpu.make_async_copy(dkv_ref.at[seat(spot // 2, core, spot % 2), c], own_kv.at[i, spot], own_sem.at[i, spot])
            own.start()
            across = begin(
                dkv_ref.at[seat(spot // 2, sib, spot % 2), c], sib_kv.at[i, spot],
                k_send.at[i, spot], k_recv.at[i, spot], core=sib,
            )
            kv_moves.append((own, across))

    def piece(i):
        z = farthest(g, i)
        begin(bundle_ref.at[far_r, z], by_in.at[z], b_send.at[i], b_recv.at[i], r=far_r)

    piece(0)
    piece(1)

    def split(total, keep, give, wide):
        for owner in range(2):
            for c in range(2):
                low = half * owner + fourth * c
                chunk = total[low : low + fourth]

                @pl.when(core == c)
                def _():
                    keep[owner] = chunk

                @pl.when(core != c)
                def _():
                    give[owner] = chunk.astype(bf16)

    def scaled(c):
        return dq_ref[c] * bf16(SCALE)

    query_total = outer(normed_ref[0], scaled(0))
    for c in range(1, GROUPS):
        query_total += outer(normed_ref[c], scaled(c))
    split(query_total, q_keep, q_give, wide_q)
    q_move = begin(q_give, q_in, q_send.at[0], q_recv.at[0], core=sib)
    sums_ref[...] = jnp.zeros_like(sums_ref)
    sums_ref[0:16] = sums_in[...]
    line_q = scaled(0).astype(f32)
    for c in range(1, GROUPS):
        line_q += scaled(c).astype(f32)
    sums_ref[pl.ds(16 + g, 1), 0:wide_q] = jnp.sum(line_q, axis=0, keepdims=True)
    wg_kv[...] = jnp.zeros_like(wg_kv)

    for i in range(GROUPS):
        for own, across in kv_moves[4 * i : 4 * i + 4]:
            own.wait()
            across.wait_recv()
        for row in range(2):
            give_x[i, row] = (
                own_kv[i, 2 * row + other].astype(f32) + sib_kv[i, 2 * row + other].astype(f32)
            ).astype(bf16)
        begin(give_x.at[i], in_x.at[i], x_send.at[i], x_recv.at[i], x=other)
        for row in range(2):
            keep_x[i, row] = own_kv[i, 2 * row + x].astype(f32) + sib_kv[i, 2 * row + x].astype(f32)
        if i == 1:
            q_move.wait_recv()
            q_pass[...] = (q_keep[other] + q_in[other].astype(f32)).astype(bf16)
    q_across = begin(q_pass, q_x, q_send.at[1], q_recv.at[1], x=other)

    chain_a = Chain(g, x, total_a, part_a, inward_a, outward_a, ca_send, ca_recv)
    chain_b = Chain(g, x, total_b, by_sum, inward_b, outward_b, cb_send, cb_recv)

    def on_x(i):
        arrived(in_x.at[i], x_send.at[i], x_recv.at[i], x)
        give_y[i] = (keep_x[i, far_r] + in_x[i, far_r].astype(f32)).astype(bf16)
        begin(give_y.at[i], in_y.at[i], y_send.at[i], y_recv.at[i], r=far_r)
        keep_x[i, r] += in_x[i, r].astype(f32)

    def on_y(i):
        c = farthest(g, i)
        arrived(in_y.at[i], y_send.at[i], y_recv.at[i], x)
        both = (keep_x[i, r] + in_y[i].astype(f32)).astype(bf16)
        part_a[c] = inner(scaled(c), wfull_ref[:, :wide_q]) + inner(both, wfull_ref[:, wide_q:])
        wg_kv[...] += outer(normed_ref[c], both)
        sums_ref[pl.ds(16 + g, 1), wide_q : wide_q + 2 * HW] += jnp.sum(both.astype(f32), axis=0, keepdims=True)

    def on_piece(i):
        z = farthest(g, i)
        arrived(by_in.at[z], b_send.at[i], b_recv.at[i], x)
        by_sum[z] = bundle_ref[r, z].astype(f32) + by_in[z].astype(f32)

    for i in range(GROUPS):
        on_x(i)
        if i < 2:
            piece(2 + i)
        on_piece(i)
        if i >= 1:
            on_y(i - 1)
        if i >= 2:
            chain_a.step(farthest(g, i - 2))
    on_y(GROUPS - 1)
    split(wg_kv, v_keep, v_give, 2 * HW)
    v_move = begin(v_give, v_in, v_send.at[0], v_recv.at[0], core=sib)
    chain_a.step(farthest(g, GROUPS - 2))
    q_across.wait_recv()
    q_sum[...] = (q_keep[x] + q_in[x].astype(f32) + q_x[...].astype(f32)).astype(bf16)
    q_over = begin(q_sum, q_y, q_send.at[2], q_recv.at[2], r=far_r)
    v_move.wait_recv()
    v_pass[...] = (v_keep[other] + v_in[other].astype(f32)).astype(bf16)
    v_across = begin(v_pass, v_x, v_send.at[1], v_recv.at[1], x=other)
    chain_b.step(farthest(g, 0))
    chain_b.step(farthest(g, 1))
    chain_a.step(g)

    grad_first = total_a[...]
    values = tokens_ref[...].astype(f32)
    mean = jnp.mean(values, axis=-1, keepdims=True)
    centred = values - mean
    scale = lax.rsqrt(jnp.mean(centred * centred, axis=-1, keepdims=True) + EPS)
    n1 = centred * scale
    pulled = grad_first * small_ref[0:1]
    inward = pulled - jnp.mean(pulled, axis=-1, keepdims=True) - n1 * jnp.mean(pulled * n1, axis=-1, keepdims=True)
    tokens_grad_ref[...] = mgrad_ref[...] + inward * scale
    sums_ref[0:1] = jnp.sum(grad_first * n1, axis=0, keepdims=True)
    sums_ref[1:2] = jnp.sum(grad_first, axis=0, keepdims=True)
    s_sib = begin(sums_ref, sums_got.at[0], s_send.at[0], s_recv.at[0], core=sib)

    def q_slot(z):
        return qout_ref.at[core, z]

    def v_slot(z):
        return kvout_ref.at[core, z]

    def b_slot(z):
        return big_ref.at[core, r, z]

    ring_q = Ring(g, x, q_slot, rq_own, rq_send, rq_recv)
    ring_v = Ring(g, x, v_slot, rv_own, rv_send, rv_recv)
    ring_b = Ring(g, x, b_slot, rb_own, rb_send, rb_recv)

    def store(value_ref, slot, sem):
        copy = pltpu.make_async_copy(value_ref, slot, sem)
        copy.start()
        copy.wait()

    settled(q_over)
    q_sum[...] = (q_sum[...].astype(f32) + q_y[...].astype(f32)).astype(bf16)
    store(q_sum, q_slot(g), l_sem.at[0])
    ring_q.start()
    begin(q_slot(g), q_slot(g), qs_send.at[0], qs_recv.at[0], core=sib)

    chain_b.step(farthest(g, 2))
    v_across.wait_recv()
    v_sum[...] = (v_keep[x] + v_in[x].astype(f32) + v_x[...].astype(f32)).astype(bf16)
    v_over = begin(v_sum, v_y, v_send.at[2], v_recv.at[2], r=far_r)
    chain_b.step(g)
    unit[...] = total_b[...].astype(bf16)
    up_rows = 96 + 48 * other
    u_move = begin(
        unit.at[pl.ds(up_rows, 48)], big_ref.at[core, r, g, pl.ds(96 + 48 * x, 48)], u_send.at[0], u_recv.at[0], x=other
    )
    copies = [
        pltpu.make_async_copy(unit.at[pl.ds(0, 96)], big_ref.at[core, r, g, pl.ds(0, 96)], l_sem.at[1]),
        pltpu.make_async_copy(
            unit.at[pl.ds(96 + 48 * x, 48)], big_ref.at[core, r, g, pl.ds(96 + 48 * x, 48)], l_sem.at[2]
        ),
        pltpu.make_async_copy(unit.at[pl.ds(192, 24)], big_ref.at[core, r, g, pl.ds(192, 24)], l_sem.at[3]),
    ]
    for copy in copies:
        copy.start()
    settled(s_sib)
    sums_ref[...] += sums_got[0]
    s_x = begin(sums_ref, sums_got.at[1], s_send.at[1], s_recv.at[1], x=other)
    for copy in copies:
        copy.wait()
    there = big_ref.at[core, r, g, pl.ds(up_rows, 48)]
    arrived(there, u_send.at[0], u_recv.at[0], x)
    ring_b.start()

    def spread_b(z, step):
        begin(b_slot(z), b_slot(z), fy_send.at[step], fy_recv.at[step], r=far_r)
        begin(b_slot(z), b_slot(z), fs_send.at[0, step], fs_recv.at[0, step], core=sib)

    def spread_far(z, step):
        what = big_ref.at[core, far_r, z]
        arrived(what, fy_send.at[step], fy_recv.at[step], x)
        begin(what, what, fs_send.at[1, step], fs_recv.at[1, step], core=sib)

    spread_b(g, 0)
    settled(v_over)
    v_sum[...] = (v_sum[...].astype(f32) + v_y[...].astype(f32)).astype(bf16)
    store(v_sum, v_slot(g), l_sem.at[0])
    ring_v.start()
    begin(v_slot(g), v_slot(g), vs_send.at[0], vs_recv.at[0], core=sib)
    settled(s_x)
    sums_ref[...] += sums_got[1]
    s_y = begin(sums_ref, sums_got.at[2], s_send.at[2], s_recv.at[2], r=far_r)
    for step in range(1, GROUPS):
        z = ring_q.step(step)
        begin(q_slot(z), q_slot(z), qs_send.at[step], qs_recv.at[step], core=sib)
        if step == 1:
            settled(s_y)
            sums_ref[...] += sums_got[2]
            for away in range(1, GROUPS):
                begin(
                    sums_ref, sums_got.at[2 + away], s_send.at[2 + away], s_recv.at[2 + away],
                    g=lax.rem(g + away, GROUPS),
                )
        z = ring_b.step(step)
        spread_b(z, step)
        spread_far(nearest(g, step - 1), step - 1)
        z = ring_v.step(step)
        begin(v_slot(z), v_slot(z), vs_send.at[step], vs_recv.at[step], core=sib)
    spread_far(nearest(g, GROUPS - 1), GROUPS - 1)

    for away in range(1, GROUPS):
        arrived(sums_got.at[2 + away], s_send.at[2 + away], s_recv.at[2 + away], x)
    for step in range(GROUPS):
        z = nearest(g, step)
        arrived(qout_ref.at[sib, z], qs_send.at[step], qs_recv.at[step], x)
        arrived(kvout_ref.at[sib, z], vs_send.at[step], vs_recv.at[step], x)
        arrived(big_ref.at[sib, r, z], fs_send.at[0, step], fs_recv.at[0, step], x)
        arrived(big_ref.at[sib, far_r, z], fs_send.at[1, step], fs_recv.at[1, step], x)
    for move in pending:
        move.wait_send()
    for item in (chain_a, chain_b, ring_q, ring_v, ring_b):
        item.finish()
    sums_ref[...] += sums_got[3] + sums_got[4] + sums_got[5]


def scatter(dkv, dq, normed, wfull, tokens, mgrad, small, bundle, sums):
    rows, width = tokens.shape
    fourth = width // 4
    dma = pltpu.SemaphoreType.DMA
    wide_q, wide_v = 2 * BLK, 2 * HW
    kv_block = (rows, wide_v)
    full = (rows, width)
    unit = (UNIT, width)

    def weight_scratch(wide):
        return [
            pltpu.VMEM((2, fourth, wide), f32),
            pltpu.VMEM((2, fourth, wide), bf16),
            pltpu.VMEM((2, fourth, wide), bf16),
            *[pltpu.VMEM((fourth, wide), bf16)] * 4,
        ]

    return pl.pallas_call(
        scatter_kernel,
        out_shape=(
            jax.ShapeDtypeStruct(full, f32),
            jax.ShapeDtypeStruct((2, 2, GROUPS, *unit), bf16),
            jax.ShapeDtypeStruct((2, GROUPS, fourth, wide_q), bf16),
            jax.ShapeDtypeStruct((2, GROUPS, fourth, wide_v), bf16),
            jax.ShapeDtypeStruct((24, width), f32),
        ),
        in_specs=[anywhere()] + [whole_vmem()] * 8,
        out_specs=(whole_vmem(), anywhere(), anywhere(), anywhere(), whole_vmem()),
        scratch_shapes=[
            pltpu.VMEM((GROUPS, 4, *kv_block), bf16),
            pltpu.VMEM((GROUPS, 4, *kv_block), bf16),
            pltpu.VMEM((GROUPS, 2, *kv_block), f32),
            pltpu.VMEM((GROUPS, 2, *kv_block), bf16),
            pltpu.VMEM((GROUPS, 2, *kv_block), bf16),
            pltpu.VMEM((GROUPS, *kv_block), bf16),
            pltpu.VMEM((GROUPS, *kv_block), bf16),
            pltpu.VMEM((GROUPS, *full), f32),
            pltpu.VMEM(full, f32),
            pltpu.VMEM((2, GROUPS, *full), bf16),
            pltpu.VMEM((GROUPS, *full), bf16),
            pltpu.VMEM((width, wide_v), f32),
            pltpu.VMEM((GROUPS, *unit), bf16),
            pltpu.VMEM((GROUPS, *unit), f32),
            pltpu.VMEM(unit, f32),
            pltpu.VMEM((2, GROUPS, *unit), bf16),
            pltpu.VMEM((GROUPS, *unit), bf16),
            pltpu.VMEM(unit, bf16),
            *weight_scratch(wide_q),
            *weight_scratch(wide_v),
            pltpu.VMEM((6, 24, width), f32),
            dma((GROUPS, 4)), dma((GROUPS, 4)), dma((GROUPS, 4)), dma((GROUPS,)), dma((GROUPS,)), dma((GROUPS,)), dma((GROUPS,)),
            dma((GROUPS,)), dma((2, GROUPS)),
            dma((GROUPS,)), dma((GROUPS,)), dma((GROUPS,)), dma((2, GROUPS)), dma((1,)), dma((1,)), dma((2,)), dma((GROUPS,)), dma((GROUPS,)),
            dma((GROUPS,)), dma((GROUPS,)), dma((2, GROUPS)), dma((2, GROUPS)),
            dma((3,)), dma((3,)), dma((2,)), dma((GROUPS,)), dma((GROUPS,)), dma((GROUPS,)), dma((GROUPS,)),
            dma((3,)), dma((3,)), dma((2,)), dma((GROUPS,)), dma((GROUPS,)), dma((GROUPS,)), dma((GROUPS,)),
            dma((6,)), dma((6,)), dma((4,)),
        ],
        compiler_params=pltpu.CompilerParams(
            collective_id=2, has_side_effects=True, vmem_limit_bytes=51 << 20
        ),
        name="scatter",
    )(dkv, dq, normed, wfull, tokens, mgrad, small, bundle, sums)


def pack_kv(key_part, value_part):
    return jnp.concatenate(
        [key_part, value_part[..., 2 * DH :], value_part[..., : 2 * DH]], axis=-1
    )


def unpack_kv(both):
    return both[..., :HW], jnp.concatenate([both[..., HW + DH :], both[..., HW : HW + DH]], axis=-1)


def layout_kernel(
    big_ref, query_ref, kv_ref, sums_ref,
    up_out, down_out, wo_out, query_out, key_out, value_out,
    low_gain, low_shift, query_bias, value_bias, out_bias, high_gain, high_shift, up_bias, down_bias,
):
    x = lax.axis_index("x")
    width = big_ref.shape[-1]
    half = width // 2
    for core in range(2):
        down_out[core] = big_ref[core, 0, 0:96].astype(f32)
        wo_out[core] = big_ref[core, 0, 192:UNIT].astype(f32)
        for owner in range(2):
            lane = (2 * owner + core) * width
            up_out[:, lane : lane + width] = big_ref[core, 0, 96 + 48 * owner : 144 + 48 * owner].astype(f32)
        query_out[core] = jnp.concatenate(
            [query_ref[core, z].astype(f32)[:, :HW] for z in range(GROUPS)], axis=1
        )
        both = [unpack_kv(kv_ref[core, z].astype(f32)) for z in range(GROUPS)]
        key_out[core] = jnp.concatenate([item[0] for item in both], axis=1)
        value_out[core] = jnp.concatenate([item[1] for item in both], axis=1)

    @pl.when(pl.program_id(0) == 0)
    def _():
        def own_half(row):
            whole = sums_ref[row : row + 1]
            return jnp.where(x == 0, whole[:, :half], whole[:, half:])

        for ref, row in (
            (low_gain, 0), (low_shift, 1), (out_bias, 2), (high_gain, 3), (high_shift, 4), (down_bias, 5),
        ):
            ref[...] = own_half(row)
        pair = [sums_ref[pl.ds(16 + 2 * x + i, 1)] for i in range(2)]
        query_bias[...] = jnp.concatenate([item[:, :HW] for item in pair], axis=1)
        value_bias[...] = jnp.concatenate(
            [unpack_kv(item[:, 2 * BLK : 2 * BLK + 2 * HW])[1] for item in pair], axis=1
        )
        up_bias[...] = jnp.concatenate([sums_ref[pl.ds(8 + 2 * x + i, 1)] for i in range(2)], axis=1)


def lay_out(big, query, kv, sums):
    width = big.shape[-1]
    half, fourth = width // 2, width // 4
    rows = fourth // PARTS

    def spec(shape, index):
        return pl.BlockSpec(shape, index)

    def fixed(wide):
        return pl.BlockSpec((1, wide), lambda p: (0, 0))

    narrow = spec((2, rows, width), lambda p: (0, p, 0))
    vector = jax.ShapeDtypeStruct((1, half), f32)
    return pl.pallas_call(
        layout_kernel,
        grid=(PARTS,),
        out_shape=(
            jax.ShapeDtypeStruct((half, 4 * width), f32),
            jax.ShapeDtypeStruct((2, width, width), f32),
            *[jax.ShapeDtypeStruct((2, fourth, width), f32)] * 4,
            *[vector] * 7,
            jax.ShapeDtypeStruct((1, 2 * width), f32),
            vector,
        ),
        in_specs=[
            spec((2, 1, UNIT, width), lambda p: (0, p, 0, 0)),
            spec((2, GROUPS, rows, query.shape[-1]), lambda p: (0, 0, p, 0)),
            spec((2, GROUPS, rows, kv.shape[-1]), lambda p: (0, 0, p, 0)),
            spec(sums.shape, lambda p: (0, 0)),
        ],
        out_specs=(
            spec((48, 4 * width), lambda p: (p, 0)),
            spec((2, 96, width), lambda p: (0, p, 0)),
            *[narrow] * 4,
            *[fixed(half)] * 7,
            fixed(2 * width),
            fixed(half),
        ),
        compiler_params=pltpu.CompilerParams(
            vmem_limit_bytes=12 << 20, dimension_semantics=("arbitrary",)
        ),
        name="lay_out",
    )(big, query, kv, sums)


ROWS = ("s", "r", "core", "x")
ALL = ("g", "s", "r", "core", "x")


def shards(
    tokens, cotangent, doc_lengths, deal, first_gain, first_shift, query_weight, query_bias,
    key_weight, value_weight, value_bias, output_weight, output_bias, second_gain, second_shift,
    up_weight, up_bias, down_weight, down_bias,
):
    rows, width = tokens.shape
    half = width // 2
    blocks = deal.shape[0]
    lines = jnp.concatenate(
        [
            first_gain, first_shift, output_bias, second_gain, second_shift, down_bias, query_bias, value_bias, up_bias,
        ]
    ).reshape(-1, half)
    kv, q, normed, small, wfull, up, wo = gather(
        tokens, query_weight, key_weight, value_weight, lines, up_weight, output_weight
    )
    wide = blocks > 8 * 2 * GROUPS
    if wide:
        kv = lax.all_gather(kv, "s", axis=0, tiled=True)
    kv = kv.reshape(blocks, BLK, 2 * HW)
    q = q.reshape(2 * GROUPS, BLK, 2 * BLK)
    out_t, kept, lse = attend_forward(deal, doc_lengths, q, kv)
    result, grad_middle, grad_t, bundle, sums = dense(
        out_t, tokens, cotangent, small, up, wo, down_weight
    )
    dq, dkv = attend_backward(deal, doc_lengths, q, kv, lse, grad_t, kept)
    dkv = dkv.reshape(-1, GROUPS, rows, 2 * HW)
    if wide:
        dkv = lax.psum_scatter(dkv, "s", scatter_dimension=0, tiled=True)
    dq = dq.reshape(GROUPS, rows, 2 * BLK)
    grad_tokens, big, query_own, kv_own, sums = scatter(
        dkv, dq, normed, wfull, tokens, grad_middle, small, bundle, sums
    )
    if wide:
        big, query_own, kv_own, sums = (
            lax.psum(item, "s") for item in (big, query_own, kv_own, sums)
        )

    (
        up_own, down_own, wo_own, query_own, key_own, value_own,
        low_gain, low_shift, query_sum, value_sum, out_sum, high_gain, high_shift, up_sum, down_sum,
    ) = lay_out(big.reshape(2, PARTS, UNIT, width), query_own, kv_own, sums)

    def flat(item):
        return item.reshape(-1, width)

    def line(item):
        return item.reshape(-1)

    return (
        result,
        grad_tokens,
        line(low_gain),
        line(low_shift),
        flat(query_own),
        line(query_sum),
        flat(key_own),
        flat(value_own),
        line(value_sum),
        flat(wo_own),
        line(out_sum),
        line(high_gain),
        line(high_shift),
        up_own,
        line(up_sum),
        flat(down_own),
        line(down_sum),
    )


def solution(mesh):
    devices = mesh.devices
    inner_mesh = Mesh(devices.reshape(GROUPS, devices.shape[0] // (4 * GROUPS), 2, 2, 2), ALL)
    row = P(ALL, None)
    mat = P("x", None)
    vec = P("x")
    in_specs = (
        row, row, P(), P(), vec, vec, mat, vec, mat, mat, vec, mat, vec, vec, vec, mat, vec, mat, vec,
    )
    out_specs = (
        row, row, vec, vec, mat, vec, mat, mat, vec, mat, vec, vec, vec, mat, vec, mat, vec,
    )
    return jax.shard_map(
        shards, mesh=inner_mesh, in_specs=in_specs, out_specs=out_specs, check_vma=False
    )
```

profile of v0, /device:TPU:0, one launch (start us, length us, event | category | flops | bytes accessed | tf_op | source)
XLA Modules:
  0.0 361.4 jit_solution(6497003650632141245)
XLA Ops:
  0.7 0.9 dynamic-update-slice
  1.5 0.9 dynamic-update-slice.1
  2.4 0.9 dynamic-update-slice.2
  3.3 0.9 dynamic-update-slice.3
  4.1 0.9 dynamic-update-slice.4
  5.0 0.9 dynamic-update-slice.5
  5.8 0.9 dynamic-update-slice.6
  6.7 0.9 dynamic-update-slice.7
  8.3 1.0 copy-done.2
  9.3 1.7 copy-done.5
  10.9 1.1 copy-done.11
  12.0 1.1 copy-done.12
  13.1 1.1 copy-done.13
  14.1 1.1 copy-done.14
  15.2 62.6 %gather.1 = (bf16[8,4,256,384]{3,2,1,0:T(8,128)(2,1)S(1)}, bf16[4,256,256]{2,1,0:T(8,128)(2,1)S(1)}, bf16[4,256,768]{2,1,0:T(8,128)(2,1)S(1)}, f32[16,768]{1,0:T...) custom-call(bf16[256,768]{1,0:T(8,128)(2,1)S(1)} %copy-done.2, ...), custom_call_target="tpu_custom_call" | custom-call | tf_op jit(solution)/shard_map/gather/pallas_call | solution.py:570
  77.9 28.3 %attend_forward.1 = (bf16[8,192,128]{2,1,0:T(8,128)(2,1)S(1)}, f32[8,192,128]{2,1,0:T(8,128)S(1)}, f32[8,1,384]{2,1,0:T(1,128)S(1)}) custom-call(s32[64]{0:T(128)S(1)} %copy-done.16, s32[4]{0:T(128)S(1)} %copy-done.17, bf16[8,128,256]{2,1,0:T(8,128)(2,1)S(1)} %bitcast.14, bf16[64,128,384]{2,1,0:T(8,128)(2,1)S(1)} %bitcast.10), custom_call_target="tpu_custom_call" | custom-call | tf_op jit(solution)/shard_map/attend_forward/pallas_call | solution.py:182
  106.2 52.5 %dense.1 = (bf16[256,768]{1,0:T(8,128)(2,1)S(1)}, f32[256,768]{1,0:T(8,128)S(1)}, bf16[8,192,128]{2,1,0:T(8,128)(2,1)S(1)}, bf16[2,4,216,768]{3,2,1,0:T(8,128)(2,1)S(1)}, f32[16,768]{1,0:T(8,128)S(1)}) custom-call(bf16[8,192,128]{2,1,0:T(8,128)(2,1)S(1)} %get-tuple-element.56.out_t_ref, bf16[256,768]{1,0:T(8,128)(2,1)S(1)} %copy-done.3, ...), custom_call_target="tpu_custom_call" | custom-call | tf_op jit(solution)/shard_map/dense/pallas_call | solution.py:803
  158.8 35.1 %attend_backward.1 = (bf16[8,128,256]{2,1,0:T(8,128)(2,1)S(1)}, bf16[64,128,384]{2,1,0:T(8,128)(2,1)S(1)}) custom-call(s32[64]{0:T(128)S(1)} %copy-done.16, s32[4]{0:T(128)S(1)} %copy-done.17, bf16[8,128,256]{2,1,0:T(8,128)(2,1)S(1)} %bitcast.15, bf16[64,128,384]{2,1,0:T(8,128)(2,1)S(1)} %bitcast.11, f32[8,1,384]{2,1,0:T(1,128)S(1)} %get-tuple-element.61.lse_ref, ...), custom_call_target="tpu_custom_call" | custom-call | tf_op jit(solution)/shard_map/attend_backward/pallas_call | solution.py:293
  193.9 2.7 copy-done
  196.6 147.4 %scatter.1 = (f32[256,768]{1,0:T(8,128)S(1)}, bf16[2,2,4,216,768]{4,3,2,1,0:T(8,128)(2,1)}, bf16[2,4,192,256]{3,2,1,0:T(8,128)(2,1)S(1)}, bf16[2,4,192,384]{3,2,1,0:T(8,128)(2,1)}, f32[24,768]{1,0:T(8,128)S(1)}) custom-call(bf16[8,4,256,384]{3,2,1,0:T(8,128)(2,1)} %bitcast.12, bf16[4,256,256]{2,1,0:T(8,128)(2,1)S(1)} %bitcast.16, ...), custom_call_target="tpu_custom_call" | custom-call | tf_op jit(solution)/shard_map/scatter/pallas_call | solution.py:1213
  344.0 2.5 copy-done.1
  346.5 1.3 copy-done.8
  347.7 6.7 %lay_out.1 = (f32[384,3072]{1,0:T(8,128)}, f32[2,768,768]{2,1,0:T(8,128)}, f32[2,192,768]{2,1,0:T(8,128)}, f32[2,192,768]{2,1,0:T(8,128)}, f32[2,192,768]{2,1,0:...) custom-call(bf16[2,8,216,768]{3,2,1,0:T(8,128)(2,1)S(1)} %bitcast.13, ...), custom_call_target="tpu_custom_call" | custom-call | tf_op jit(solution)/shard_map/lay_out/pallas_call | solution.py:1323
  360.6 0.9 copy.48
  (40 shorter events, 6.9 us)
Async XLA Ops:
  8.3 1.0 copy-start.2
  9.3 1.7 copy-start.5
  10.9 1.1 copy-start.11
  12.0 1.1 copy-start.12
  13.1 1.1 copy-start.13
  14.1 1.1 copy-start.14
  15.2 62.6 %copy-start.16 = (s32[64]{0:T(128)S(1)}, s32[64]{0:T(128)}, u32[]{:S(2)}) copy-start(s32[64]{0:T(128)} %deal_ref.3) | copy-start | bytes 772
  15.2 62.7 %copy-start.17 = (s32[4]{0:T(128)S(1)}, s32[4]{0:T(128)}, u32[]{:S(2)}) copy-start(s32[4]{0:T(128)} %lengths_ref.3) | copy-start | bytes 52
  77.8 28.4 %copy-start.7 = (bf16[4,256,768]{2,1,0:T(8,128)(2,1)}, bf16[4,256,768]{2,1,0:T(8,128)(2,1)S(1)}, u32[]{:S(2)}) copy-start(bf16[4,256,768]{2,1,0:T(8,128)(2,1)S(1)} %get-tuple-element.66.normed_ref) | copy-start | bytes 4718596
  77.8 28.4 %copy-start.9 = (bf16[768,640]{1,0:T(8,128)(2,1)}, bf16[768,640]{1,0:T(8,128)(2,1)S(1)}, u32[]{:S(2)}) copy-start(bf16[768,640]{1,0:T(8,128)(2,1)S(1)} %get-tuple-element.67.wfull_ref) | copy-start | bytes 2949124
  77.8 28.3 %copy-start.3 = (bf16[256,768]{1,0:T(8,128)(2,1)S(1)}, bf16[256,768]{1,0:T(8,128)(2,1)}, u32[]{:S(2)}) copy-start(bf16[256,768]{1,0:T(8,128)(2,1)} %tokens_ref.5) | copy-start | bytes 1179652
  77.9 28.3 %copy-start.6 = (bf16[1536,768]{1,0:T(8,128)(2,1)S(1)}, bf16[1536,768]{1,0:T(8,128)(2,1)}, u32[]{:S(2)}) copy-start(bf16[1536,768]{1,0:T(8,128)(2,1)} %down_any.1) | copy-start | bytes 7077892
  77.9 28.3 %copy-start.15 = (bf16[256,768]{1,0:T(8,128)(2,1)S(1)}, bf16[256,768]{1,0:T(8,128)(2,1)}, u32[]{:S(2)}) copy-start(bf16[256,768]{1,0:T(8,128)(2,1)} %cot_ref.1) | copy-start | bytes 1179652
  158.7 35.2 %copy-start.4 = (bf16[2,4,216,768]{3,2,1,0:T(8,128)(2,1)}, bf16[2,4,216,768]{3,2,1,0:T(8,128)(2,1)S(1)}, u32[]{:S(2)}) copy-start(bf16[2,4,216,768]{3,2,1,0:T(8,128)(2,1)S(1)} %get-tuple-element.69.bundle_ref) | copy-start | bytes 7962628
  158.8 35.2 %copy-start.10 = (f32[256,768]{1,0:T(8,128)}, f32[256,768]{1,0:T(8,128)S(1)}, u32[]{:S(2)}) copy-start(f32[256,768]{1,0:T(8,128)S(1)} %get-tuple-element.68.mgrad_ref) | copy-start | bytes 2359300
  193.9 2.7 copy-start
  344.0 2.5 copy-start.1
  346.5 1.3 copy-start.8
where the time goes:
time: 361 us
  Pallas kernels  333 us (92%)
  local copies, waits for them, and re-layouts  22.6 us (6%)
  other arithmetic  5.38 us (1%)
    pallas_call x1, Pallas kernels, scatter(): pl.pallas_call(scatter_kernel, out_shape=(jax.ShapeDtypeStruct(full, f32)...  147 us
    pallas_call x1, Pallas kernels, gather(): pl.pallas_call(gather_kernel, out_shape=(jax.ShapeDtypeStruct((8, GROUPS,...  62.6 us
    pallas_call x1, Pallas kernels, dense(): pl.pallas_call(dense_kernel, out_shape=(jax.ShapeDtypeStruct(full, bf16),...  52.5 us
    pallas_call x1, Pallas kernels, attend_backward(): pl.pallas_call(backward_kernel, out_shape=(jax.ShapeDtypeStruct((slots, B...  35.1 us
    pallas_call x1, Pallas kernels, attend_forward(): pl.pallas_call(forward_kernel, out_shape=(jax.ShapeDtypeStruct((slots, HW...  28.3 us
    unnamed x46, local copies, waits for them, and re-layouts  21.9 us

commit v1 on v0

--- a/solution.py
+++ b/solution.py
@@ -201,6 +201,7 @@
 def backward_kernel(
     deal_ref, lengths_ref, q_ref, kv_ref, lse_ref, do_ref, wide_ref,
     dq_ref, dkv_ref, where_ref, text_ref, low_ref, high_ref, first_ref, qt_ref, qm_ref, dot_ref, dom_ref, delta_ref, acc_ref, dk_acc, dv_acc,
+    packed_ref, out_sem,
 ):
     survey(deal_ref, lengths_ref, where_ref, text_ref, low_ref, high_ref, first_ref)
     slots = q_ref.shape[0]
@@ -236,7 +237,12 @@
 
     lax.fori_loop(0, slots, ready, 0)
 
-    def one_chunk(chunk, _):
+    def written(chunk, i):
+        return pltpu.make_async_copy(
+            packed_ref.at[chunk % 2, i], dkv_ref.at[where_ref[2 * chunk + i]], out_sem.at[chunk % 2, i]
+        )
+
+    def one_chunk(chunk, kept):
         part = load_chunk(kv_ref, where_ref, chunk)
         keys = part[:, : 2 * BLK]
         vals = part[:, BLK:]
@@ -269,11 +275,21 @@
             ],
             axis=1,
         ).astype(bf16)
-        dkv_ref[where_ref[2 * chunk]] = packed[:BLK]
-        dkv_ref[where_ref[2 * chunk + 1]] = packed[BLK:]
-        return _
+
+        @pl.when(chunk >= 2)
+        def _():
+            for i in range(2):
+                written(chunk - 2, i).wait()
+
+        for i in range(2):
+            packed_ref[chunk % 2, i] = packed[BLK * i : BLK * i + BLK]
+            written(chunk, i).start()
+        return kept
 
     lax.fori_loop(0, chunks, one_chunk, 0)
+    for last in range(2):
+        for i in range(2):
+            written(chunks - 2 + last, i).wait()
 
     def finish(slot, _):
         total = acc_ref[slot]
@@ -297,7 +313,7 @@
             jax.ShapeDtypeStruct(kv.shape, bf16),
         ),
         in_specs=[whole_smem()] * 2 + [whole_vmem()] * 5,
-        out_specs=(whole_vmem(),) * 2,
+        out_specs=(whole_vmem(), in_hbm()),
         scratch_shapes=[
             *survey_scratch(kv.shape[0]),
             pltpu.VMEM((slots, 2 * BLK, WIDE), bf16),
@@ -308,9 +324,11 @@
             pltpu.VMEM((slots, HW, WIDE), f32),
             pltpu.VMEM((CHUNK, 2 * BLK), f32),
             pltpu.VMEM((CHUNK, 2 * BLK), f32),
+            pltpu.VMEM((2, 2, BLK, 2 * HW), bf16),
+            pltpu.SemaphoreType.DMA((2, 2)),
         ],
         compiler_params=pltpu.CompilerParams(
-            vmem_limit_bytes=min((17 << 20) + kv.size // 5 * 21, VMEM_LIMIT + (4 << 20))
+            vmem_limit_bytes=max(48 << 20, (17 << 20) + kv.size * 2)
         ),
         name="attend_backward",
     )(deal, lengths, q, kv, lse, grad_t, wide)
@@ -362,37 +380,36 @@
     return picked
 
 
-def prepare(g, x, query_ref, key_ref, value_ref, lines_ref, narrow_ref, small_ref):
-    half = lines_ref.shape[1]
+def prepare(g, x, weights, lines, narrow_ref, small_ref):
+    half = weights.shape[1]
     odd = lax.rem(g, 2) == 1
 
-    def columns(ref):
+    def columns(i):
         low = pl.multiple_of(3 * g // 2 * BLK, BLK)
-        window = ref[:, pl.ds(low, 2 * BLK)]
+        window = weights[i, :, pl.ds(low, 2 * BLK)]
         moved = jnp.concatenate([window[:, DH:], window[:, :DH]], axis=1)
         return jnp.where(odd, moved, window)
 
     lane = lax.broadcasted_iota(jnp.int32, (half, 2 * BLK), 1)
-    query = columns(query_ref)
+    query = columns(0)
     narrow_ref[:, : 2 * BLK] = jnp.where(lane < HW, query, jnp.zeros_like(query))
-    narrow_ref[:, 2 * BLK :] = pack_kv(columns(key_ref)[:, :HW], columns(value_ref)[:, :HW])
-
-    lines = lines_ref[...].astype(f32)
+    narrow_ref[:, 2 * BLK :] = pack_kv(columns(1)[:, :HW], columns(2)[:, :HW])
+
+    def line(i):
+        return lines[i][...].astype(f32).reshape(1, -1)
+
     zero = jnp.zeros((1, half), f32)
     small_ref[...] = jnp.zeros_like(small_ref)
     for row in range(6):
-        line = lines[row : row + 1]
         small_ref[row : row + 1] = jnp.where(
-            x == 0, jnp.concatenate([line, zero], axis=1), jnp.concatenate([zero, line], axis=1)
+            x == 0, jnp.concatenate([line(row), zero], axis=1), jnp.concatenate([zero, line(row)], axis=1)
         )
+    ups = line(8)
     for i in range(2):
-        small_ref[pl.ds(8 + 2 * x + i, 1)] = jnp.concatenate(
-            [lines[8 + 2 * i : 9 + 2 * i], lines[9 + 2 * i : 10 + 2 * i]], axis=1
-        )
-
-    def part(row):
-        line = lines[row : row + 1]
-        mine = jnp.where(odd, line[:, HW:], line[:, :HW])
+        small_ref[pl.ds(8 + 2 * x + i, 1)] = ups[:, 2 * half * i : 2 * half * i + 2 * half]
+
+    def part(i):
+        mine = jnp.where(odd, line(i)[:, HW:], line(i)[:, :HW])
         return jnp.where(g // 2 == x, mine, jnp.zeros_like(mine))
 
     value = part(7)
@@ -402,10 +419,10 @@
 
 
 def gather_kernel(
-    tokens_ref, query_ref, key_ref, value_ref, lines_ref, up_ref, wo_ref,
+    tokens_ref, query_any, key_any, value_any, up_ref, wo_ref, l0, l1, l2, l3, l4, l5, l6, l7, l8,
     kv_ref, q_ref, normed_ref, small_out, wfull, up_out, wo_out,
-    lined, narrow_ref, small_ref, small_in, kvs,
-    z_own, z_send, z_recv, s_sem, n_send, n_recv, kv_send, kv_recv, kv_local, w_send, w_recv, w_local,
+    lined, attn_w, narrow_ref, small_ref, small_in, kvs,
+    z_own, z_send, z_recv, s_sem, n_send, n_recv, kv_send, kv_recv, kv_local, w_send, w_recv, w_local, a_sem,
 ):
     g, r, core, x = place()
     other = 1 - x
@@ -413,6 +430,11 @@
     half = width // 2
     fourth = half // 2
     eighth = half // 4
+    loads = [
+        pltpu.make_async_copy(ref, attn_w.at[i], a_sem.at[i]) for i, ref in enumerate((query_any, key_any, value_any))
+    ]
+    for load in loads:
+        load.start()
     greet(g, r, core, x, False)
 
     def along(source, away, sem):
@@ -422,7 +444,9 @@
     pl.when(g > 0)(lambda: along(g, -1, z_own.at[0]).start())
     pl.when(g < GROUPS - 1)(lambda: along(g, 1, z_own.at[1]).start())
 
-    prepare(g, x, query_ref, key_ref, value_ref, lines_ref, narrow_ref, small_ref)
+    for load in loads:
+        load.wait()
+    prepare(g, x, attn_w, (l0, l1, l2, l3, l4, l5, l6, l7, l8), narrow_ref, small_ref)
     small_move = send(small_ref, small_in, s_sem.at[0], s_sem.at[1], x=other)
     small_move.start()
     mine = pl.ds(x * half + core * fourth, fourth)
@@ -562,7 +586,11 @@
     return pl.BlockSpec(memory_space=pl.ANY)
 
 
-def gather(tokens, query, key, value, lines, up, wo):
+def in_hbm():
+    return pl.BlockSpec(memory_space=pltpu.HBM)
+
+
+def gather(tokens, query, key, value, up, wo, *lines):
     rows, width = tokens.shape
     wide = 2 * BLK + 2 * HW
     small = (16, width)
@@ -578,22 +606,23 @@
             jax.ShapeDtypeStruct((width, width), bf16),
             jax.ShapeDtypeStruct((width, width), bf16),
         ),
-        in_specs=[whole_vmem()] * 5 + [anywhere()] * 2,
+        in_specs=[whole_vmem(), *[in_hbm()] * 5, *[whole_vmem()] * len(lines)],
         out_specs=(anywhere(), *(whole_vmem(),) * 4, anywhere(), anywhere()),
         scratch_shapes=[
             pltpu.VMEM((GROUPS, rows, width), bf16),
+            pltpu.VMEM((3, width // 2, width), bf16),
             pltpu.VMEM((width // 2, wide), bf16),
             pltpu.VMEM(small, f32),
             pltpu.VMEM(small, f32),
             pltpu.VMEM((GROUPS, rows, 2 * HW), bf16),
             dma((2,)), dma((GROUPS,)), dma((GROUPS,)), dma((2,)), dma((2,)), dma((2,)),
-            dma((7, GROUPS)), dma((7, GROUPS)), dma((GROUPS,)), dma((8,)), dma((8,)), dma((2,)),
+            dma((7, GROUPS)), dma((7, GROUPS)), dma((GROUPS,)), dma((8,)), dma((8,)), dma((2,)), dma((3,)),
         ],
         compiler_params=pltpu.CompilerParams(
-            collective_id=0, has_side_effects=True, vmem_limit_bytes=14 << 20
+            collective_id=0, has_side_effects=True, vmem_limit_bytes=60 << 20
         ),
         name="gather",
-    )(tokens, query, key, value, lines, up, wo)
+    )(tokens, query, key, value, up, wo, *lines)
 
 
 def erf_parts(values):
@@ -607,7 +636,7 @@
 
 def dense_kernel(
     out_t_ref, tokens_ref, cot_ref, small_ref, up_ref, wo_ref, down_any,
-    result_ref, middle_grad_ref, grad_t_ref, bundle_ref, sums_ref,
+    result_ref, middle_grad_ref, grad_t_ref, keep_ref, give_ref, sums_ref,
     down_ref, attn_in, attn_t, cots, h2s, mid_ref, n2_ref, part_y, part_d, in_y, in_d, pass_y, pass_d, x_y, x_d,
     hids, dus, grad_out, wo_keep, wo_give, wo_in, wo_pass, wo_x,
     down_sem, a_send, a_recv, c_send, c_recv, h_send, h_recv, y_send, y_recv, d_send, d_recv, o_send, o_recv,
@@ -725,10 +754,20 @@
 
     down_grad = over_rows(hids, cots)
     up_grad = over_rows(h2s, dus)
-    for p in range(PARTS):
-        bundle_ref[p // GROUPS, p % GROUPS, 0:96] = down_grad[96 * p : 96 * p + 96]
-        bundle_ref[p // GROUPS, p % GROUPS, 96:144] = up_grad[48 * p : 48 * p + 48]
-        bundle_ref[p // GROUPS, p % GROUPS, 144:192] = up_grad[half + 48 * p : half + 48 * p + 48]
+
+    def parts(write):
+        for y in range(2):
+            pl.when(r == y)(lambda: write(keep_ref, y))
+            pl.when(r != y)(lambda: write(give_ref, y))
+
+    def write_dense(ref, y):
+        for z in range(GROUPS):
+            p = y * GROUPS + z
+            ref[z, 0:96] = down_grad[96 * p : 96 * p + 96]
+            ref[z, 96:144] = up_grad[48 * p : 48 * p + 48]
+            ref[z, 144:192] = up_grad[half + 48 * p : half + 48 * p + 48]
+
+    parts(write_dense)
 
     d_sib.wait_recv()
     d_x.wait_recv()
@@ -781,8 +820,13 @@
     mine = wo_keep[x] + wo_in[x].astype(f32)
     w_x.wait_recv()
     wo_sum = (mine + wo_x[...].astype(f32)).astype(bf16)
-    for p in range(PARTS):
-        bundle_ref[p // GROUPS, p % GROUPS, 192:UNIT] = wo_sum[24 * p : 24 * p + 24]
+
+    def write_wo(ref, y):
+        for z in range(GROUPS):
+            p = y * GROUPS + z
+            ref[z, 192:UNIT] = wo_sum[24 * p : 24 * p + 24]
+
+    parts(write_wo)
     for away in range(1, GROUPS):
         source = other_group(away)
         send(
@@ -806,11 +850,12 @@
             jax.ShapeDtypeStruct(full, bf16),
             jax.ShapeDtypeStruct(full, f32),
             jax.ShapeDtypeStruct(out_t.shape, bf16),
-            jax.ShapeDtypeStruct((2, GROUPS, UNIT, width), bf16),
+            jax.ShapeDtypeStruct((GROUPS, UNIT, width), bf16),
+            jax.ShapeDtypeStruct((GROUPS, UNIT, width), bf16),
             jax.ShapeDtypeStruct(small.shape, f32),
         ),
-        in_specs=[whole_vmem()] * 6 + [anywhere()],
-        out_specs=(whole_vmem(),) * 5,
+        in_specs=[whole_vmem()] * 6 + [in_hbm()],
+        out_specs=(whole_vmem(),) * 6,
         scratch_shapes=[
             pltpu.VMEM((width, width), bf16),
             pltpu.VMEM((GROUPS, 2, HW, BLK), bf16),
@@ -934,14 +979,14 @@
 
 
 def scatter_kernel(
-    dkv_ref, dq_ref, normed_ref, wfull_ref, tokens_ref, mgrad_ref, small_ref, bundle_ref, sums_in,
+    dkv_ref, dq_ref, normed_ref, wfull_ref, tokens_ref, mgrad_ref, small_ref, bundle_ref, by_in, sums_in,
     tokens_grad_ref, big_ref, qout_ref, kvout_ref, sums_ref,
     own_kv, sib_kv, keep_x, give_x, in_x, give_y, in_y, part_a, total_a, inward_a, outward_a, wg_kv,
-    by_in, by_sum, total_b, inward_b, outward_b, unit,
+    by_sum, total_b, inward_b, outward_b, unit,
     q_keep, q_give, q_in, q_pass, q_x, q_y, q_sum, v_keep, v_give, v_in, v_pass, v_x, v_y, v_sum,
     sums_got,
     own_sem, k_send, k_recv, x_send, x_recv, y_send, y_recv, ca_send, ca_recv,
-    b_send, b_recv, cb_send, cb_recv, u_send, u_recv, rb_own, rb_send, rb_recv,
+    cb_send, cb_recv, u_send, u_recv, rb_own, rb_send, rb_recv,
     fy_send, fy_recv, fs_send, fs_recv,
     q_send, q_recv, rq_own, rq_send, rq_recv, qs_send, qs_recv,
     v_send, v_recv, rv_own, rv_send, rv_recv, vs_send, vs_recv,
@@ -979,13 +1024,6 @@
             )
             kv_moves.append((own, across))
 
-    def piece(i):
-        z = farthest(g, i)
-        begin(bundle_ref.at[far_r, z], by_in.at[z], b_send.at[i], b_recv.at[i], r=far_r)
-
-    piece(0)
-    piece(1)
-
     def split(total, keep, give, wide):
         for owner in range(2):
             for c in range(2):
@@ -1003,11 +1041,14 @@
     def scaled(c):
         return dq_ref[c] * bf16(SCALE)
 
-    query_total = outer(normed_ref[0], scaled(0))
-    for c in range(1, GROUPS):
-        query_total += outer(normed_ref[c], scaled(c))
-    split(query_total, q_keep, q_give, wide_q)
-    q_move = begin(q_give, q_in, q_send.at[0], q_recv.at[0], core=sib)
+    def query_grad():
+        query_total = outer(normed_ref[0], scaled(0))
+        for c in range(1, GROUPS):
+            query_total += outer(normed_ref[c], scaled(c))
+        split(query_total, q_keep, q_give, wide_q)
+        q_move.start()
+
+    q_move = send(q_give, q_in, q_send.at[0], q_recv.at[0], core=sib)
     sums_ref[...] = jnp.zeros_like(sums_ref)
     sums_ref[0:16] = sums_in[...]
     line_q = scaled(0).astype(f32)
@@ -1016,65 +1057,147 @@
     sums_ref[pl.ds(16 + g, 1), 0:wide_q] = jnp.sum(line_q, axis=0, keepdims=True)
     wg_kv[...] = jnp.zeros_like(wg_kv)
 
-    for i in range(GROUPS):
+    def q_slot(z):
+        return qout_ref.at[core, z]
+
+    def v_slot(z):
+        return kvout_ref.at[core, z]
+
+    def b_slot(z):
+        return big_ref.at[core, r, z]
+
+    ring_q = Ring(g, x, q_slot, rq_own, rq_send, rq_recv)
+    ring_v = Ring(g, x, v_slot, rv_own, rv_send, rv_recv)
+    ring_b = Ring(g, x, b_slot, rb_own, rb_send, rb_recv)
+
+    def store(value_ref, slot, sem):
+        copy = pltpu.make_async_copy(value_ref, slot, sem)
+        copy.start()
+        copy.wait()
+
+    def spread_b(z, step):
+        begin(b_slot(z), b_slot(z), fy_send.at[step], fy_recv.at[step], r=far_r)
+        begin(b_slot(z), b_slot(z), fs_send.at[0, step], fs_recv.at[0, step], core=sib)
+
+    def spread_far(z, step):
+        what = big_ref.at[core, far_r, z]
+        arrived(what, fy_send.at[step], fy_recv.at[step], x)
+        begin(what, what, fs_send.at[1, step], fs_recv.at[1, step], core=sib)
+
+    chain_a = Chain(g, x, total_a, part_a, inward_a, outward_a, ca_send, ca_recv)
+    chain_b = Chain(g, x, total_b, by_sum, inward_b, outward_b, cb_send, cb_recv)
+    at_end = (g == 0) | (g == GROUPS - 1)
+    between = jnp.logical_not(at_end)
+
+    def steps(chain, *which):
+        for i in which:
+            chain.step(farthest(g, i))
+
+    def on_sibling(i):
         for own, across in kv_moves[4 * i : 4 * i + 4]:
             own.wait()
             across.wait_recv()
-        for row in range(2):
-            give_x[i, row] = (
-                own_kv[i, 2 * row + other].astype(f32) + sib_kv[i, 2 * row + other].astype(f32)
-            ).astype(bf16)
-        begin(give_x.at[i], in_x.at[i], x_send.at[i], x_recv.at[i], x=other)
-        for row in range(2):
-            keep_x[i, row] = own_kv[i, 2 * row + x].astype(f32) + sib_kv[i, 2 * row + x].astype(f32)
-        if i == 1:
-            q_move.wait_recv()
-            q_pass[...] = (q_keep[other] + q_in[other].astype(f32)).astype(bf16)
-    q_across = begin(q_pass, q_x, q_send.at[1], q_recv.at[1], x=other)
-
-    chain_a = Chain(g, x, total_a, part_a, inward_a, outward_a, ca_send, ca_recv)
-    chain_b = Chain(g, x, total_b, by_sum, inward_b, outward_b, cb_send, cb_recv)
-
-    def on_x(i):
+
+        def total(row, column):
+            spot = 2 * row + column
+            return own_kv[i, spot].astype(f32) + sib_kv[i, spot].astype(f32)
+
+        for k in range(2):
+            give_x[i, k] = (total(k, other) if i % 2 == 0 else total(far_r, k)).astype(bf16)
+            keep_x[i, k] = total(k, x) if i % 2 == 0 else total(r, k)
+
+    def go_first(i):
+        along = {"x": other} if i % 2 == 0 else {"r": far_r}
+        begin(give_x.at[i], in_x.at[i], x_send.at[i], x_recv.at[i], **along)
+
+    def on_first(i):
         arrived(in_x.at[i], x_send.at[i], x_recv.at[i], x)
-        give_y[i] = (keep_x[i, far_r] + in_x[i, far_r].astype(f32)).astype(bf16)
-        begin(give_y.at[i], in_y.at[i], y_send.at[i], y_recv.at[i], r=far_r)
-        keep_x[i, r] += in_x[i, r].astype(f32)
-
-    def on_y(i):
+        away, stay, along = (far_r, r, {"r": far_r}) if i % 2 == 0 else (other, x, {"x": other})
+        give_y[i] = (keep_x[i, away] + in_x[i, away].astype(f32)).astype(bf16)
+        begin(give_y.at[i], in_y.at[i], y_send.at[i], y_recv.at[i], **along)
+        keep_x[i, stay] += in_x[i, stay].astype(f32)
+
+    def on_second(i):
         c = farthest(g, i)
         arrived(in_y.at[i], y_send.at[i], y_recv.at[i], x)
-        both = (keep_x[i, r] + in_y[i].astype(f32)).astype(bf16)
+        both = (keep_x[i, r if i % 2 == 0 else x] + in_y[i].astype(f32)).astype(bf16)
         part_a[c] = inner(scaled(c), wfull_ref[:, :wide_q]) + inner(both, wfull_ref[:, wide_q:])
         wg_kv[...] += outer(normed_ref[c], both)
         sums_ref[pl.ds(16 + g, 1), wide_q : wide_q + 2 * HW] += jnp.sum(both.astype(f32), axis=0, keepdims=True)
 
-    def on_piece(i):
-        z = farthest(g, i)
-        arrived(by_in.at[z], b_send.at[i], b_recv.at[i], x)
-        by_sum[z] = bundle_ref[r, z].astype(f32) + by_in[z].astype(f32)
-
-    for i in range(GROUPS):
-        on_x(i)
-        if i < 2:
-            piece(2 + i)
-        on_piece(i)
-        if i >= 1:
-            on_y(i - 1)
-        if i >= 2:
-            chain_a.step(farthest(g, i - 2))
-    on_y(GROUPS - 1)
-    split(wg_kv, v_keep, v_give, 2 * HW)
-    v_move = begin(v_give, v_in, v_send.at[0], v_recv.at[0], core=sib)
-    chain_a.step(farthest(g, GROUPS - 2))
+    by_sum[...] = bundle_ref[...].astype(f32) + by_in[...].astype(f32)
+    on_sibling(0)
+    go_first(0)
+    on_sibling(1)
+    go_first(1)
+    pl.when(at_end)(lambda: steps(chain_b, 0, 1, 2))
+    on_sibling(2)
+    on_sibling(3)
+    query_grad()
+    pl.when(between)(lambda: steps(chain_b, 0))
+    on_first(0)
+    on_first(1)
+    go_first(2)
+    go_first(3)
+    settled(q_move)
+    q_pass[...] = (q_keep[other] + q_in[other].astype(f32)).astype(bf16)
+    q_across = begin(q_pass, q_x, q_send.at[1], q_recv.at[1], x=other)
+    on_second(0)
+    on_second(1)
+    pl.when(at_end)(lambda: steps(chain_a, 0, 1))
+    pl.when(between)(lambda: steps(chain_b, 1, 2))
+    on_first(2)
+    on_first(3)
+    chain_b.step(g)
+    unit[...] = total_b[...].astype(bf16)
+    up_rows = 96 + 48 * other
+    begin(unit.at[pl.ds(up_rows, 48)], big_ref.at[core, r, g, pl.ds(96 + 48 * x, 48)], u_send.at[0], u_recv.at[0], x=other)
+    copies = [
+        pltpu.make_async_copy(unit.at[pl.ds(0, 96)], big_ref.at[core, r, g, pl.ds(0, 96)], l_sem.at[1]),
+        pltpu.make_async_copy(
+            unit.at[pl.ds(96 + 48 * x, 48)], big_ref.at[core, r, g, pl.ds(96 + 48 * x, 48)], l_sem.at[2]
+        ),
+        pltpu.make_async_copy(unit.at[pl.ds(192, 24)], big_ref.at[core, r, g, pl.ds(192, 24)], l_sem.at[3]),
+    ]
+    for copy in copies:
+        copy.start()
     q_across.wait_recv()
     q_sum[...] = (q_keep[x] + q_in[x].astype(f32) + q_x[...].astype(f32)).astype(bf16)
     q_over = begin(q_sum, q_y, q_send.at[2], q_recv.at[2], r=far_r)
+    on_second(2)
+    on_second(3)
+    pl.when(at_end)(lambda: steps(chain_a, 2))
+    split(wg_kv, v_keep, v_give, 2 * HW)
+    v_move = begin(v_give, v_in, v_send.at[0], v_recv.at[0], core=sib)
+    for copy in copies:
+        copy.wait()
+    arrived(big_ref.at[core, r, g, pl.ds(up_rows, 48)], u_send.at[0], u_recv.at[0], x)
+    ring_b.start()
+    spread_b(g, 0)
     v_move.wait_recv()
     v_pass[...] = (v_keep[other] + v_in[other].astype(f32)).astype(bf16)
     v_across = begin(v_pass, v_x, v_send.at[1], v_recv.at[1], x=other)
-    chain_b.step(farthest(g, 0))
-    chain_b.step(farthest(g, 1))
+    pl.when(between)(lambda: steps(chain_a, 0))
+    settled(q_over)
+    q_sum[...] = (q_sum[...].astype(f32) + q_y[...].astype(f32)).astype(bf16)
+    store(q_sum, q_slot(g), l_sem.at[0])
+    ring_q.start()
+    begin(q_slot(g), q_slot(g), qs_send.at[0], qs_recv.at[0], core=sib)
+    v_across.wait_recv()
+    v_sum[...] = (v_keep[x] + v_in[x].astype(f32) + v_x[...].astype(f32)).astype(bf16)
+    v_over = begin(v_sum, v_y, v_send.at[2], v_recv.at[2], r=far_r)
+    spread_far(g, 0)
+    pl.when(between)(lambda: steps(chain_a, 1, 2))
+    settled(v_over)
+    v_sum[...] = (v_sum[...].astype(f32) + v_y[...].astype(f32)).astype(bf16)
+    store(v_sum, v_slot(g), l_sem.at[0])
+    ring_v.start()
+    begin(v_slot(g), v_slot(g), vs_send.at[0], vs_recv.at[0], core=sib)
+    spread_b(ring_b.step(1), 1)
+    z = ring_q.step(1)
+    begin(q_slot(z), q_slot(z), qs_send.at[1], qs_recv.at[1], core=sib)
+    z = ring_v.step(1)
+    begin(v_slot(z), v_slot(z), vs_send.at[1], vs_recv.at[1], core=sib)
     chain_a.step(g)
 
     grad_first = total_a[...]
@@ -1090,93 +1213,32 @@
     sums_ref[1:2] = jnp.sum(grad_first, axis=0, keepdims=True)
     s_sib = begin(sums_ref, sums_got.at[0], s_send.at[0], s_recv.at[0], core=sib)
 
-    def q_slot(z):
-        return qout_ref.at[core, z]
-
-    def v_slot(z):
-        return kvout_ref.at[core, z]
-
-    def b_slot(z):
-        return big_ref.at[core, r, z]
-
-    ring_q = Ring(g, x, q_slot, rq_own, rq_send, rq_recv)
-    ring_v = Ring(g, x, v_slot, rv_own, rv_send, rv_recv)
-    ring_b = Ring(g, x, b_slot, rb_own, rb_send, rb_recv)
-
-    def store(value_ref, slot, sem):
-        copy = pltpu.make_async_copy(value_ref, slot, sem)
-        copy.start()
-        copy.wait()
-
-    settled(q_over)
-    q_sum[...] = (q_sum[...].astype(f32) + q_y[...].astype(f32)).astype(bf16)
-    store(q_sum, q_slot(g), l_sem.at[0])
-    ring_q.start()
-    begin(q_slot(g), q_slot(g), qs_send.at[0], qs_recv.at[0], core=sib)
-
-    chain_b.step(farthest(g, 2))
-    v_across.wait_recv()
-    v_sum[...] = (v_keep[x] + v_in[x].astype(f32) + v_x[...].astype(f32)).astype(bf16)
-    v_over = begin(v_sum, v_y, v_send.at[2], v_recv.at[2], r=far_r)
-    chain_b.step(g)
-    unit[...] = total_b[...].astype(bf16)
-    up_rows = 96 + 48 * other
-    u_move = begin(
-        unit.at[pl.ds(up_rows, 48)], big_ref.at[core, r, g, pl.ds(96 + 48 * x, 48)], u_send.at[0], u_recv.at[0], x=other
-    )
-    copies = [
-        pltpu.make_async_copy(unit.at[pl.ds(0, 96)], big_ref.at[core, r, g, pl.ds(0, 96)], l_sem.at[1]),
-        pltpu.make_async_copy(
-            unit.at[pl.ds(96 + 48 * x, 48)], big_ref.at[core, r, g, pl.ds(96 + 48 * x, 48)], l_sem.at[2]
-        ),
-        pltpu.make_async_copy(unit.at[pl.ds(192, 24)], big_ref.at[core, r, g, pl.ds(192, 24)], l_sem.at[3]),
-    ]
-    for copy in copies:
-        copy.start()
     settled(s_sib)
     sums_ref[...] += sums_got[0]
     s_x = begin(sums_ref, sums_got.at[1], s_send.at[1], s_recv.at[1], x=other)
-    for copy in copies:
-        copy.wait()
-    there = big_ref.at[core, r, g, pl.ds(up_rows, 48)]
-    arrived(there, u_send.at[0], u_recv.at[0], x)
-    ring_b.start()
-
-    def spread_b(z, step):
-        begin(b_slot(z), b_slot(z), fy_send.at[step], fy_recv.at[step], r=far_r)
-        begin(b_slot(z), b_slot(z), fs_send.at[0, step], fs_recv.at[0, step], core=sib)
-
-    def spread_far(z, step):
-        what = big_ref.at[core, far_r, z]
-        arrived(what, fy_send.at[step], fy_recv.at[step], x)
-        begin(what, what, fs_send.at[1, step], fs_recv.at[1, step], core=sib)
-
-    spread_b(g, 0)
-    settled(v_over)
-    v_sum[...] = (v_sum[...].astype(f32) + v_y[...].astype(f32)).astype(bf16)
-    store(v_sum, v_slot(g), l_sem.at[0])
-    ring_v.start()
-    begin(v_slot(g), v_slot(g), vs_send.at[0], vs_recv.at[0], core=sib)
+    spread_b(ring_b.step(2), 2)
+    spread_far(nearest(g, 1), 1)
     settled(s_x)
     sums_ref[...] += sums_got[1]
     s_y = begin(sums_ref, sums_got.at[2], s_send.at[2], s_recv.at[2], r=far_r)
-    for step in range(1, GROUPS):
-        z = ring_q.step(step)
-        begin(q_slot(z), q_slot(z), qs_send.at[step], qs_recv.at[step], core=sib)
-        if step == 1:
-            settled(s_y)
-            sums_ref[...] += sums_got[2]
-            for away in range(1, GROUPS):
-                begin(
-                    sums_ref, sums_got.at[2 + away], s_send.at[2 + away], s_recv.at[2 + away],
-                    g=lax.rem(g + away, GROUPS),
-                )
-        z = ring_b.step(step)
-        spread_b(z, step)
-        spread_far(nearest(g, step - 1), step - 1)
-        z = ring_v.step(step)
-        begin(v_slot(z), v_slot(z), vs_send.at[step], vs_recv.at[step], core=sib)
-    spread_far(nearest(g, GROUPS - 1), GROUPS - 1)
+    z = ring_q.step(2)
+    begin(q_slot(z), q_slot(z), qs_send.at[2], qs_recv.at[2], core=sib)
+    z = ring_v.step(2)
+    begin(v_slot(z), v_slot(z), vs_send.at[2], vs_recv.at[2], core=sib)
+    settled(s_y)
+    sums_ref[...] += sums_got[2]
+    for away in range(1, GROUPS):
+        begin(
+            sums_ref, sums_got.at[2 + away], s_send.at[2 + away], s_recv.at[2 + away],
+            g=lax.rem(g + away, GROUPS),
+        )
+    spread_b(ring_b.step(3), 3)
+    spread_far(nearest(g, 2), 2)
+    z = ring_q.step(3)
+    begin(q_slot(z), q_slot(z), qs_send.at[3], qs_recv.at[3], core=sib)
+    z = ring_v.step(3)
+    begin(v_slot(z), v_slot(z), vs_send.at[3], vs_recv.at[3], core=sib)
+    spread_far(nearest(g, 3), 3)
 
     for away in range(1, GROUPS):
         arrived(sums_got.at[2 + away], s_send.at[2 + away], s_recv.at[2 + away], x)
@@ -1193,7 +1255,7 @@
     sums_ref[...] += sums_got[3] + sums_got[4] + sums_got[5]
 
 
-def scatter(dkv, dq, normed, wfull, tokens, mgrad, small, bundle, sums):
+def scatter(dkv, dq, normed, wfull, tokens, mgrad, small, bundle, over, sums):
     rows, width = tokens.shape
     fourth = width // 4
     dma = pltpu.SemaphoreType.DMA
@@ -1219,7 +1281,7 @@
             jax.ShapeDtypeStruct((2, GROUPS, fourth, wide_v), bf16),
             jax.ShapeDtypeStruct((24, width), f32),
         ),
-        in_specs=[anywhere()] + [whole_vmem()] * 8,
+        in_specs=[in_hbm()] + [whole_vmem()] * 9,
         out_specs=(whole_vmem(), anywhere(), anywhere(), anywhere(), whole_vmem()),
         scratch_shapes=[
             pltpu.VMEM((GROUPS, 4, *kv_block), bf16),
@@ -1234,7 +1296,6 @@
             pltpu.VMEM((2, GROUPS, *full), bf16),
             pltpu.VMEM((GROUPS, *full), bf16),
             pltpu.VMEM((width, wide_v), f32),
-            pltpu.VMEM((GROUPS, *unit), bf16),
             pltpu.VMEM((GROUPS, *unit), f32),
             pltpu.VMEM(unit, f32),
             pltpu.VMEM((2, GROUPS, *unit), bf16),
@@ -1245,7 +1306,7 @@
             pltpu.VMEM((6, 24, width), f32),
             dma((GROUPS, 4)), dma((GROUPS, 4)), dma((GROUPS, 4)), dma((GROUPS,)), dma((GROUPS,)), dma((GROUPS,)), dma((GROUPS,)),
             dma((GROUPS,)), dma((2, GROUPS)),
-            dma((GROUPS,)), dma((GROUPS,)), dma((GROUPS,)), dma((2, GROUPS)), dma((1,)), dma((1,)), dma((2,)), dma((GROUPS,)), dma((GROUPS,)),
+            dma((GROUPS,)), dma((2, GROUPS)), dma((1,)), dma((1,)), dma((2,)), dma((GROUPS,)), dma((GROUPS,)),
             dma((GROUPS,)), dma((GROUPS,)), dma((2, GROUPS)), dma((2, GROUPS)),
             dma((3,)), dma((3,)), dma((2,)), dma((GROUPS,)), dma((GROUPS,)), dma((GROUPS,)), dma((GROUPS,)),
             dma((3,)), dma((3,)), dma((2,)), dma((GROUPS,)), dma((GROUPS,)), dma((GROUPS,)), dma((GROUPS,)),
@@ -1255,7 +1316,7 @@
             collective_id=2, has_side_effects=True, vmem_limit_bytes=51 << 20
         ),
         name="scatter",
-    )(dkv, dq, normed, wfull, tokens, mgrad, small, bundle, sums)
+    )(dkv, dq, normed, wfull, tokens, mgrad, small, bundle, over, sums)
 
 
 def pack_kv(key_part, value_part):
@@ -1293,18 +1354,20 @@
     def _():
         def own_half(row):
             whole = sums_ref[row : row + 1]
-            return jnp.where(x == 0, whole[:, :half], whole[:, half:])
+            return jnp.where(x == 0, whole[:, :half], whole[:, half:]).reshape(half)
 
         for ref, row in (
             (low_gain, 0), (low_shift, 1), (out_bias, 2), (high_gain, 3), (high_shift, 4), (down_bias, 5),
         ):
             ref[...] = own_half(row)
         pair = [sums_ref[pl.ds(16 + 2 * x + i, 1)] for i in range(2)]
-        query_bias[...] = jnp.concatenate([item[:, :HW] for item in pair], axis=1)
+        query_bias[...] = jnp.concatenate([item[:, :HW] for item in pair], axis=1).reshape(half)
         value_bias[...] = jnp.concatenate(
             [unpack_kv(item[:, 2 * BLK : 2 * BLK + 2 * HW])[1] for item in pair], axis=1
-        )
-        up_bias[...] = jnp.concatenate([sums_ref[pl.ds(8 + 2 * x + i, 1)] for i in range(2)], axis=1)
+        ).reshape(half)
+        up_bias[...] = jnp.concatenate(
+            [sums_ref[pl.ds(8 + 2 * x + i, 1)] for i in range(2)], axis=1
+        ).reshape(2 * width)
 
 
 def lay_out(big, query, kv, sums):
@@ -1316,10 +1379,10 @@
         return pl.BlockSpec(shape, index)
 
     def fixed(wide):
-        return pl.BlockSpec((1, wide), lambda p: (0, 0))
+        return pl.BlockSpec((wide,), lambda p: (0,))
 
     narrow = spec((2, rows, width), lambda p: (0, p, 0))
-    vector = jax.ShapeDtypeStruct((1, half), f32)
+    vector = jax.ShapeDtypeStruct((half,), f32)
     return pl.pallas_call(
         layout_kernel,
         grid=(PARTS,),
@@ -1328,7 +1391,7 @@
             jax.ShapeDtypeStruct((2, width, width), f32),
             *[jax.ShapeDtypeStruct((2, fourth, width), f32)] * 4,
             *[vector] * 7,
-            jax.ShapeDtypeStruct((1, 2 * width), f32),
+            jax.ShapeDtypeStruct((2 * width,), f32),
             vector,
         ),
         in_specs=[
@@ -1346,7 +1409,7 @@
             fixed(half),
         ),
         compiler_params=pltpu.CompilerParams(
-            vmem_limit_bytes=12 << 20, dimension_semantics=("arbitrary",)
+            vmem_limit_bytes=VMEM_LIMIT, dimension_semantics=("arbitrary",)
         ),
         name="lay_out",
     )(big, query, kv, sums)
@@ -1364,13 +1427,9 @@
     rows, width = tokens.shape
     half = width // 2
     blocks = deal.shape[0]
-    lines = jnp.concatenate(
-        [
-            first_gain, first_shift, output_bias, second_gain, second_shift, down_bias, query_bias, value_bias, up_bias,
-        ]
-    ).reshape(-1, half)
     kv, q, normed, small, wfull, up, wo = gather(
-        tokens, query_weight, key_weight, value_weight, lines, up_weight, output_weight
+        tokens, query_weight, key_weight, value_weight, up_weight, output_weight,
+        first_gain, first_shift, output_bias, second_gain, second_shift, down_bias, query_bias, value_bias, up_bias,
     )
     wide = blocks > 8 * 2 * GROUPS
     if wide:
@@ -1378,16 +1437,17 @@
     kv = kv.reshape(blocks, BLK, 2 * HW)
     q = q.reshape(2 * GROUPS, BLK, 2 * BLK)
     out_t, kept, lse = attend_forward(deal, doc_lengths, q, kv)
-    result, grad_middle, grad_t, bundle, sums = dense(
+    result, grad_middle, grad_t, bundle, over, sums = dense(
         out_t, tokens, cotangent, small, up, wo, down_weight
     )
+    over = lax.ppermute(over, "r", ((0, 1), (1, 0)))
     dq, dkv = attend_backward(deal, doc_lengths, q, kv, lse, grad_t, kept)
     dkv = dkv.reshape(-1, GROUPS, rows, 2 * HW)
     if wide:
         dkv = lax.psum_scatter(dkv, "s", scatter_dimension=0, tiled=True)
     dq = dq.reshape(GROUPS, rows, 2 * BLK)
     grad_tokens, big, query_own, kv_own, sums = scatter(
-        dkv, dq, normed, wfull, tokens, grad_middle, small, bundle, sums
+        dkv, dq, normed, wfull, tokens, grad_middle, small, bundle, over, sums
     )
     if wide:
         big, query_own, kv_own, sums = (
@@ -1402,27 +1462,24 @@
     def flat(item):
         return item.reshape(-1, width)
 
-    def line(item):
-        return item.reshape(-1)
-
     return (
         result,
         grad_tokens,
-        line(low_gain),
-        line(low_shift),
+        low_gain,
+        low_shift,
         flat(query_own),
-        line(query_sum),
+        query_sum,
         flat(key_own),
         flat(value_own),
-        line(value_sum),
+        value_sum,
         flat(wo_own),
-        line(out_sum),
-        line(high_gain),
-        line(high_shift),
+        out_sum,
+        high_gain,
+        high_shift,
         up_own,
-        line(up_sum),
+        up_sum,
         flat(down_own),
-        line(down_sum),
+        down_sum,
     )
 
 

time: 361 us -> 315 us (0.87)
  Pallas kernels: 333 us -> 303 us
  local copies, waits for them, and re-layouts: 22.6 us -> 9.99 us
  other arithmetic: 5.38 us -> 0 us
  starting transfers between devices: 0 us -> 4.66 us
    pallas_call x1, Pallas kernels: 147 us -> 121 us  [scatter(): pl.pallas_call(scatter_kernel, out_shape=(jax.ShapeDtypeStruct(full, f32)...]
    unnamed x46 -> x34, local copies, waits for them, and re-layouts: 21.9 us -> 9.99 us
    pallas_call x1, Pallas kernels: 28.3 us -> 16.7 us  [attend_forward(): pl.pallas_call(forward_kernel, out_shape=(jax.ShapeDtypeStruct((slots, HW...]
    pallas_call x1, Pallas kernels: 52.5 us -> 61.3 us  [dense(): pl.pallas_call(dense_kernel, out_shape=(jax.ShapeDtypeStruct(full, bf16),...]
    pallas_call x1, Pallas kernels: 35.1 us -> 28 us  [attend_backward(): pl.pallas_call(backward_kernel, out_shape=(jax.ShapeDtypeStruct((slots, B...]
    pallas_call x9 -> x0, other arithmetic: 5.38 us -> none  [lay_out(): pl.pallas_call(layout_kernel, grid=(PARTS,), out_shape=(jax.ShapeDtypeStr...]
    ppermute x0 -> x1, starting transfers between devices: none -> 4.66 us  [shards(): over = lax.ppermute(over, 'r', ((0, 1), (1, 0)))]
  transfers between devices with their start and end apart: 0 -> 1, of which waited for: 0 -> 1; matrix products, arithmetic and copies ran while one was open for 0% -> 0% of each run, Pallas kernels for 0% -> 9%
where the time goes in v1:
time: 315 us; the launch traced here: 318 us
  Pallas kernels  303 us (96%)
  local copies, waits for them, and re-layouts  9.99 us (3%)
  starting transfers between devices  4.66 us (1%)
    pallas_call x1, Pallas kernels, scatter(): pl.pallas_call(scatter_kernel, out_shape=(jax.ShapeDtypeStruct(full, f32)...  121 us
    pallas_call x1, Pallas kernels, gather(): pl.pallas_call(gather_kernel, out_shape=(jax.ShapeDtypeStruct((8, GROUPS,...  65.6 us
    pallas_call x1, Pallas kernels, dense(): pl.pallas_call(dense_kernel, out_shape=(jax.ShapeDtypeStruct(full, bf16),...  61.3 us
    pallas_call x1, Pallas kernels, attend_backward(): pl.pallas_call(backward_kernel, out_shape=(jax.ShapeDtypeStruct((slots, B...  28 us
    pallas_call x1, Pallas kernels, attend_forward(): pl.pallas_call(forward_kernel, out_shape=(jax.ShapeDtypeStruct((slots, HW...  16.7 us
    unnamed x34, local copies, waits for them, and re-layouts  9.99 us
    pallas_call x1, Pallas kernels, lay_out(): pl.pallas_call(layout_kernel, grid=(PARTS,), out_shape=(jax.ShapeDtypeStr...  9.88 us
  transfers between devices with their start and end apart: 1, of which 1 were waited for; matrix products, arithmetic and copies ran while one was open for 0% of the time, Pallas kernels for 9%

profile of v1, /device:TPU:0, one launch (start us, length us, event | category | flops | bytes accessed | tf_op | source)
XLA Modules:
  0.0 318.3 jit_solution(13451772069990005708)
XLA Ops:
  0.7 0.0 copy-start.13
  0.7 0.0 copy-start.14
  0.7 65.6 %gather.1 = (bf16[8,4,256,384]{3,2,1,0:T(8,128)(2,1)}, bf16[4,256,256]{2,1,0:T(8,128)(2,1)}, bf16[4,256,768]{2,1,0:T(8,128)(2,1)}, f32[16,768]{1,0:T(8,128)}, bf...) custom-call(bf16[256,768]{1,0:T(8,128)(2,1)} %tokens_ref.5, ...), custom_call_target="tpu_custom_call" | custom-call | tf_op jit(solution)/shard_map/gather/pallas_call | solution.py:598
  66.3 0.0 copy-done.13
  66.4 2.8 copy-done
  69.1 1.0 copy-done.3
  70.2 0.0 copy-start.10
  70.2 16.7 %attend_forward.1 = (bf16[8,192,128]{2,1,0:T(8,128)(2,1)S(1)}, f32[8,192,128]{2,1,0:T(8,128)S(1)}, f32[8,1,384]{2,1,0:T(1,128)S(1)}) custom-call(s32[64]{0:T(128)S(1)} %copy-done.13, s32[4]{0:T(128)S(1)} %copy-done.14, bf16[8,128,256]{2,1,0:T(8,128)(2,1)S(1)} %bitcast.12, bf16[64,128,384]{2,1,0:T(8,128)(2,1)S(1)} %bitcast.11), custom_call_target="tpu_custom_call" | custom-call | tf_op jit(solution)/shard_map/attend_forward/pallas_call | solution.py:182
  87.0 61.3 %dense.1 = (bf16[256,768]{1,0:T(8,128)(2,1)S(1)}, f32[256,768]{1,0:T(8,128)S(1)}, bf16[8,192,128]{2,1,0:T(8,128)(2,1)S(1)}, bf16[4,216,768]{2,1,0:T(8,128)(2,1)S...) custom-call(bf16[8,192,128]{2,1,0:T(8,128)(2,1)S(1)} %get-tuple-element.57.out_t_ref, ...), custom_call_target="tpu_custom_call" | custom-call | tf_op jit(solution)/shard_map/dense/pallas_call | solution.py:847
  148.4 0.0 copy-start.5
  148.4 1.1 copy-done.5
  149.4 0.9 copy-done.8
  150.3 4.7 %collective-permute-start = (bf16[4,216,768]{2,1,0:T(8,128)(2,1)S(1)}, bf16[4,216,768]{2,1,0:T(8,128)(2,1)S(1)}, u32[]{:S(2)}, u32[]{:S(2)}) collective-permute-start(bf16[4,216,768]{2,1,0:T(8,128)(2,1)S(1)} %get-tuple-element.71), channel_id=1, source_target_pairs={{0,4},{4,0},{1,5},{5,1},{2,6},{6,2},{3,7},{7,3},{8,12},{12,8},{9,1... | collective-permute-start | bytes 3981320 | tf_op jit(solution)/shard_map/ppermute | solution.py:1443
  155.0 0.0 copy-done.4
  155.0 28.0 %attend_backward.1 = (bf16[8,128,256]{2,1,0:T(8,128)(2,1)S(1)}, bf16[64,128,384]{2,1,0:T(8,128)(2,1)}) custom-call(s32[64]{0:T(128)S(1)} %copy-done.13, s32[4]{0:T(128)S(1)} %copy-done.14, bf16[8,128,256]{2,1,0:T(8,128)(2,1)S(1)} %bitcast.13, bf16[64,128,384]{2,1,0:T(8,128)(2,1)} %bitcast.10, f32[8,1,384]{2,1,0:T(1,128)S(1)} %get-tuple-element.62.lse_ref, ...), custom_call_target="tpu_custom_call" | custom-call | tf_op jit(solution)/shard_map/attend_backward/pallas_call | solution.py:309
  182.9 0.2 collective-permute-done.by_in
  183.2 1.1 copy-done.15
  184.2 121.0 %scatter.1 = (f32[256,768]{1,0:T(8,128)S(1)}, bf16[2,2,4,216,768]{4,3,2,1,0:T(8,128)(2,1)}, bf16[2,4,192,256]{3,2,1,0:T(8,128)(2,1)S(1)}, bf16[2,4,192,384]{3,2,1,0:T(8,128)(2,1)}, f32[24,768]{1,0:T(8,128)S(1)}) custom-call(bf16[8,4,256,384]{3,2,1,0:T(8,128)(2,1)} %bitcast.15, bf16[4,256,256]{2,1,0:T(8,128)(2,1)S(1)} %bitcast.14, ...), custom_call_target="tpu_custom_call" | custom-call | tf_op jit(solution)/shard_map/scatter/pallas_call | solution.py:1275
  305.3 0.0 copy-start.9
  305.3 0.9 copy-done.9
  306.1 0.6 copy-done.12
  306.8 9.9 %lay_out.1 = (f32[384,3072]{1,0:T(8,128)}, f32[2,768,768]{2,1,0:T(8,128)}, f32[2,192,768]{2,1,0:T(8,128)}, f32[2,192,768]{2,1,0:T(8,128)}, f32[2,192,768]{2,1,0:...) custom-call(bf16[2,8,216,768]{3,2,1,0:T(8,128)(2,1)} %bitcast.16, ...), custom_call_target="tpu_custom_call" | custom-call | tf_op jit(solution)/shard_map/lay_out/pallas_call | solution.py:1386
  316.7 0.7 copy.38
  317.4 0.9 copy.39
  (18 shorter events, 0.0 us)
Async XLA Ops:
  0.7 65.7 %copy-start.13 = (s32[64]{0:T(128)S(1)}, s32[64]{0:T(128)}, u32[]{:S(2)}) copy-start(s32[64]{0:T(128)} %deal_ref.3) | copy-start | bytes 772
  0.7 65.7 %copy-start.14 = (s32[4]{0:T(128)S(1)}, s32[4]{0:T(128)}, u32[]{:S(2)}) copy-start(s32[4]{0:T(128)} %lengths_ref.3) | copy-start | bytes 52
  66.4 2.8 copy-start
  69.1 1.0 copy-start.3
  70.2 16.8 %copy-start.1 = (bf16[256,768]{1,0:T(8,128)(2,1)S(1)}, bf16[256,768]{1,0:T(8,128)(2,1)}, u32[]{:S(2)}) copy-start(bf16[256,768]{1,0:T(8,128)(2,1)} %tokens_ref.5) | copy-start | bytes 1179652
  70.2 16.8 %copy-start.2 = (bf16[1536,768]{1,0:T(8,128)(2,1)S(1)}, bf16[1536,768]{1,0:T(8,128)(2,1)}, u32[]{:S(2)}) copy-start(bf16[1536,768]{1,0:T(8,128)(2,1)} %down_any.1) | copy-start | bytes 7077892
  70.2 16.8 %copy-start.6 = (bf16[768,768]{1,0:T(8,128)(2,1)S(1)}, bf16[768,768]{1,0:T(8,128)(2,1)}, u32[]{:S(2)}) copy-start(bf16[768,768]{1,0:T(8,128)(2,1)} %get-tuple-element.59.up_ref) | copy-start | bytes 3538948
  70.2 16.8 %copy-start.7 = (bf16[768,768]{1,0:T(8,128)(2,1)S(1)}, bf16[768,768]{1,0:T(8,128)(2,1)}, u32[]{:S(2)}) copy-start(bf16[768,768]{1,0:T(8,128)(2,1)} %get-tuple-element.60.wo_ref) | copy-start | bytes 3538948
  70.2 16.8 %copy-start.10 = (bf16[256,768]{1,0:T(8,128)(2,1)S(1)}, bf16[256,768]{1,0:T(8,128)(2,1)}, u32[]{:S(2)}) copy-start(bf16[256,768]{1,0:T(8,128)(2,1)} %cot_ref.1) | copy-start | bytes 1179652
  70.2 16.8 %copy-start.11 = (f32[16,768]{1,0:T(8,128)S(1)}, f32[16,768]{1,0:T(8,128)}, u32[]{:S(2)}) copy-start(f32[16,768]{1,0:T(8,128)} %get-tuple-element.58.small_ref) | copy-start | bytes 147460
  87.0 68.0 %copy-start.4 = (bf16[4,256,256]{2,1,0:T(8,128)(2,1)S(1)}, bf16[4,256,256]{2,1,0:T(8,128)(2,1)}, u32[]{:S(2)}) copy-start(bf16[4,256,256]{2,1,0:T(8,128)(2,1)} %get-tuple-element.55) | copy-start | bytes 1572868
  148.4 1.1 copy-start.5
  149.4 0.9 copy-start.8
  150.3 32.8 %collective-permute-start = (bf16[4,216,768]{2,1,0:T(8,128)(2,1)S(1)}, bf16[4,216,768]{2,1,0:T(8,128)(2,1)S(1)}, u32[]{:S(2)}, u32[]{:S(2)}) collective-permute-start(bf16[4,216,768]{2,1,0:T(8,128)(2,1)S(1)} %get-tuple-element.71), channel_id=1, source_target_pairs={{0,4},{4,0},{1,5},{5,1},{2,6},{6,2},{3,7},{7,3},{8,12},{12,8},{9,1... | collective-permute-start | bytes 3981320 | tf_op jit(solution)/shard_map/ppermute | solution.py:1443
  183.1 1.1 copy-start.15
  305.3 0.9 copy-start.9
  306.1 0.6 copy-start.12

commit v2 on v1

--- a/solution.py
+++ b/solution.py
@@ -419,8 +419,8 @@
 
 
 def gather_kernel(
-    tokens_ref, query_any, key_any, value_any, up_ref, wo_ref, l0, l1, l2, l3, l4, l5, l6, l7, l8,
-    kv_ref, q_ref, normed_ref, small_out, wfull, up_out, wo_out,
+    tokens_ref, query_any, key_any, value_any, wo_ref, l0, l1, l2, l3, l4, l5, l6, l7, l8,
+    kv_ref, q_ref, normed_ref, small_out, wfull, wo_out,
     lined, attn_w, narrow_ref, small_ref, small_in, kvs,
     z_own, z_send, z_recv, s_sem, n_send, n_recv, kv_send, kv_recv, kv_local, w_send, w_recv, w_local, a_sem,
 ):
@@ -456,27 +456,14 @@
     def wo_rows(owner, part):
         return wo_out.at[pl.ds(owner * half + core * fourth + part * eighth, eighth)]
 
-    def up_rows(owner, part):
-        return up_out.at[pl.ds(owner * half + part * fourth, fourth)]
-
-    def up_columns(owner):
-        return pl.ds(pl.multiple_of((2 * owner + core) * width, width), width)
-
     wo_x = send(wo_ref.at[pl.ds(core * fourth + r * eighth, eighth)], wo_rows(x, r), w_send.at[0], w_recv.at[0], x=other)
-    up_x = send(
-        up_ref.at[pl.ds(r * fourth, fourth), up_columns(other)], up_rows(x, r), w_send.at[1], w_recv.at[1], x=other
-    )
     wo_y = send(wo_rows(other, r), wo_rows(other, r), w_send.at[3], w_recv.at[3], r=1 - r)
-    up_y = send(up_rows(other, r), up_rows(other, r), w_send.at[4], w_recv.at[4], r=1 - r)
     wo_s = [
         send(wo_rows(other, part), wo_rows(other, part), w_send.at[6 + i], w_recv.at[6 + i], core=1 - core)
         for i, part in enumerate((r, 1 - r))
     ]
     wo_x.start()
-    locals_ = [
-        pltpu.make_async_copy(wo_ref, wo_out.at[pl.ds(x * half, half)], w_local.at[0]),
-        pltpu.make_async_copy(up_ref.at[:, up_columns(x)], up_out.at[pl.ds(x * half, half)], w_local.at[1]),
-    ]
+    locals_ = [pltpu.make_async_copy(wo_ref, wo_out.at[pl.ds(x * half, half)], w_local.at[0])]
     for item in locals_:
         item.start()
 
@@ -537,8 +524,6 @@
         push(step, 1, here, r=1 - r)
         push(step, 2, here, core=1 - core)
         pltpu.make_async_copy(kvs.at[step], block(own, source), kv_local.at[step]).start()
-        if step == 0:
-            up_x.start()
         if step > 0:
             forward(step - 1)
         if step > 1:
@@ -548,8 +533,6 @@
     wo_s[0].start()
     forward(GROUPS - 1)
     forward_far(GROUPS - 2)
-    up_x.wait_recv()
-    up_y.start()
     send(wo_rows(other, 1 - r), wo_rows(other, 1 - r), w_send.at[3], w_recv.at[3], r=1 - r).wait_recv()
     wo_s[1].start()
     forward_far(GROUPS - 1)
@@ -574,9 +557,8 @@
     narrow_s.wait_send()
     for item in locals_:
         item.wait()
-    for item in (wo_x, up_x, wo_y, up_y, *wo_s):
+    for item in (wo_x, wo_y, *wo_s):
         item.wait_send()
-    send(up_rows(other, 1 - r), up_rows(other, 1 - r), w_send.at[4], w_recv.at[4], r=1 - r).wait_recv()
     for i, part in enumerate((r, 1 - r)):
         there = wo_out.at[pl.ds(other * half + (1 - core) * fourth + part * eighth, eighth)]
         send(there, there, w_send.at[6 + i], w_recv.at[6 + i], core=1 - core).wait_recv()
@@ -590,7 +572,7 @@
     return pl.BlockSpec(memory_space=pltpu.HBM)
 
 
-def gather(tokens, query, key, value, up, wo, *lines):
+def gather(tokens, query, key, value, wo, *lines):
     rows, width = tokens.shape
     wide = 2 * BLK + 2 * HW
     small = (16, width)
@@ -604,10 +586,9 @@
             jax.ShapeDtypeStruct(small, f32),
             jax.ShapeDtypeStruct((width, wide), bf16),
             jax.ShapeDtypeStruct((width, width), bf16),
-            jax.ShapeDtypeStruct((width, width), bf16),
         ),
-        in_specs=[whole_vmem(), *[in_hbm()] * 5, *[whole_vmem()] * len(lines)],
-        out_specs=(anywhere(), *(whole_vmem(),) * 4, anywhere(), anywhere()),
+        in_specs=[whole_vmem(), *[in_hbm()] * 4, *[whole_vmem()] * len(lines)],
+        out_specs=(anywhere(), *(whole_vmem(),) * 5),
         scratch_shapes=[
             pltpu.VMEM((GROUPS, rows, width), bf16),
             pltpu.VMEM((3, width // 2, width), bf16),
@@ -622,7 +603,7 @@
             collective_id=0, has_side_effects=True, vmem_limit_bytes=60 << 20
         ),
         name="gather",
-    )(tokens, query, key, value, up, wo, *lines)
+    )(tokens, query, key, value, wo, *lines)
 
 
 def erf_parts(values):
@@ -635,168 +616,197 @@
 
 
 def dense_kernel(
-    out_t_ref, tokens_ref, cot_ref, small_ref, up_ref, wo_ref, down_any,
-    result_ref, middle_grad_ref, grad_t_ref, keep_ref, give_ref, sums_ref,
-    down_ref, attn_in, attn_t, cots, h2s, mid_ref, n2_ref, part_y, part_d, in_y, in_d, pass_y, pass_d, x_y, x_d,
-    hids, dus, grad_out, wo_keep, wo_give, wo_in, wo_pass, wo_x,
-    down_sem, a_send, a_recv, c_send, c_recv, h_send, h_recv, y_send, y_recv, d_send, d_recv, o_send, o_recv,
+    out_t_ref, tokens_ref, cot_ref, cot_x_ref, small_ref, wo_ref, up_mine, up_other, down_any,
+    base_ref, y_give_ref, middle_grad_ref, grad_t_ref, keep_ref, give_ref, sums_ref,
+    down_ref, up_ref, attn_in, attn_t, cots, h2s, mid_ref, n2_ref, scales, part_y, part_d, in_y, in_d, pass_y, pass_d,
+    x_y, x_d, hids, dus, branch_ref, grad_out, wo_keep, wo_give, wo_in, wo_pass, wo_x,
+    l_sem, a_send, a_recv, c_send, c_recv, h_send, h_recv, y_send, y_recv, d_send, d_recv, o_send, o_recv,
     w_send, w_recv,
 ):
     g, r, core, x = place()
-    other = 1 - x
+    other, sib = 1 - x, 1 - core
     rows, width = tokens_ref.shape
     half = width // 2
     fourth = half // 2
-    load = pltpu.make_async_copy(
-        down_any.at[pl.ds(pl.multiple_of(core * width, width), width)], down_ref, down_sem
-    )
-    load.start()
+    loads = [
+        pltpu.make_async_copy(
+            down_any.at[pl.ds(pl.multiple_of(core * width, width), width)], down_ref, l_sem.at[0]
+        ),
+        pltpu.make_async_copy(up_mine, up_ref.at[pl.ds(x * half, half)], l_sem.at[1]),
+        pltpu.make_async_copy(up_other, up_ref.at[pl.ds(other * half, half)], l_sem.at[2]),
+    ]
+    for load in loads:
+        load.start()
     greet(g, r, core, x, True)
-    cots[0] = cot_ref[...]
-
-    def share(rows_ref, out_sem, in_sem):
-        moves = (
-            send(rows_ref.at[0], rows_ref.at[2], out_sem.at[1], in_sem.at[1], x=other),
-            send(rows_ref.at[0], rows_ref.at[1], out_sem.at[0], in_sem.at[0], core=1 - core),
-        )
-        for move in moves:
-            move.start()
-        return moves
-
-    def pass_on(rows_ref, moves, out_sem, in_sem):
-        moves[0].wait_recv()
-        move = send(rows_ref.at[2], rows_ref.at[3], out_sem.at[2], in_sem.at[2], core=1 - core)
+    pending = []
+
+    def begin(src, dst, out_sem, in_sem, **device):
+        move = send(src, dst, out_sem, in_sem, **device)
         move.start()
+        pending.append(move)
         return move
 
     def other_group(away):
         return lax.rem(g + away, GROUPS)
 
-    attn_moves = []
-    for away in range(1, GROUPS):
-        to = other_group(away)
-        attn_moves.append(
-            send(out_t_ref.at[pl.ds(2 * to, 2)], attn_in.at[g], a_send.at[away], a_recv.at[g], g=to)
-        )
-        attn_moves[-1].start()
-    cot_moves = share(cots, c_send, c_recv)
-    attn_in[g] = out_t_ref[pl.ds(2 * g, 2)]
+    def rows_of(b):
+        return pl.ds(BLK * b, BLK)
+
+    for b in range(2):
+        for away in range(1, GROUPS):
+            to = other_group(away)
+            begin(out_t_ref.at[2 * to + b], attn_in.at[g, b], a_send.at[b, away], a_recv.at[b, g], g=to)
+        attn_in[g, b] = out_t_ref[2 * g + b]
+        cots[b, 0] = cot_ref[rows_of(b)]
+        cots[b, 2] = cot_x_ref[rows_of(b)]
+    cot_moves = [
+        begin(cots.at[:, 2 * i], cots.at[:, 2 * i + 1], c_send.at[i], c_recv.at[i], core=sib) for i in range(2)
+    ]
     sums_ref[...] = jnp.zeros_like(sums_ref)
     sums_ref[5:6] = jnp.sum(cot_ref[...].astype(f32), axis=0, keepdims=True)
-    for away in range(1, GROUPS):
-        source = other_group(away)
-        send(attn_in.at[source], attn_in.at[source], a_send.at[away], a_recv.at[source], g=source).wait_recv()
-    for source in range(GROUPS):
-        attn_t[HW * source : HW * source + HW] = jnp.concatenate(
-            [attn_in[source, 0], attn_in[source, 1]], axis=1
+    h2_moves = []
+
+    def norm(b):
+        for away in range(1, GROUPS):
+            source = other_group(away)
+            arrived(attn_in.at[source, b], a_send.at[b, away], a_recv.at[b, source], x)
+        for source in range(GROUPS):
+            attn_t[HW * source : HW * source + HW, BLK * b : BLK * b + BLK] = attn_in[source, b]
+        middle = (
+            tokens_ref[rows_of(b)].astype(f32)
+            + outer(attn_t[:, BLK * b : BLK * b + BLK], wo_ref[...])
+            + small_ref[2:3]
         )
-    middle = tokens_ref[...].astype(f32) + outer(attn_t[...], wo_ref[...]) + small_ref[2:3]
-    mid_ref[...] = middle
-    mean = jnp.mean(middle, axis=-1, keepdims=True)
-    centred = middle - mean
-    spread = jnp.mean(centred * centred, axis=-1, keepdims=True)
-    scale = lax.rsqrt(spread + EPS)
-    n2_ref[...] = centred * scale
-    h2s[0] = (n2_ref[...] * small_ref[3:4] + small_ref[4:5]).astype(bf16)
-    h2_moves = share(h2s, h_send, h_recv)
-    cot_pass = pass_on(cots, cot_moves, c_send, c_recv)
-    load.wait()
+        mid_ref[b] = middle
+        mean = jnp.mean(middle, axis=-1, keepdims=True)
+        centred = middle - mean
+        scale = lax.rsqrt(jnp.mean(centred * centred, axis=-1, keepdims=True) + EPS)
+        scales[b] = scale
+        n2_ref[b] = centred * scale
+        h2s[b, 0] = (n2_ref[b] * small_ref[3:4] + small_ref[4:5]).astype(bf16)
+        h2_moves.append(
+            (
+                begin(h2s.at[b, 0], h2s.at[b, 2], h_send.at[b, 1], h_recv.at[b, 1], x=other),
+                begin(h2s.at[b, 0], h2s.at[b, 1], h_send.at[b, 0], h_recv.at[b, 0], core=sib),
+            )
+        )
+
+    def pass_on(b):
+        h2_moves[b][0].wait_recv()
+        return begin(h2s.at[b, 2], h2s.at[b, 3], h_send.at[b, 2], h_recv.at[b, 2], core=sib)
+
     bias_row = 8 + 2 * x + core
-    bias = small_ref[pl.ds(bias_row, 1)]
-    sums_ref[pl.ds(bias_row, 1)] = jnp.zeros((1, width), f32)
-
-    def one_part(part):
-        expanded = dot(h2s[part], up_ref[...]) + bias
+
+    def pair_of(ref, b, pair):
+        return ref[b, 2 * pair : 2 * pair + 2].reshape(2 * BLK, width)
+
+    def forward_backward(b, pair):
+        cot = pair_of(cots, b, pair)
+        expanded = dot(pair_of(h2s, b, pair), up_ref[...]) + small_ref[pl.ds(bias_row, 1)]
         below, density = erf_parts(expanded)
         hidden = (expanded * below).astype(bf16)
-        hids[part] = hidden
+        hids[b, pair] = hidden
         slope = below + expanded * density
-        grad_hidden = inner(cots[part], down_ref[...]).astype(bf16).astype(f32)
+        grad_hidden = inner(cot, down_ref[...]).astype(bf16).astype(f32)
         grad_expand = (grad_hidden * slope).astype(bf16)
-        dus[part] = grad_expand
-        part_d[part] = inner(grad_expand, up_ref[...])
-        part_y[part] = dot(hidden, down_ref[...])
+        dus[b, pair] = grad_expand
+        part_d[b, pair] = inner(grad_expand, up_ref[...])
+        part_y[b, pair] = dot(hidden, down_ref[...])
         sums_ref[pl.ds(bias_row, 1)] += jnp.sum(grad_expand.astype(f32), axis=0, keepdims=True)
 
-    one_part(0)
-    cot_moves[1].wait_recv()
-    h2_moves[1].wait_recv()
-    h2_pass = pass_on(h2s, h2_moves, h_send, h_recv)
-    one_part(1)
-    d_sib = send(part_d.at[1], in_d, d_send.at[0], d_recv.at[0], core=1 - core)
-    d_sib.start()
-    cot_pass.wait_recv()
-    h2_pass.wait_recv()
-    one_part(3)
-    x_d[0] = part_d[3].astype(bf16)
-    x_y[0] = part_y[3].astype(bf16)
-    d_pass = send(x_d.at[0], pass_d, d_send.at[1], d_recv.at[1], core=1 - core)
-    y_pass = send(x_y.at[0], pass_y, y_send.at[1], y_recv.at[1], core=1 - core)
-    d_pass.start()
-    y_pass.start()
-    one_part(2)
-    d_pass.wait_recv()
-    x_d[1] = (part_d[2] + pass_d[...].astype(f32)).astype(bf16)
-    d_x = send(x_d.at[1], x_d.at[2], d_send.at[2], d_recv.at[2], x=other)
-    d_x.start()
-    y_pass.wait_recv()
-    x_y[1] = (part_y[2] + pass_y[...].astype(f32)).astype(bf16)
-    y_x = send(x_y.at[1], x_y.at[2], y_send.at[2], y_recv.at[2], x=other)
-    y_x.start()
-    y_sib = send(part_y.at[1], in_y, y_send.at[0], y_recv.at[0], core=1 - core)
-    y_sib.start()
+    d_moves, y_passes = [None, None], [None, None]
+
+    def near_pair(b):
+        if b == 0:
+            cot_moves[0].wait_recv()
+        h2_moves[b][1].wait_recv()
+        forward_backward(b, 0)
+        return begin(part_d.at[b, 0, pl.ds(BLK, BLK)], in_d.at[b], d_send.at[b, 0], d_recv.at[b, 0], core=sib)
+
+    def far_pair(b, passed):
+        if b == 0:
+            cot_moves[1].wait_recv()
+        passed.wait_recv()
+        forward_backward(b, 1)
+        x_d[b, 0] = part_d[b, 1, BLK:].astype(bf16)
+        across = begin(x_d.at[b, 0], pass_d.at[b], d_send.at[b, 1], d_recv.at[b, 1], core=sib)
+        x_y[b] = part_y[b, 1, BLK:].astype(bf16)
+        y_passes[b] = begin(x_y.at[b], pass_y.at[b], y_send.at[b, 1], y_recv.at[b, 1], core=sib)
+        across.wait_recv()
+        x_d[b, 1] = (part_d[b, 1, :BLK] + pass_d[b].astype(f32)).astype(bf16)
+        return begin(x_d.at[b, 1], x_d.at[b, 2], d_send.at[b, 2], d_recv.at[b, 2], x=other)
+
+    def back(b, near, far):
+        near.wait_recv()
+        far.wait_recv()
+        grad_second = part_d[b, 0, :BLK] + in_d[b] + x_d[b, 2].astype(f32)
+        n2 = n2_ref[b]
+        sums_ref[3:4] += jnp.sum(grad_second * n2, axis=0, keepdims=True)
+        sums_ref[4:5] += jnp.sum(grad_second, axis=0, keepdims=True)
+        pulled = grad_second * small_ref[3:4]
+        inward = (
+            pulled - jnp.mean(pulled, axis=-1, keepdims=True) - n2 * jnp.mean(pulled * n2, axis=-1, keepdims=True)
+        )
+        grad_middle = cot_ref[rows_of(b)].astype(f32) + inward * scales[b]
+        middle_grad_ref[rows_of(b)] = grad_middle
+        branch = grad_middle.astype(bf16)
+        branch_ref[rows_of(b)] = branch
+        sums_ref[2:3] += jnp.sum(branch.astype(f32), axis=0, keepdims=True)
+        grad_out_t = inner(wo_ref[...], branch).astype(bf16)
+        for group in range(GROUPS):
+            grad_out[group, b] = grad_out_t[HW * group : HW * group + HW]
+        for away in range(1, GROUPS):
+            to = other_group(away)
+            begin(grad_out.at[to, b], grad_t_ref.at[2 * g + b], o_send.at[b, away], o_recv.at[b, g], g=to)
+        grad_t_ref[2 * g + b] = grad_out[g, b]
+
+    norm(0)
+    norm(1)
+    for load in loads:
+        load.wait()
+    near = [near_pair(0), None]
+    passed = [pass_on(0), None]
+    near[1] = near_pair(1)
+    far = [far_pair(0, passed[0]), None]
+    passed[1] = pass_on(1)
+    far[1] = far_pair(1, passed[1])
 
     def over_rows(left, right):
-        total = outer(left[0], right[0])
-        for part in range(1, 4):
-            total += outer(left[part], right[part])
+        total = None
+        for b in range(2):
+            for pair in range(2):
+                term = outer(left(b, pair), right(b, pair))
+                total = term if total is None else total + term
         return total.astype(bf16)
-
-    down_grad = over_rows(hids, cots)
-    up_grad = over_rows(h2s, dus)
 
     def parts(write):
         for y in range(2):
             pl.when(r == y)(lambda: write(keep_ref, y))
             pl.when(r != y)(lambda: write(give_ref, y))
 
-    def write_dense(ref, y):
+    down_grad = over_rows(lambda b, pair: hids[b, pair], lambda b, pair: pair_of(cots, b, pair))
+
+    def write_down(ref, y):
         for z in range(GROUPS):
             p = y * GROUPS + z
             ref[z, 0:96] = down_grad[96 * p : 96 * p + 96]
+
+    parts(write_down)
+    back(0, near[0], far[0])
+    up_grad = over_rows(lambda b, pair: pair_of(h2s, b, pair), lambda b, pair: dus[b, pair])
+
+    def write_up(ref, y):
+        for z in range(GROUPS):
+            p = y * GROUPS + z
             ref[z, 96:144] = up_grad[48 * p : 48 * p + 48]
             ref[z, 144:192] = up_grad[half + 48 * p : half + 48 * p + 48]
 
-    parts(write_dense)
-
-    d_sib.wait_recv()
-    d_x.wait_recv()
-    grad_second = part_d[0] + in_d[...] + x_d[2].astype(f32)
-    n2 = n2_ref[...]
-    sums_ref[3:4] = jnp.sum(grad_second * n2, axis=0, keepdims=True)
-    sums_ref[4:5] = jnp.sum(grad_second, axis=0, keepdims=True)
-    pulled = grad_second * small_ref[3:4]
-    inward = pulled - jnp.mean(pulled, axis=-1, keepdims=True) - n2 * jnp.mean(pulled * n2, axis=-1, keepdims=True)
-    grad_middle = cot_ref[...].astype(f32) + inward * scale
-    middle_grad_ref[...] = grad_middle
-    branch = grad_middle.astype(bf16)
-    sums_ref[2:3] = jnp.sum(branch.astype(f32), axis=0, keepdims=True)
-    grad_out_t = inner(wo_ref[...], branch).astype(bf16)
-    for group in range(GROUPS):
-        for b in range(2):
-            grad_out[group, b] = grad_out_t[HW * group : HW * group + HW, BLK * b : BLK * b + BLK]
-    grad_moves = []
-    for away in range(1, GROUPS):
-        to = other_group(away)
-        grad_moves.append(
-            send(grad_out.at[to], grad_t_ref.at[pl.ds(2 * g, 2)], o_send.at[away], o_recv.at[g], g=to)
-        )
-        grad_moves[-1].start()
-    grad_t_ref[pl.ds(2 * g, 2)] = grad_out[g]
+    parts(write_up)
+    back(1, near[1], far[1])
 
     for owner in range(2):
         for c in range(2):
-            piece = dot(attn_t[half * owner + fourth * c : half * owner + fourth * c + fourth], branch)
+            piece = dot(attn_t[half * owner + fourth * c : half * owner + fourth * c + fourth], branch_ref[...])
 
             @pl.when(core == c)
             def _():
@@ -806,18 +816,24 @@
             def _():
                 wo_give[owner] = piece.astype(bf16)
 
-    w_sib = send(wo_give, wo_in, w_send.at[0], w_recv.at[0], core=1 - core)
-    w_sib.start()
-    y_x.wait_recv()
-    y_sib.wait_recv()
-    result_ref[...] = (
-        mid_ref[...] + part_y[0] + in_y[...] + x_y[2].astype(f32) + small_ref[5:6]
-    ).astype(bf16)
+    w_sib = begin(wo_give, wo_in, w_send.at[0], w_recv.at[0], core=sib)
+    y_sibs = [
+        begin(part_y.at[b, 0, pl.ds(BLK, BLK)], in_y.at[b], y_send.at[b, 0], y_recv.at[b, 0], core=sib)
+        for b in range(2)
+    ]
     w_sib.wait_recv()
     wo_pass[...] = (wo_keep[other] + wo_in[other].astype(f32)).astype(bf16)
-    w_x = send(wo_pass, wo_x, w_send.at[1], w_recv.at[1], x=other)
-    w_x.start()
+    w_x = begin(wo_pass, wo_x, w_send.at[1], w_recv.at[1], x=other)
+    for b in range(2):
+        y_passes[b].wait_recv()
+        y_give_ref[rows_of(b)] = (part_y[b, 1, :BLK] + pass_y[b].astype(f32)).astype(bf16)
+        y_sibs[b].wait_recv()
+        base_ref[rows_of(b)] = mid_ref[b] + part_y[b, 0, :BLK] + in_y[b] + small_ref[5:6]
     mine = wo_keep[x] + wo_in[x].astype(f32)
+    for b in range(2):
+        for away in range(1, GROUPS):
+            source = other_group(away)
+            arrived(grad_t_ref.at[2 * source + b], o_send.at[b, away], o_recv.at[b, source], x)
     w_x.wait_recv()
     wo_sum = (mine + wo_x[...].astype(f32)).astype(bf16)
 
@@ -827,26 +843,21 @@
             ref[z, 192:UNIT] = wo_sum[24 * p : 24 * p + 24]
 
     parts(write_wo)
-    for away in range(1, GROUPS):
-        source = other_group(away)
-        send(
-            grad_t_ref.at[pl.ds(2 * source, 2)], grad_t_ref.at[pl.ds(2 * source, 2)],
-            o_send.at[away], o_recv.at[source], g=source,
-        ).wait_recv()
-    for item in (
-        *cot_moves, cot_pass, *h2_moves, h2_pass, d_sib, d_pass, d_x, y_sib, y_pass, y_x, w_sib, w_x, *attn_moves, *grad_moves,
-    ):
-        item.wait_send()
-
-
-def dense(out_t, tokens, cot, small, up, wo, down):
+    for move in pending:
+        move.wait_send()
+
+
+def dense(out_t, tokens, cot, cot_x, small, wo, up_mine, up_other, down):
     rows, width = tokens.shape
     dma = pltpu.SemaphoreType.DMA
     full = (rows, width)
+    part = (BLK, width)
+    pair = (2 * BLK, width)
     fourth = (width // 4, width)
     return pl.pallas_call(
         dense_kernel,
         out_shape=(
+            jax.ShapeDtypeStruct(full, f32),
             jax.ShapeDtypeStruct(full, bf16),
             jax.ShapeDtypeStruct(full, f32),
             jax.ShapeDtypeStruct(out_t.shape, bf16),
@@ -854,40 +865,43 @@
             jax.ShapeDtypeStruct((GROUPS, UNIT, width), bf16),
             jax.ShapeDtypeStruct(small.shape, f32),
         ),
-        in_specs=[whole_vmem()] * 6 + [in_hbm()],
-        out_specs=(whole_vmem(),) * 6,
+        in_specs=[whole_vmem()] * 6 + [anywhere()] * 3,
+        out_specs=(whole_vmem(),) * 7,
         scratch_shapes=[
+            pltpu.VMEM((width, width), bf16),
             pltpu.VMEM((width, width), bf16),
             pltpu.VMEM((GROUPS, 2, HW, BLK), bf16),
             pltpu.VMEM((width, rows), bf16),
-            pltpu.VMEM((4, *full), bf16),
-            pltpu.VMEM((4, *full), bf16),
-            pltpu.VMEM(full, f32),
-            pltpu.VMEM(full, f32),
-            pltpu.VMEM((4, *full), f32),
-            pltpu.VMEM((4, *full), f32),
-            pltpu.VMEM(full, f32),
-            pltpu.VMEM(full, f32),
+            pltpu.VMEM((2, 4, *part), bf16),
+            pltpu.VMEM((2, 4, *part), bf16),
+            pltpu.VMEM((2, *part), f32),
+            pltpu.VMEM((2, *part), f32),
+            pltpu.VMEM((2, BLK, 1), f32),
+            pltpu.VMEM((2, 2, *pair), f32),
+            pltpu.VMEM((2, 2, *pair), f32),
+            pltpu.VMEM((2, *part), f32),
+            pltpu.VMEM((2, *part), f32),
+            pltpu.VMEM((2, *part), bf16),
+            pltpu.VMEM((2, *part), bf16),
+            pltpu.VMEM((2, *part), bf16),
+            pltpu.VMEM((2, 3, *part), bf16),
+            pltpu.VMEM((2, 2, *pair), bf16),
+            pltpu.VMEM((2, 2, *pair), bf16),
             pltpu.VMEM(full, bf16),
-            pltpu.VMEM(full, bf16),
-            pltpu.VMEM((3, *full), bf16),
-            pltpu.VMEM((3, *full), bf16),
-            pltpu.VMEM((4, *full), bf16),
-            pltpu.VMEM((4, *full), bf16),
             pltpu.VMEM((GROUPS, 2, HW, BLK), bf16),
             pltpu.VMEM((2, *fourth), f32),
             pltpu.VMEM((2, *fourth), bf16),
             pltpu.VMEM((2, *fourth), bf16),
             pltpu.VMEM(fourth, bf16),
             pltpu.VMEM(fourth, bf16),
-            dma(()), dma((GROUPS,)), dma((GROUPS,)), dma((3,)), dma((3,)), dma((3,)), dma((3,)),
-            dma((3,)), dma((3,)), dma((3,)), dma((3,)), dma((GROUPS,)), dma((GROUPS,)), dma((2,)), dma((2,)),
+            dma((3,)), dma((2, GROUPS)), dma((2, GROUPS)), dma((2,)), dma((2,)), dma((2, 3)), dma((2, 3)),
+            dma((2, 2)), dma((2, 2)), dma((2, 3)), dma((2, 3)), dma((2, GROUPS)), dma((2, GROUPS)), dma((2,)), dma((2,)),
         ],
         compiler_params=pltpu.CompilerParams(
             collective_id=1, has_side_effects=True, vmem_limit_bytes=40 << 20
         ),
         name="dense",
-    )(out_t, tokens, cot, small, up, wo, down)
+    )(out_t, tokens, cot, cot_x, small, wo, up_mine, up_other, down)
 
 
 FARTHEST = ((3, 2, 1, 0), (3, 0, 2, 1), (0, 3, 1, 2), (0, 1, 2, 3))
@@ -1330,13 +1344,14 @@
 
 
 def layout_kernel(
-    big_ref, query_ref, kv_ref, sums_ref,
+    big_ref, query_ref, kv_ref, sums_ref, base_ref, got_ref,
     up_out, down_out, wo_out, query_out, key_out, value_out,
-    low_gain, low_shift, query_bias, value_bias, out_bias, high_gain, high_shift, up_bias, down_bias,
+    low_gain, low_shift, query_bias, value_bias, out_bias, high_gain, high_shift, up_bias, down_bias, result_out,
 ):
     x = lax.axis_index("x")
     width = big_ref.shape[-1]
     half = width // 2
+    result_out[...] = (base_ref[...] + got_ref[...].astype(f32)).astype(bf16)
     for core in range(2):
         down_out[core] = big_ref[core, 0, 0:96].astype(f32)
         wo_out[core] = big_ref[core, 0, 192:UNIT].astype(f32)
@@ -1370,7 +1385,7 @@
         ).reshape(2 * width)
 
 
-def lay_out(big, query, kv, sums):
+def lay_out(big, query, kv, sums, base, got):
     width = big.shape[-1]
     half, fourth = width // 2, width // 4
     rows = fourth // PARTS
@@ -1393,12 +1408,15 @@
             *[vector] * 7,
             jax.ShapeDtypeStruct((2 * width,), f32),
             vector,
+            jax.ShapeDtypeStruct(base.shape, bf16),
         ),
         in_specs=[
             spec((2, 1, UNIT, width), lambda p: (0, p, 0, 0)),
             spec((2, GROUPS, rows, query.shape[-1]), lambda p: (0, 0, p, 0)),
             spec((2, GROUPS, rows, kv.shape[-1]), lambda p: (0, 0, p, 0)),
             spec(sums.shape, lambda p: (0, 0)),
+            spec((base.shape[0] // PARTS, width), lambda p: (p, 0)),
+            spec((base.shape[0] // PARTS, width), lambda p: (p, 0)),
         ],
         out_specs=(
             spec((48, 4 * width), lambda p: (p, 0)),
@@ -1407,12 +1425,13 @@
             *[fixed(half)] * 7,
             fixed(2 * width),
             fixed(half),
+            spec((base.shape[0] // PARTS, width), lambda p: (p, 0)),
         ),
         compiler_params=pltpu.CompilerParams(
             vmem_limit_bytes=VMEM_LIMIT, dimension_semantics=("arbitrary",)
         ),
         name="lay_out",
-    )(big, query, kv, sums)
+    )(big, query, kv, sums, base, got)
 
 
 ROWS = ("s", "r", "core", "x")
@@ -1427,8 +1446,14 @@
     rows, width = tokens.shape
     half = width // 2
     blocks = deal.shape[0]
-    kv, q, normed, small, wfull, up, wo = gather(
-        tokens, query_weight, key_weight, value_weight, up_weight, output_weight,
+    core, x = lax.axis_index("core"), lax.axis_index("x")
+    swap = ((0, 1), (1, 0))
+
+    def up_columns(owner):
+        return lax.dynamic_slice_in_dim(up_weight, (2 * owner + core) * width, width, 1)
+
+    kv, q, normed, small, wfull, wo = gather(
+        tokens, query_weight, key_weight, value_weight, output_weight,
         first_gain, first_shift, output_bias, second_gain, second_shift, down_bias, query_bias, value_bias, up_bias,
     )
     wide = blocks > 8 * 2 * GROUPS
@@ -1436,11 +1461,15 @@
         kv = lax.all_gather(kv, "s", axis=0, tiled=True)
     kv = kv.reshape(blocks, BLK, 2 * HW)
     q = q.reshape(2 * GROUPS, BLK, 2 * BLK)
+    cot_x, up_other, kv = lax.optimization_barrier((cotangent, up_columns(1 - x), kv))
+    up_other = lax.ppermute(up_other, "x", swap)
+    cot_x = lax.ppermute(cot_x, "x", swap)
     out_t, kept, lse = attend_forward(deal, doc_lengths, q, kv)
-    result, grad_middle, grad_t, bundle, over, sums = dense(
-        out_t, tokens, cotangent, small, up, wo, down_weight
+    base, y_give, grad_middle, grad_t, bundle, over, sums = dense(
+        out_t, tokens, cotangent, cot_x, small, wo, up_columns(x), up_other, down_weight
     )
-    over = lax.ppermute(over, "r", ((0, 1), (1, 0)))
+    y_got = lax.ppermute(y_give, "x", swap)
+    over = lax.ppermute(over, "r", swap)
     dq, dkv = attend_backward(deal, doc_lengths, q, kv, lse, grad_t, kept)
     dkv = dkv.reshape(-1, GROUPS, rows, 2 * HW)
     if wide:
@@ -1456,8 +1485,8 @@
 
     (
         up_own, down_own, wo_own, query_own, key_own, value_own,
-        low_gain, low_shift, query_sum, value_sum, out_sum, high_gain, high_shift, up_sum, down_sum,
-    ) = lay_out(big.reshape(2, PARTS, UNIT, width), query_own, kv_own, sums)
+        low_gain, low_shift, query_sum, value_sum, out_sum, high_gain, high_shift, up_sum, down_sum, result,
+    ) = lay_out(big.reshape(2, PARTS, UNIT, width), query_own, kv_own, sums, base, y_got)
 
     def flat(item):
         return item.reshape(-1, width)

time: 315 us -> 307 us (0.975); the launches traced: 318 us -> 303 us
  Pallas kernels: 303 us -> 286 us
    pallas_call x1, Pallas kernels: 61.3 us -> 46.5 us  [dense(): pl.pallas_call(dense_kernel, out_shape=(jax.ShapeDtypeStruct(full, f32),...]
    pallas_call x1, Pallas kernels: 65.6 us -> 61.7 us  [gather(): pl.pallas_call(gather_kernel, out_shape=(jax.ShapeDtypeStruct((8, GROUPS,...]
    pallas_call x1, Pallas kernels: 121 us -> 117 us  [scatter(): pl.pallas_call(scatter_kernel, out_shape=(jax.ShapeDtypeStruct(full, f32)...]
    unnamed x34 -> x35, local copies, waits for them, and re-layouts: 9.99 us -> 10.9 us
  transfers between devices with their start and end apart: 1 -> 4, of which waited for: 1 -> 0; matrix products, arithmetic and copies ran while one was open for 0% -> 0% of each run, Pallas kernels for 9% -> 55%
where the time goes in v2:
time: 307 us; the launch traced here: 303 us
  Pallas kernels  286 us (93%)
  local copies, waits for them, and re-layouts  12.2 us (4%)
  starting transfers between devices  4.11 us (1%)
    pallas_call x1, Pallas kernels, scatter(): pl.pallas_call(scatter_kernel, out_shape=(jax.ShapeDtypeStruct(full, f32)...  117 us
    pallas_call x1, Pallas kernels, gather(): pl.pallas_call(gather_kernel, out_shape=(jax.ShapeDtypeStruct((8, GROUPS,...  61.7 us
    pallas_call x1, Pallas kernels, dense(): pl.pallas_call(dense_kernel, out_shape=(jax.ShapeDtypeStruct(full, f32),...  46.5 us
    pallas_call x1, Pallas kernels, attend_backward(): pl.pallas_call(backward_kernel, out_shape=(jax.ShapeDtypeStruct((slots, B...  30.8 us
    pallas_call x1, Pallas kernels, attend_forward(): pl.pallas_call(forward_kernel, out_shape=(jax.ShapeDtypeStruct((slots, HW...  19.5 us
    unnamed x35, local copies, waits for them, and re-layouts  10.9 us
    pallas_call x1, Pallas kernels, lay_out(): pl.pallas_call(layout_kernel, grid=(PARTS,), out_shape=(jax.ShapeDtypeStr...  10.5 us
  transfers between devices with their start and end apart: 4, of which 0 were waited for; matrix products, arithmetic and copies ran while one was open for 0% of the time, Pallas kernels for 55%

profile of v2, /device:TPU:0, one launch (start us, length us, event | category | flops | bytes accessed | tf_op | source)
XLA Modules:
  0.0 303.4 jit_solution(804974622611549238)
XLA Ops:
  0.7 1.3 constant_dynamic-slice_fusion
  2.0 0.0 copy-start.10
  2.0 0.0 copy-start.13
  2.0 0.0 copy-start.14
  2.0 61.7 %gather.1 = (bf16[8,4,256,384]{3,2,1,0:T(8,128)(2,1)}, bf16[4,256,256]{2,1,0:T(8,128)(2,1)}, bf16[4,256,768]{2,1,0:T(8,128)(2,1)}, f32[16,768]{1,0:T(8,128)}, bf...) custom-call(bf16[256,768]{1,0:T(8,128)(2,1)} %tokens_ref.5, bf16[384,768]{1,0:T(8,128)(2,1)} %query_any.1, ...), custom_call_target="tpu_custom_call" | custom-call | tf_op jit(solution)/shard_map/gather/pallas_call | solution.py:580
  63.7 1.2 collective-permute-start.1
  65.0 0.9 collective-permute-start
  65.9 2.8 copy-done
  68.7 1.0 copy-done.3
  69.7 19.5 %attend_forward.1 = (bf16[8,192,128]{2,1,0:T(8,128)(2,1)S(1)}, f32[8,192,128]{2,1,0:T(8,128)S(1)}, f32[8,1,384]{2,1,0:T(1,128)S(1)}) custom-call(s32[64]{0:T(128)S(1)} %copy-done.13, s32[4]{0:T(128)S(1)} %copy-done.14, bf16[8,128,256]{2,1,0:T(8,128)(2,1)S(1)} %bitcast.12, bf16[64,128,384]{2,1,0:T(8,128)(2,1)S(1)} %bitcast.11), custom_call_target="tpu_custom_call" | custom-call | tf_op jit(solution)/shard_map/attend_forward/pallas_call | solution.py:182
  89.3 46.5 %dense.1 = (f32[256,768]{1,0:T(8,128)S(1)}, bf16[256,768]{1,0:T(8,128)(2,1)S(1)}, f32[256,768]{1,0:T(8,128)S(1)}, bf16[8,192,128]{2,1,0:T(8,128)(2,1)S(1)}, bf16...) custom-call(bf16[8,192,128]{2,1,0:T(8,128)(2,1)S(1)} %get-tuple-element.63.out_t_ref, ...), custom_call_target="tpu_custom_call" | custom-call | tf_op jit(solution)/shard_map/dense/pallas_call | solution.py:857
  135.8 1.1 copy-done.5
  136.8 0.9 copy-done.7
  137.7 0.9 copy-done.8
  138.6 2.0 collective-permute-start.3
  140.6 30.8 %attend_backward.1 = (bf16[8,128,256]{2,1,0:T(8,128)(2,1)S(1)}, bf16[64,128,384]{2,1,0:T(8,128)(2,1)}) custom-call(s32[64]{0:T(128)S(1)} %copy-done.13, s32[4]{0:T(128)S(1)} %copy-done.14, bf16[8,128,256]{2,1,0:T(8,128)(2,1)S(1)} %bitcast.13, bf16[64,128,384]{2,1,0:T(8,128)(2,1)} %bitcast.10, f32[8,1,384]{2,1,0:T(1,128)S(1)} %get-tuple-element.62.lse_ref, ...), custom_call_target="tpu_custom_call" | custom-call | tf_op jit(solution)/shard_map/attend_backward/pallas_call | solution.py:309
  171.4 1.1 copy-done.15
  172.4 117.3 %scatter.1 = (f32[256,768]{1,0:T(8,128)S(1)}, bf16[2,2,4,216,768]{4,3,2,1,0:T(8,128)(2,1)}, bf16[2,4,192,256]{3,2,1,0:T(8,128)(2,1)S(1)}, bf16[2,4,192,384]{3,2,1,0:T(8,128)(2,1)}, f32[24,768]{1,0:T(8,128)S(1)}) custom-call(bf16[8,4,256,384]{3,2,1,0:T(8,128)(2,1)} %bitcast.15, bf16[4,256,256]{2,1,0:T(8,128)(2,1)S(1)} %bitcast.14, ...), custom_call_target="tpu_custom_call" | custom-call | tf_op jit(solution)/shard_map/scatter/pallas_call | solution.py:1289
  289.8 0.0 copy-start.9
  289.8 0.9 copy-done.9
  290.6 0.6 copy-done.12
  291.3 0.8 copy-done.16
  292.1 10.5 %lay_out.1 = (f32[384,3072]{1,0:T(8,128)}, f32[2,768,768]{2,1,0:T(8,128)}, f32[2,192,768]{2,1,0:T(8,128)}, f32[2,192,768]{2,1,0:T(8,128)}, f32[2,192,768]{2,1,0:...) custom-call(bf16[2,8,216,768]{3,2,1,0:T(8,128)(2,1)} %bitcast.16, ...), custom_call_target="tpu_custom_call" | custom-call | tf_op jit(solution)/shard_map/lay_out/pallas_call | solution.py:1401
  302.5 0.9 copy.37
  (26 shorter events, 0.1 us)
Async XLA Ops:
  2.0 63.0 %copy-start.10 = (bf16[256,768]{1,0:T(8,128)(2,1)S(1)}, bf16[256,768]{1,0:T(8,128)(2,1)}, u32[]{:S(2)}) copy-start(bf16[256,768]{1,0:T(8,128)(2,1)} %cot_ref.1) | copy-start | bytes 1179652
  2.0 63.9 %copy-start.13 = (s32[64]{0:T(128)S(1)}, s32[64]{0:T(128)}, u32[]{:S(2)}) copy-start(s32[64]{0:T(128)} %deal_ref.3) | copy-start | bytes 772
  2.0 63.9 %copy-start.14 = (s32[4]{0:T(128)S(1)}, s32[4]{0:T(128)}, u32[]{:S(2)}) copy-start(s32[4]{0:T(128)} %lengths_ref.3) | copy-start | bytes 52
  63.7 25.5 %collective-permute-start.1 = (bf16[384,768]{1,0:T(8,128)(2,1)S(1)}, bf16[384,768]{1,0:T(8,128)(2,1)S(1)}, u32[]{:S(2)}, u32[]{:S(2)}) collective-permute-start(bf16[384,768]{1,0:T(8,128)(2,1)S(1)} %get-tuple-element.67), channel_id=1, source_target_pairs={{0,1},{1,0},{2,3},{3,2},{4,5},{5,4},{6,7},{7,6},{8,9},{9,8},{10,11... | collective-permute-start | bytes 1769480 | tf_op jit(solution)/shard_map/ppermute | solution.py:1465
  65.0 24.2 %collective-permute-start = (bf16[256,768]{1,0:T(8,128)(2,1)S(1)}, bf16[256,768]{1,0:T(8,128)(2,1)S(1)}, u32[]{:S(2)}, u32[]{:S(2)}) collective-permute-start(bf16[256,768]{1,0:T(8,128)(2,1)S(1)} %copy-done.10), channel_id=1, source_target_pairs={{0,1},{1,0},{2,3},{3,2},{4,5},{5,4},{6,7},{7,6},{8,9},{9,8},{10,11... | collective-permute-start | bytes 1179656 | tf_op jit(solution)/shard_map/ppermute | solution.py:1466
  65.9 2.8 copy-start
  68.7 1.0 copy-start.3
  69.7 19.5 %copy-start.1 = (bf16[256,768]{1,0:T(8,128)(2,1)S(1)}, bf16[256,768]{1,0:T(8,128)(2,1)}, u32[]{:S(2)}) copy-start(bf16[256,768]{1,0:T(8,128)(2,1)} %tokens_ref.5) | copy-start | bytes 1179652
  69.7 19.5 %copy-start.2 = (bf16[1536,768]{1,0:T(8,128)(2,1)S(1)}, bf16[1536,768]{1,0:T(8,128)(2,1)}, u32[]{:S(2)}) copy-start(bf16[1536,768]{1,0:T(8,128)(2,1)} %down_any.1) | copy-start | bytes 7077892
  69.7 19.5 %copy-start.6 = (bf16[768,768]{1,0:T(8,128)(2,1)S(1)}, bf16[768,768]{1,0:T(8,128)(2,1)}, u32[]{:S(2)}) copy-start(bf16[768,768]{1,0:T(8,128)(2,1)} %get-tuple-element.66.wo_ref) | copy-start | bytes 3538948
  69.7 19.5 %copy-start.11 = (f32[16,768]{1,0:T(8,128)S(1)}, f32[16,768]{1,0:T(8,128)}, u32[]{:S(2)}) copy-start(f32[16,768]{1,0:T(8,128)} %get-tuple-element.65.small_ref) | copy-start | bytes 147460
  89.3 51.3 %copy-start.4 = (bf16[4,256,256]{2,1,0:T(8,128)(2,1)S(1)}, bf16[4,256,256]{2,1,0:T(8,128)(2,1)}, u32[]{:S(2)}) copy-start(bf16[4,256,256]{2,1,0:T(8,128)(2,1)} %get-tuple-element.59) | copy-start | bytes 1572868
  135.8 1.1 copy-start.5
  136.8 0.9 copy-start.7
  137.7 0.9 copy-start.8
  138.6 32.8 %collective-permute-start.2 = (bf16[4,216,768]{2,1,0:T(8,128)(2,1)S(1)}, bf16[4,216,768]{2,1,0:T(8,128)(2,1)S(1)}, u32[]{:S(2)}, u32[]{:S(2)}) collective-permute-start(bf16[4,216,768]{2,1,0:T(8,128)(2,1)S(1)} %get-tuple-element.76), channel_id=1, source_target_pairs={{0,4},{4,0},{1,5},{5,1},{2,6},{6,2},{3,7},{7,3},{8,12},{12,8},{9,1... | collective-permute-start | bytes 3981320 | tf_op jit(solution)/shard_map/ppermute | solution.py:1472
  138.6 152.7 %collective-permute-start.3 = (bf16[256,768]{1,0:T(8,128)(2,1)S(1)}, bf16[256,768]{1,0:T(8,128)(2,1)S(1)}, u32[]{:S(2)}, u32[]{:S(2)}) collective-permute-start(bf16[256,768]{1,0:T(8,128)(2,1)S(1)} %get-tuple-element.83), channel_id=1, source_target_pairs={{0,1},{1,0},{2,3},{3,2},{4,5},{5,4},{6,7},{7,6},{8,9},{9,8},{10,11... | collective-permute-start | bytes 1179656 | tf_op jit(solution)/shard_map/ppermute | solution.py:1471
  171.4 1.1 copy-start.15
  289.8 0.9 copy-start.9
  290.6 0.6 copy-start.12
  291.3 0.8 copy-start.16

commit v3 on v2

--- a/solution.py
+++ b/solution.py
@@ -351,26 +351,39 @@
     return (r * 2 + core) * 2 + x
 
 
-def greet(g, r, core, x, line):
+AROUND = ((0, 0, 1), (0, 1, 0), (0, 1, 1), (1, 0, 0), (1, 0, 1), (1, 1, 0), (1, 1, 1))
+
+
+def neighbour(r, core, x, step):
+    dr, dc, dx = AROUND[step]
+    return {"r": 1 - r if dr else r, "core": 1 - core if dc else core, "x": 1 - x if dx else x}
+
+
+def greet(g, r, core, x, line, around=False):
     barrier = pltpu.get_barrier_semaphore()
 
     def hello(**device):
         pl.semaphore_signal(barrier, inc=1, device_id=device, device_id_type=MESH)
 
-    hello(core=1 - core)
-    hello(x=1 - x)
-    hello(r=1 - r)
+    if around:
+        for step in range(len(AROUND)):
+            hello(**neighbour(r, core, x, step))
+    else:
+        hello(core=1 - core)
+        hello(x=1 - x)
+        hello(r=1 - r)
+    near = len(AROUND) if around else 3
     if line:
         for away in range(1, GROUPS):
             hello(g=lax.rem(g + away, GROUPS))
-        pl.semaphore_wait(barrier, 3 + GROUPS - 1)
+        pl.semaphore_wait(barrier, near + GROUPS - 1)
     else:
         pl.when(g > 0)(lambda: hello(g=g - 1))
         pl.when(g < GROUPS - 1)(lambda: hello(g=g + 1))
-        pl.semaphore_wait(barrier, 5 - jnp.where(g == 0, 1, 0) - jnp.where(g == GROUPS - 1, 1, 0))
-
-
-NEAREST = tuple(tuple(sorted(range(GROUPS), key=lambda s: (abs(s - z), s))) for z in range(GROUPS))
+        pl.semaphore_wait(barrier, near + 2 - jnp.where(g == 0, 1, 0) - jnp.where(g == GROUPS - 1, 1, 0))
+
+
+NEAREST = ((0, 1, 2, 3), (1, 2, 0, 3), (2, 1, 3, 0), (3, 2, 1, 0))
 
 
 def nearest(g, step):
@@ -613,11 +626,12 @@
 
 PARTS = 8
 UNIT = 216
+KEPT = 168
 
 
 def dense_kernel(
     out_t_ref, tokens_ref, cot_ref, cot_x_ref, small_ref, wo_ref, up_mine, up_other, down_any,
-    base_ref, y_give_ref, middle_grad_ref, grad_t_ref, keep_ref, give_ref, sums_ref,
+    base_ref, x_give_ref, middle_grad_ref, grad_t_ref, keep_ref, give_ref, far_ref, sums_ref,
     down_ref, up_ref, attn_in, attn_t, cots, h2s, mid_ref, n2_ref, scales, part_y, part_d, in_y, in_d, pass_y, pass_d,
     x_y, x_d, hids, dus, branch_ref, grad_out, wo_keep, wo_give, wo_in, wo_pass, wo_x,
     l_sem, a_send, a_recv, c_send, c_recv, h_send, h_recv, y_send, y_recv, d_send, d_recv, o_send, o_recv,
@@ -795,13 +809,33 @@
     back(0, near[0], far[0])
     up_grad = over_rows(lambda b, pair: pair_of(h2s, b, pair), lambda b, pair: dus[b, pair])
 
-    def write_up(ref, y):
-        for z in range(GROUPS):
-            p = y * GROUPS + z
-            ref[z, 96:144] = up_grad[48 * p : 48 * p + 48]
-            ref[z, 144:192] = up_grad[half + 48 * p : half + 48 * p + 48]
-
-    parts(write_up)
+    def up_part(p, h):
+        return up_grad[half * h + 48 * p : half * h + 48 * p + 48]
+
+    def write_up(y, h):
+        @pl.when((r == y) & (x == h))
+        def _():
+            for z in range(GROUPS):
+                keep_ref[z, 96:144] = up_part(y * GROUPS + z, h)
+
+        @pl.when((r != y) & (x == h))
+        def _():
+            for z in range(GROUPS):
+                give_ref[z, 96:144] = up_part(y * GROUPS + z, h)
+
+        @pl.when((r == y) & (x != h))
+        def _():
+            for z in range(GROUPS):
+                x_give_ref[rows + 48 * z : rows + 48 * z + 48] = up_part(y * GROUPS + z, h)
+
+        @pl.when((r != y) & (x != h))
+        def _():
+            for z in range(GROUPS):
+                far_ref[z] = up_part(y * GROUPS + z, h)
+
+    for y in range(2):
+        for h in range(2):
+            write_up(y, h)
     back(1, near[1], far[1])
 
     for owner in range(2):
@@ -826,7 +860,7 @@
     w_x = begin(wo_pass, wo_x, w_send.at[1], w_recv.at[1], x=other)
     for b in range(2):
         y_passes[b].wait_recv()
-        y_give_ref[rows_of(b)] = (part_y[b, 1, :BLK] + pass_y[b].astype(f32)).astype(bf16)
+        x_give_ref[rows_of(b)] = (part_y[b, 1, :BLK] + pass_y[b].astype(f32)).astype(bf16)
         y_sibs[b].wait_recv()
         base_ref[rows_of(b)] = mid_ref[b] + part_y[b, 0, :BLK] + in_y[b] + small_ref[5:6]
     mine = wo_keep[x] + wo_in[x].astype(f32)
@@ -840,7 +874,7 @@
     def write_wo(ref, y):
         for z in range(GROUPS):
             p = y * GROUPS + z
-            ref[z, 192:UNIT] = wo_sum[24 * p : 24 * p + 24]
+            ref[z, 144:KEPT] = wo_sum[24 * p : 24 * p + 24]
 
     parts(write_wo)
     for move in pending:
@@ -858,15 +892,16 @@
         dense_kernel,
         out_shape=(
             jax.ShapeDtypeStruct(full, f32),
-            jax.ShapeDtypeStruct(full, bf16),
+            jax.ShapeDtypeStruct((rows + 48 * GROUPS, width), bf16),
             jax.ShapeDtypeStruct(full, f32),
             jax.ShapeDtypeStruct(out_t.shape, bf16),
-            jax.ShapeDtypeStruct((GROUPS, UNIT, width), bf16),
-            jax.ShapeDtypeStruct((GROUPS, UNIT, width), bf16),
+            jax.ShapeDtypeStruct((GROUPS, KEPT, width), bf16),
+            jax.ShapeDtypeStruct((GROUPS, KEPT, width), bf16),
+            jax.ShapeDtypeStruct((GROUPS, 48, width), bf16),
             jax.ShapeDtypeStruct(small.shape, f32),
         ),
         in_specs=[whole_vmem()] * 6 + [anywhere()] * 3,
-        out_specs=(whole_vmem(),) * 7,
+        out_specs=(whole_vmem(),) * 8,
         scratch_shapes=[
             pltpu.VMEM((width, width), bf16),
             pltpu.VMEM((width, width), bf16),
@@ -993,18 +1028,19 @@
 
 
 def scatter_kernel(
-    dkv_ref, dq_ref, normed_ref, wfull_ref, tokens_ref, mgrad_ref, small_ref, bundle_ref, by_in, sums_in,
+    dkv_ref, dq_any, normed_any, wfull_any, tokens_any, mgrad_any, keep_any, over_any, near_any, far_any, small_ref, sums_in,
     tokens_grad_ref, big_ref, qout_ref, kvout_ref, sums_ref,
+    dq_ref, normed_ref, wfull_ref, tokens_ref, mgrad_ref, kept, over, near, far,
     own_kv, sib_kv, keep_x, give_x, in_x, give_y, in_y, part_a, total_a, inward_a, outward_a, wg_kv,
     by_sum, total_b, inward_b, outward_b, unit,
     q_keep, q_give, q_in, q_pass, q_x, q_y, q_sum, v_keep, v_give, v_in, v_pass, v_x, v_y, v_sum,
-    sums_got,
-    own_sem, k_send, k_recv, x_send, x_recv, y_send, y_recv, ca_send, ca_recv,
-    cb_send, cb_recv, u_send, u_recv, rb_own, rb_send, rb_recv,
+    sums_got, late, late_sum, late_got,
+    load_sem, own_sem, k_send, k_recv, x_send, x_recv, y_send, y_recv, ca_send, ca_recv,
+    cb_send, cb_recv, rb_own, rb_send, rb_recv,
     fy_send, fy_recv, fs_send, fs_recv,
     q_send, q_recv, rq_own, rq_send, rq_recv, qs_send, qs_recv,
     v_send, v_recv, rv_own, rv_send, rv_recv, vs_send, vs_recv,
-    s_send, s_recv, l_sem,
+    s_send, s_recv, t_send, t_recv, l_sem,
 ):
     g, r, core, x = place()
     other, sib, far_r = 1 - x, 1 - core, 1 - r
@@ -1012,7 +1048,19 @@
     half = width // 2
     fourth = half // 2
     wide_q = 2 * BLK
-    greet(g, r, core, x, True)
+    loads = [
+        pltpu.make_async_copy(what, where, load_sem.at[i])
+        for i, (what, where) in enumerate(
+            (
+                (keep_any, kept), (over_any, over), (near_any.at[pl.ds(rows, 48 * GROUPS)], near), (far_any, far),
+                (dq_any, dq_ref), (normed_any, normed_ref), (wfull_any, wfull_ref), (tokens_any, tokens_ref),
+                (mgrad_any, mgrad_ref),
+            )
+        )
+    ]
+    for load in loads:
+        load.start()
+    greet(g, r, core, x, True, True)
     pending = []
 
     def begin(src, dst, out_sem, in_sem, **device):
@@ -1030,7 +1078,9 @@
     for i in range(GROUPS):
         c = farthest(g, i)
         for spot in range(4):
-            own = pltpu.make_async_copy(dkv_ref.at[seat(spot // 2, core, spot % 2), c], own_kv.at[i, spot], own_sem.at[i, spot])
+            own = pltpu.make_async_copy(
+                dkv_ref.at[seat(spot // 2, core, spot % 2), c], own_kv.at[i, spot], own_sem.at[i, spot]
+            )
             own.start()
             across = begin(
                 dkv_ref.at[seat(spot // 2, sib, spot % 2), c], sib_kv.at[i, spot],
@@ -1038,7 +1088,7 @@
             )
             kv_moves.append((own, across))
 
-    def split(total, keep, give, wide):
+    def split(total, keep, give):
         for owner in range(2):
             for c in range(2):
                 low = half * owner + fourth * c
@@ -1055,20 +1105,23 @@
     def scaled(c):
         return dq_ref[c] * bf16(SCALE)
 
+    q_move = send(q_give, q_in, q_send.at[0], q_recv.at[0], core=sib)
+
     def query_grad():
+        loads[4].wait()
+        loads[5].wait()
         query_total = outer(normed_ref[0], scaled(0))
         for c in range(1, GROUPS):
             query_total += outer(normed_ref[c], scaled(c))
-        split(query_total, q_keep, q_give, wide_q)
+        split(query_total, q_keep, q_give)
         q_move.start()
-
-    q_move = send(q_give, q_in, q_send.at[0], q_recv.at[0], core=sib)
+        line_q = scaled(0).astype(f32)
+        for c in range(1, GROUPS):
+            line_q += scaled(c).astype(f32)
+        sums_ref[pl.ds(16 + g, 1), 0:wide_q] = jnp.sum(line_q, axis=0, keepdims=True)
+
     sums_ref[...] = jnp.zeros_like(sums_ref)
     sums_ref[0:16] = sums_in[...]
-    line_q = scaled(0).astype(f32)
-    for c in range(1, GROUPS):
-        line_q += scaled(c).astype(f32)
-    sums_ref[pl.ds(16 + g, 1), 0:wide_q] = jnp.sum(line_q, axis=0, keepdims=True)
     wg_kv[...] = jnp.zeros_like(wg_kv)
 
     def q_slot(z):
@@ -1093,10 +1146,21 @@
         begin(b_slot(z), b_slot(z), fy_send.at[step], fy_recv.at[step], r=far_r)
         begin(b_slot(z), b_slot(z), fs_send.at[0, step], fs_recv.at[0, step], core=sib)
 
-    def spread_far(z, step):
-        what = big_ref.at[core, far_r, z]
+    def spread_far(step):
+        what = big_ref.at[core, far_r, nearest(g, step)]
         arrived(what, fy_send.at[step], fy_recv.at[step], x)
         begin(what, what, fs_send.at[1, step], fs_recv.at[1, step], core=sib)
+
+    def on_ring_b(step):
+        spread_b(ring_b.step(step), step)
+
+    def on_ring_q(step):
+        z = ring_q.step(step)
+        begin(q_slot(z), q_slot(z), qs_send.at[step], qs_recv.at[step], core=sib)
+
+    def on_ring_v(step):
+        z = ring_v.step(step)
+        begin(v_slot(z), v_slot(z), vs_send.at[step], vs_recv.at[step], core=sib)
 
     chain_a = Chain(g, x, total_a, part_a, inward_a, outward_a, ca_send, ca_recv)
     chain_b = Chain(g, x, total_b, by_sum, inward_b, outward_b, cb_send, cb_recv)
@@ -1139,81 +1203,96 @@
         wg_kv[...] += outer(normed_ref[c], both)
         sums_ref[pl.ds(16 + g, 1), wide_q : wide_q + 2 * HW] += jnp.sum(both.astype(f32), axis=0, keepdims=True)
 
-    by_sum[...] = bundle_ref[...].astype(f32) + by_in[...].astype(f32)
+    for load in loads[:4]:
+        load.wait()
+    own_up = pl.ds(pl.multiple_of(96 + 48 * x, 48), 48)
+    their_up = pl.ds(pl.multiple_of(96 + 48 * other, 48), 48)
+    for z in range(GROUPS):
+        pair = kept[z].astype(f32) + over[z].astype(f32)
+        by_sum[z, 0:96] = pair[0:96]
+        by_sum[z, own_up] = pair[96:144]
+        by_sum[z, 192:UNIT] = pair[144:KEPT]
+        by_sum[z, their_up] = near[48 * z : 48 * z + 48].astype(f32) + far[z].astype(f32)
+    pl.when(at_end)(lambda: steps(chain_b, 0, 1, 2))
     on_sibling(0)
     go_first(0)
     on_sibling(1)
     go_first(1)
-    pl.when(at_end)(lambda: steps(chain_b, 0, 1, 2))
     on_sibling(2)
     on_sibling(3)
+    pl.when(between)(lambda: steps(chain_b, 0))
     query_grad()
-    pl.when(between)(lambda: steps(chain_b, 0))
     on_first(0)
     on_first(1)
     go_first(2)
     go_first(3)
+    pl.when(between)(lambda: steps(chain_b, 1, 2))
     settled(q_move)
     q_pass[...] = (q_keep[other] + q_in[other].astype(f32)).astype(bf16)
     q_across = begin(q_pass, q_x, q_send.at[1], q_recv.at[1], x=other)
+    loads[6].wait()
     on_second(0)
     on_second(1)
-    pl.when(at_end)(lambda: steps(chain_a, 0, 1))
-    pl.when(between)(lambda: steps(chain_b, 1, 2))
+    pl.when(at_end)(lambda: steps(chain_a, 0))
+    chain_b.step(g)
+    unit[...] = total_b[...].astype(bf16)
+    store(unit, b_slot(g), l_sem.at[0])
+    ring_b.start()
+    spread_b(g, 0)
+    pl.when(at_end)(lambda: steps(chain_a, 1))
     on_first(2)
     on_first(3)
-    chain_b.step(g)
-    unit[...] = total_b[...].astype(bf16)
-    up_rows = 96 + 48 * other
-    begin(unit.at[pl.ds(up_rows, 48)], big_ref.at[core, r, g, pl.ds(96 + 48 * x, 48)], u_send.at[0], u_recv.at[0], x=other)
-    copies = [
-        pltpu.make_async_copy(unit.at[pl.ds(0, 96)], big_ref.at[core, r, g, pl.ds(0, 96)], l_sem.at[1]),
-        pltpu.make_async_copy(
-            unit.at[pl.ds(96 + 48 * x, 48)], big_ref.at[core, r, g, pl.ds(96 + 48 * x, 48)], l_sem.at[2]
-        ),
-        pltpu.make_async_copy(unit.at[pl.ds(192, 24)], big_ref.at[core, r, g, pl.ds(192, 24)], l_sem.at[3]),
-    ]
-    for copy in copies:
-        copy.start()
     q_across.wait_recv()
     q_sum[...] = (q_keep[x] + q_in[x].astype(f32) + q_x[...].astype(f32)).astype(bf16)
     q_over = begin(q_sum, q_y, q_send.at[2], q_recv.at[2], r=far_r)
+    pl.when(between)(lambda: steps(chain_a, 0))
     on_second(2)
     on_second(3)
     pl.when(at_end)(lambda: steps(chain_a, 2))
-    split(wg_kv, v_keep, v_give, 2 * HW)
+    split(wg_kv, v_keep, v_give)
     v_move = begin(v_give, v_in, v_send.at[0], v_recv.at[0], core=sib)
-    for copy in copies:
-        copy.wait()
-    arrived(big_ref.at[core, r, g, pl.ds(up_rows, 48)], u_send.at[0], u_recv.at[0], x)
-    ring_b.start()
-    spread_b(g, 0)
-    v_move.wait_recv()
-    v_pass[...] = (v_keep[other] + v_in[other].astype(f32)).astype(bf16)
-    v_across = begin(v_pass, v_x, v_send.at[1], v_recv.at[1], x=other)
-    pl.when(between)(lambda: steps(chain_a, 0))
+    s_sib = begin(sums_ref, sums_got.at[0], s_send.at[0], s_recv.at[0], core=sib)
+    spread_far(0)
     settled(q_over)
     q_sum[...] = (q_sum[...].astype(f32) + q_y[...].astype(f32)).astype(bf16)
     store(q_sum, q_slot(g), l_sem.at[0])
     ring_q.start()
     begin(q_slot(g), q_slot(g), qs_send.at[0], qs_recv.at[0], core=sib)
+    on_ring_b(1)
+    v_move.wait_recv()
+    v_pass[...] = (v_keep[other] + v_in[other].astype(f32)).astype(bf16)
+    v_across = begin(v_pass, v_x, v_send.at[1], v_recv.at[1], x=other)
+    settled(s_sib)
+    sums_ref[...] += sums_got[0]
+    s_x = begin(sums_ref, sums_got.at[1], s_send.at[1], s_recv.at[1], x=other)
+    pl.when(between)(lambda: steps(chain_a, 1))
     v_across.wait_recv()
     v_sum[...] = (v_keep[x] + v_in[x].astype(f32) + v_x[...].astype(f32)).astype(bf16)
     v_over = begin(v_sum, v_y, v_send.at[2], v_recv.at[2], r=far_r)
-    spread_far(g, 0)
-    pl.when(between)(lambda: steps(chain_a, 1, 2))
+    settled(s_x)
+    sums_ref[...] += sums_got[1]
+    s_y = begin(sums_ref, sums_got.at[2], s_send.at[2], s_recv.at[2], r=far_r)
+    on_ring_b(2)
+    pl.when(between)(lambda: steps(chain_a, 2))
     settled(v_over)
     v_sum[...] = (v_sum[...].astype(f32) + v_y[...].astype(f32)).astype(bf16)
     store(v_sum, v_slot(g), l_sem.at[0])
     ring_v.start()
     begin(v_slot(g), v_slot(g), vs_send.at[0], vs_recv.at[0], core=sib)
-    spread_b(ring_b.step(1), 1)
-    z = ring_q.step(1)
-    begin(q_slot(z), q_slot(z), qs_send.at[1], qs_recv.at[1], core=sib)
-    z = ring_v.step(1)
-    begin(v_slot(z), v_slot(z), vs_send.at[1], vs_recv.at[1], core=sib)
+    settled(s_y)
+    sums_ref[...] += sums_got[2]
+    for away in range(1, GROUPS):
+        begin(
+            sums_ref, sums_got.at[2 + away], s_send.at[2 + away], s_recv.at[2 + away],
+            g=lax.rem(g + away, GROUPS),
+        )
+    spread_far(1)
+    on_ring_q(1)
+    on_ring_b(3)
     chain_a.step(g)
 
+    loads[7].wait()
+    loads[8].wait()
     grad_first = total_a[...]
     values = tokens_ref[...].astype(f32)
     mean = jnp.mean(values, axis=-1, keepdims=True)
@@ -1223,39 +1302,32 @@
     pulled = grad_first * small_ref[0:1]
     inward = pulled - jnp.mean(pulled, axis=-1, keepdims=True) - n1 * jnp.mean(pulled * n1, axis=-1, keepdims=True)
     tokens_grad_ref[...] = mgrad_ref[...] + inward * scale
-    sums_ref[0:1] = jnp.sum(grad_first * n1, axis=0, keepdims=True)
-    sums_ref[1:2] = jnp.sum(grad_first, axis=0, keepdims=True)
-    s_sib = begin(sums_ref, sums_got.at[0], s_send.at[0], s_recv.at[0], core=sib)
-
-    settled(s_sib)
-    sums_ref[...] += sums_got[0]
-    s_x = begin(sums_ref, sums_got.at[1], s_send.at[1], s_recv.at[1], x=other)
-    spread_b(ring_b.step(2), 2)
-    spread_far(nearest(g, 1), 1)
-    settled(s_x)
-    sums_ref[...] += sums_got[1]
-    s_y = begin(sums_ref, sums_got.at[2], s_send.at[2], s_recv.at[2], r=far_r)
-    z = ring_q.step(2)
-    begin(q_slot(z), q_slot(z), qs_send.at[2], qs_recv.at[2], core=sib)
-    z = ring_v.step(2)
-    begin(v_slot(z), v_slot(z), vs_send.at[2], vs_recv.at[2], core=sib)
-    settled(s_y)
-    sums_ref[...] += sums_got[2]
+    late[...] = jnp.zeros_like(late)
+    late[0:1] = jnp.sum(grad_first * n1, axis=0, keepdims=True)
+    late[1:2] = jnp.sum(grad_first, axis=0, keepdims=True)
+    for step in range(len(AROUND)):
+        begin(late, late_got.at[step], t_send.at[step], t_recv.at[step], **neighbour(r, core, x, step))
+    on_ring_v(1)
+    on_ring_q(2)
+    on_ring_q(3)
+    spread_far(2)
+    on_ring_v(2)
+    late_sum[...] = late[...]
+    for step in range(len(AROUND)):
+        arrived(late_got.at[step], t_send.at[step], t_recv.at[step], x)
+        late_sum[...] += late_got[step]
+    first_z = len(AROUND) - 1
     for away in range(1, GROUPS):
         begin(
-            sums_ref, sums_got.at[2 + away], s_send.at[2 + away], s_recv.at[2 + away],
+            late_sum, late_got.at[first_z + away], t_send.at[first_z + away], t_recv.at[first_z + away],
             g=lax.rem(g + away, GROUPS),
         )
-    spread_b(ring_b.step(3), 3)
-    spread_far(nearest(g, 2), 2)
-    z = ring_q.step(3)
-    begin(q_slot(z), q_slot(z), qs_send.at[3], qs_recv.at[3], core=sib)
-    z = ring_v.step(3)
-    begin(v_slot(z), v_slot(z), vs_send.at[3], vs_recv.at[3], core=sib)
-    spread_far(nearest(g, 3), 3)
+    on_ring_v(3)
+    spread_far(3)
 
     for away in range(1, GROUPS):
         arrived(sums_got.at[2 + away], s_send.at[2 + away], s_recv.at[2 + away], x)
+        arrived(late_got.at[first_z + away], t_send.at[first_z + away], t_recv.at[first_z + away], x)
     for step in range(GROUPS):
         z = nearest(g, step)
         arrived(qout_ref.at[sib, z], qs_send.at[step], qs_recv.at[step], x)
@@ -1267,9 +1339,11 @@
     for item in (chain_a, chain_b, ring_q, ring_v, ring_b):
         item.finish()
     sums_ref[...] += sums_got[3] + sums_got[4] + sums_got[5]
-
-
-def scatter(dkv, dq, normed, wfull, tokens, mgrad, small, bundle, over, sums):
+    total = late_sum[...] + late_got[first_z + 1] + late_got[first_z + 2] + late_got[first_z + 3]
+    sums_ref[0:2] = total[0:2]
+
+
+def scatter(dkv, dq, normed, wfull, tokens, mgrad, small, keep, over, near, far, sums):
     rows, width = tokens.shape
     fourth = width // 4
     dma = pltpu.SemaphoreType.DMA
@@ -1295,9 +1369,15 @@
             jax.ShapeDtypeStruct((2, GROUPS, fourth, wide_v), bf16),
             jax.ShapeDtypeStruct((24, width), f32),
         ),
-        in_specs=[in_hbm()] + [whole_vmem()] * 9,
+        in_specs=[anywhere()] * 10 + [whole_vmem()] * 2,
         out_specs=(whole_vmem(), anywhere(), anywhere(), anywhere(), whole_vmem()),
         scratch_shapes=[
+            *[
+                pltpu.VMEM(item.shape, item.dtype)
+                for item in (dq, normed, wfull, tokens, mgrad, keep, over)
+            ],
+            pltpu.VMEM((48 * GROUPS, width), bf16),
+            pltpu.VMEM(far.shape, bf16),
             pltpu.VMEM((GROUPS, 4, *kv_block), bf16),
             pltpu.VMEM((GROUPS, 4, *kv_block), bf16),
             pltpu.VMEM((GROUPS, 2, *kv_block), f32),
@@ -1318,19 +1398,23 @@
             *weight_scratch(wide_q),
             *weight_scratch(wide_v),
             pltpu.VMEM((6, 24, width), f32),
+            pltpu.VMEM((8, width), f32),
+            pltpu.VMEM((8, width), f32),
+            pltpu.VMEM((len(AROUND) + GROUPS - 1, 8, width), f32),
+            dma((9,)),
             dma((GROUPS, 4)), dma((GROUPS, 4)), dma((GROUPS, 4)), dma((GROUPS,)), dma((GROUPS,)), dma((GROUPS,)), dma((GROUPS,)),
             dma((GROUPS,)), dma((2, GROUPS)),
-            dma((GROUPS,)), dma((2, GROUPS)), dma((1,)), dma((1,)), dma((2,)), dma((GROUPS,)), dma((GROUPS,)),
+            dma((GROUPS,)), dma((2, GROUPS)), dma((2,)), dma((GROUPS,)), dma((GROUPS,)),
             dma((GROUPS,)), dma((GROUPS,)), dma((2, GROUPS)), dma((2, GROUPS)),
             dma((3,)), dma((3,)), dma((2,)), dma((GROUPS,)), dma((GROUPS,)), dma((GROUPS,)), dma((GROUPS,)),
             dma((3,)), dma((3,)), dma((2,)), dma((GROUPS,)), dma((GROUPS,)), dma((GROUPS,)), dma((GROUPS,)),
-            dma((6,)), dma((6,)), dma((4,)),
+            dma((6,)), dma((6,)), dma((10,)), dma((10,)), dma((1,)),
         ],
         compiler_params=pltpu.CompilerParams(
-            collective_id=2, has_side_effects=True, vmem_limit_bytes=51 << 20
+            collective_id=2, has_side_effects=True, vmem_limit_bytes=54 << 20
         ),
         name="scatter",
-    )(dkv, dq, normed, wfull, tokens, mgrad, small, bundle, over, sums)
+    )(dkv, dq, normed, wfull, tokens, mgrad, keep, over, near, far, small, sums)
 
 
 def pack_kv(key_part, value_part):
@@ -1465,18 +1549,19 @@
     up_other = lax.ppermute(up_other, "x", swap)
     cot_x = lax.ppermute(cot_x, "x", swap)
     out_t, kept, lse = attend_forward(deal, doc_lengths, q, kv)
-    base, y_give, grad_middle, grad_t, bundle, over, sums = dense(
+    base, x_give, grad_middle, grad_t, kept_part, over, far, sums = dense(
         out_t, tokens, cotangent, cot_x, small, wo, up_columns(x), up_other, down_weight
     )
-    y_got = lax.ppermute(y_give, "x", swap)
     over = lax.ppermute(over, "r", swap)
+    x_got = lax.ppermute(x_give, "x", swap)
+    far = lax.ppermute(far, ("r", "x"), ((0, 3), (1, 2), (2, 1), (3, 0)))
     dq, dkv = attend_backward(deal, doc_lengths, q, kv, lse, grad_t, kept)
     dkv = dkv.reshape(-1, GROUPS, rows, 2 * HW)
     if wide:
         dkv = lax.psum_scatter(dkv, "s", scatter_dimension=0, tiled=True)
     dq = dq.reshape(GROUPS, rows, 2 * BLK)
     grad_tokens, big, query_own, kv_own, sums = scatter(
-        dkv, dq, normed, wfull, tokens, grad_middle, small, bundle, over, sums
+        dkv, dq, normed, wfull, tokens, grad_middle, small, kept_part, over, x_got, far, sums
     )
     if wide:
         big, query_own, kv_own, sums = (
@@ -1486,7 +1571,7 @@
     (
         up_own, down_own, wo_own, query_own, key_own, value_own,
         low_gain, low_shift, query_sum, value_sum, out_sum, high_gain, high_shift, up_sum, down_sum, result,
-    ) = lay_out(big.reshape(2, PARTS, UNIT, width), query_own, kv_own, sums, base, y_got)
+    ) = lay_out(big.reshape(2, PARTS, UNIT, width), query_own, kv_own, sums, base, x_got)
 
     def flat(item):
         return item.reshape(-1, width)

time: 307 us -> 297 us (0.967); the launches traced: 303 us -> 299 us
  Pallas kernels: 286 us -> 281 us
    pallas_call x1, Pallas kernels: 117 us -> 104 us  [scatter(): pl.pallas_call(scatter_kernel, out_shape=(jax.ShapeDtypeStruct(full, f32)...]
    pallas_call x1, Pallas kernels: 19.5 us -> 23.4 us  [attend_forward(): pl.pallas_call(forward_kernel, out_shape=(jax.ShapeDtypeStruct((slots, HW...]
    pallas_call x1, Pallas kernels: 30.8 us -> 34.1 us  [attend_backward(): pl.pallas_call(backward_kernel, out_shape=(jax.ShapeDtypeStruct((slots, B...]
    unnamed x35 -> x39, local copies, waits for them, and re-layouts: 10.9 us -> 10.1 us
  transfers between devices with their start and end apart: 4 -> 5, of which waited for: 0 -> 0; matrix products, arithmetic and copies ran while one was open for 0% -> 0% of each run, Pallas kernels for 55% -> 19%
where the time goes in v3:
time: 297 us; the launch traced here: 299 us
  Pallas kernels  281 us (95%)
  local copies, waits for them, and re-layouts  11.5 us (4%)
  starting transfers between devices  5.6 us (2%)
    pallas_call x1, Pallas kernels, scatter(): pl.pallas_call(scatter_kernel, out_shape=(jax.ShapeDtypeStruct(full, f32)...  104 us
    pallas_call x1, Pallas kernels, gather(): pl.pallas_call(gather_kernel, out_shape=(jax.ShapeDtypeStruct((8, GROUPS,...  61.3 us
    pallas_call x1, Pallas kernels, dense(): pl.pallas_call(dense_kernel, out_shape=(jax.ShapeDtypeStruct(full, f32),...  47.6 us
    pallas_call x1, Pallas kernels, attend_backward(): pl.pallas_call(backward_kernel, out_shape=(jax.ShapeDtypeStruct((slots, B...  34.1 us
    pallas_call x1, Pallas kernels, attend_forward(): pl.pallas_call(forward_kernel, out_shape=(jax.ShapeDtypeStruct((slots, HW...  23.4 us
    pallas_call x1, Pallas kernels, lay_out(): pl.pallas_call(layout_kernel, grid=(PARTS,), out_shape=(jax.ShapeDtypeStr...  10.5 us
    unnamed x39, local copies, waits for them, and re-layouts  10.1 us
  transfers between devices with their start and end apart: 5, of which 0 were waited for; matrix products, arithmetic and copies ran while one was open for 0% of the time, Pallas kernels for 19%

profile of v3, /device:TPU:0, one launch (start us, length us, event | category | flops | bytes accessed | tf_op | source)
XLA Modules:
  0.0 298.7 jit_solution(5389614575325438673)
XLA Ops:
  0.7 1.4 constant_dynamic-slice_fusion
  2.1 61.3 %gather.1 = (bf16[8,4,256,384]{3,2,1,0:T(8,128)(2,1)}, bf16[4,256,256]{2,1,0:T(8,128)(2,1)}, bf16[4,256,768]{2,1,0:T(8,128)(2,1)}, f32[16,768]{1,0:T(8,128)}, bf...) custom-call(bf16[256,768]{1,0:T(8,128)(2,1)} %tokens_any.1, bf16[384,768]{1,0:T(8,128)(2,1)} %query_any.1, ...), custom_call_target="tpu_custom_call" | custom-call | tf_op jit(solution)/shard_map/gather/pallas_call | solution.py:593
  63.4 1.6 collective-permute-start.1
  65.0 0.6 collective-permute-start
  65.5 2.8 copy-done
  68.3 1.0 copy-done.3
  69.4 23.4 %attend_forward.1 = (bf16[8,192,128]{2,1,0:T(8,128)(2,1)S(1)}, f32[8,192,128]{2,1,0:T(8,128)S(1)}, f32[8,1,384]{2,1,0:T(1,128)S(1)}) custom-call(s32[64]{0:T(128)S(1)} %copy-done.13, s32[4]{0:T(128)S(1)} %copy-done.14, bf16[8,128,256]{2,1,0:T(8,128)(2,1)S(1)} %bitcast.12, bf16[64,128,384]{2,1,0:T(8,128)(2,1)S(1)} %bitcast.11), custom_call_target="tpu_custom_call" | custom-call | tf_op jit(solution)/shard_map/attend_forward/pallas_call | solution.py:182
  92.8 47.6 %dense.1 = (f32[256,768]{1,0:T(8,128)S(1)}, bf16[448,768]{1,0:T(8,128)(2,1)S(1)}, f32[256,768]{1,0:T(8,128)S(1)}, bf16[8,192,128]{2,1,0:T(8,128)(2,1)S(1)}, bf16...) custom-call(bf16[8,192,128]{2,1,0:T(8,128)(2,1)S(1)} %get-tuple-elem, ...), custom_call_target="tpu_custom_call" | custom-call | tf_op jit(solution)/shard_map/dense/pallas_call | solution.py:891
  140.4 0.0 copy-start.6
  140.4 1.0 copy-done.6
  141.4 0.9 copy-done.7
  142.3 0.9 copy-done.8
  143.1 0.6 copy-done.12
  143.8 0.1 collective-permute-start.3
  143.9 3.4 %collective-permute-start.4 = (bf16[4,48,768]{2,1,0:T(8,128)(2,1)S(1)}, bf16[4,48,768]{2,1,0:T(8,128)(2,1)S(1)}, u32[]{:S(2)}, u32[]{:S(2)}) collective-permute-start(bf16[4,48,768]{2,1,0:T(8,128)(2,1)S(1)} %get-tuple-element.79), channel_id=1, source_target_pairs={{0,5},{1,4},{4,1},{5,0},{2,7},{3,6},{6,3},{7,2},{8,13},{9,12},{12,... | collective-permute-start | bytes 884744 | tf_op jit(solution)/shard_map/ppermute | solution.py:1557
  147.3 34.1 %attend_backward.1 = (bf16[8,128,256]{2,1,0:T(8,128)(2,1)S(1)}, bf16[64,128,384]{2,1,0:T(8,128)(2,1)}) custom-call(s32[64]{0:T(128)S(1)} %copy-done.13, s32[4]{0:T(128)S(1)} %copy-done.14, bf16[8,128,256]{2,1,0:T(8,128)(2,1)S(1)} %bitcast.13, bf16[64,128,384]{2,1,0:T(8,128)(2,1)} %bitcast.10, f32[8,1,384]{2,1,0:T(1,128)S(1)} %get-tuple-element.63.lse_ref, ...), custom_call_target="tpu_custom_call" | custom-call | tf_op jit(solution)/shard_map/attend_backward/pallas_call | solution.py:309
  181.4 0.0 copy-start.9
  181.4 0.8 copy-done.9
  182.2 0.7 copy-done.18
  182.9 0.2 copy-done.15
  183.2 0.3 copy-done.16
  183.5 103.8 %scatter.1 = (f32[256,768]{1,0:T(8,128)}, bf16[2,2,4,216,768]{4,3,2,1,0:T(8,128)(2,1)}, bf16[2,4,192,256]{3,2,1,0:T(8,128)(2,1)}, bf16[2,4,192,384]{3,2,1,0:T(8,128)(2,1)}, f32[24,768]{1,0:T(8,128)}) custom-call(bf16[8,4,256,384]{3,2,1,0:T(8,128)(2,1)} %bitcast.15, bf16[4,256,256]{2,1,0:T(8,128)(2,1)} %bitcast.14, ...), custom_call_target="tpu_custom_call" | custom-call | tf_op jit(solution)/shard_map/scatter/pallas_call | solution.py:1363
  287.3 10.5 %lay_out.1 = (f32[384,3072]{1,0:T(8,128)}, f32[2,768,768]{2,1,0:T(8,128)}, f32[2,192,768]{2,1,0:T(8,128)}, f32[2,192,768]{2,1,0:T(8,128)}, f32[2,192,768]{2,1,0:...) custom-call(bf16[2,8,216,768]{3,2,1,0:T(8,128)(2,1)} %bitcast.16, ...), custom_call_target="tpu_custom_call" | custom-call | tf_op jit(solution)/shard_map/lay_out/pallas_call | solution.py:1485
  297.8 0.9 copy.37
  (32 shorter events, 0.1 us)
Async XLA Ops:
  0.7 64.3 %copy-start.10 = (bf16[256,768]{1,0:T(8,128)(2,1)S(1)}, bf16[256,768]{1,0:T(8,128)(2,1)}, u32[]{:S(2)}) copy-start(bf16[256,768]{1,0:T(8,128)(2,1)} %cot_ref.1) | copy-start | bytes 1179652
  0.7 64.9 %copy-start.13 = (s32[64]{0:T(128)S(1)}, s32[64]{0:T(128)}, u32[]{:S(2)}) copy-start(s32[64]{0:T(128)} %deal_ref.3) | copy-start | bytes 772
  0.7 64.9 %copy-start.14 = (s32[4]{0:T(128)S(1)}, s32[4]{0:T(128)}, u32[]{:S(2)}) copy-start(s32[4]{0:T(128)} %lengths_ref.3) | copy-start | bytes 52
  63.4 29.4 %collective-permute-start.1 = (bf16[384,768]{1,0:T(8,128)(2,1)S(1)}, bf16[384,768]{1,0:T(8,128)(2,1)S(1)}, u32[]{:S(2)}, u32[]{:S(2)}) collective-permute-start(bf16[384,768]{1,0:T(8,128)(2,1)S(1)} %get-tuple-element.68), channel_id=1, source_target_pairs={{0,1},{1,0},{2,3},{3,2},{4,5},{5,4},{6,7},{7,6},{8,9},{9,8},{10,11... | collective-permute-start | bytes 1769480 | tf_op jit(solution)/shard_map/ppermute | solution.py:1549
  65.0 27.8 %collective-permute-start = (bf16[256,768]{1,0:T(8,128)(2,1)S(1)}, bf16[256,768]{1,0:T(8,128)(2,1)S(1)}, u32[]{:S(2)}, u32[]{:S(2)}) collective-permute-start(bf16[256,768]{1,0:T(8,128)(2,1)S(1)} %copy-done.10), channel_id=1, source_target_pairs={{0,1},{1,0},{2,3},{3,2},{4,5},{5,4},{6,7},{7,6},{8,9},{9,8},{10,11... | collective-permute-start | bytes 1179656 | tf_op jit(solution)/shard_map/ppermute | solution.py:1550
  65.5 2.8 copy-start
  68.3 1.0 copy-start.3
  69.4 23.4 %copy-start.1 = (bf16[256,768]{1,0:T(8,128)(2,1)S(1)}, bf16[256,768]{1,0:T(8,128)(2,1)}, u32[]{:S(2)}) copy-start(bf16[256,768]{1,0:T(8,128)(2,1)} %tokens_any.1) | copy-start | bytes 1179652
  69.4 23.4 %copy-start.2 = (bf16[1536,768]{1,0:T(8,128)(2,1)S(1)}, bf16[1536,768]{1,0:T(8,128)(2,1)}, u32[]{:S(2)}) copy-start(bf16[1536,768]{1,0:T(8,128)(2,1)} %down_any.1) | copy-start | bytes 7077892
  69.4 23.4 %copy-start.5 = (bf16[768,768]{1,0:T(8,128)(2,1)S(1)}, bf16[768,768]{1,0:T(8,128)(2,1)}, u32[]{:S(2)}) copy-start(bf16[768,768]{1,0:T(8,128)(2,1)} %get-tuple-element.67.wo_ref) | copy-start | bytes 3538948
  69.4 23.4 %copy-start.11 = (f32[16,768]{1,0:T(8,128)S(1)}, f32[16,768]{1,0:T(8,128)}, u32[]{:S(2)}) copy-start(f32[16,768]{1,0:T(8,128)} %get-tuple-element.66.small_ref) | copy-start | bytes 147460
  92.8 54.4 %copy-start.4 = (bf16[4,256,256]{2,1,0:T(8,128)(2,1)S(1)}, bf16[4,256,256]{2,1,0:T(8,128)(2,1)}, u32[]{:S(2)}) copy-start(bf16[4,256,256]{2,1,0:T(8,128)(2,1)} %get-tuple-element.60) | copy-start | bytes 1572868
  140.4 1.0 copy-start.6
  141.4 0.9 copy-start.7
  142.3 0.9 copy-start.8
  143.1 0.6 copy-start.12
  143.8 38.5 %collective-permute-start.2 = (bf16[4,168,768]{2,1,0:T(8,128)(2,1)S(1)}, bf16[4,168,768]{2,1,0:T(8,128)(2,1)S(1)}, u32[]{:S(2)}, u32[]{:S(2)}) collective-permute-start(bf16[4,168,768]{2,1,0:T(8,128)(2,1)S(1)} %get-tuple-element.77), channel_id=1, source_target_pairs={{0,4},{4,0},{1,5},{5,1},{2,6},{6,2},{3,7},{7,3},{8,12},{12,8},{9,1... | collective-permute-start | bytes 3096584 | tf_op jit(solution)/shard_map/ppermute | solution.py:1555
  143.8 38.4 %collective-permute-start.3 = (bf16[448,768]{1,0:T(8,128)(2,1)S(1)}, bf16[448,768]{1,0:T(8,128)(2,1)S(1)}, u32[]{:S(2)}, u32[]{:S(2)}) collective-permute-start(bf16[448,768]{1,0:T(8,128)(2,1)S(1)} %get-tuple-element.78), channel_id=1, source_target_pairs={{0,1},{1,0},{2,3},{3,2},{4,5},{5,4},{6,7},{7,6},{8,9},{9,8},{10,11... | collective-permute-start | bytes 2064392 | tf_op jit(solution)/shard_map/ppermute | solution.py:1556
  143.9 38.3 %collective-permute-start.4 = (bf16[4,48,768]{2,1,0:T(8,128)(2,1)S(1)}, bf16[4,48,768]{2,1,0:T(8,128)(2,1)S(1)}, u32[]{:S(2)}, u32[]{:S(2)}) collective-permute-start(bf16[4,48,768]{2,1,0:T(8,128)(2,1)S(1)} %get-tuple-element.79), channel_id=1, source_target_pairs={{0,5},{1,4},{4,1},{5,0},{2,7},{3,6},{6,3},{7,2},{8,13},{9,12},{12,... | collective-permute-start | bytes 884744 | tf_op jit(solution)/shard_map/ppermute | solution.py:1557
  181.4 0.8 copy-start.9
  182.2 0.7 copy-start.18
  182.2 1.0 copy-start.15
  182.2 1.3 copy-start.16
  287.3 10.6 %copy-start.17 = (f32[256,768]{1,0:T(8,128)S(1)}, f32[256,768]{1,0:T(8,128)}, u32[]{:S(2)}) copy-start(f32[256,768]{1,0:T(8,128)} %get-tuple-element.123) | copy-start | bytes 2359300

commit v4 on v3

--- a/solution.py
+++ b/solution.py
@@ -119,38 +119,35 @@
 def forward_kernel(
     deal_ref, lengths_ref, q_ref, kv_ref,
     out_ref, wide_ref, lse_ref,
-    where_ref, text_ref, low_ref, high_ref, first_ref, vt_ref, acc_ref,
+    where_ref, text_ref, low_ref, high_ref, first_ref, acc_ref,
 ):
     survey(deal_ref, lengths_ref, where_ref, text_ref, low_ref, high_ref, first_ref)
-    chunks = kv_ref.shape[0] // 2
-
-    def turn(chunk, _):
-        vt_ref[chunk] = load_chunk(kv_ref, where_ref, chunk)[:, BLK : 3 * BLK].T[DH:]
-        return _
-
-    lax.fori_loop(0, chunks, turn, 0)
-
-    def one_slot(slot, _):
+
+    def one_slot(slot, kept):
         wide_q = spread_heads_t(q_ref[slot].T[:HW], K_ORDER)
         first = first_ref[slot]
         own = text_ref[slot] * BLK + lax.broadcasted_iota(jnp.int32, (1, BLK), 1)
+        last_first = jnp.max(first)
         acc_ref[...] = jnp.zeros_like(acc_ref)
 
-        def step(chunk, carry):
+        def step(double, carry):
             top, total = carry
-            part = load_chunk(kv_ref, where_ref, chunk)
-            scores = dot(part[:, : 2 * BLK], wide_q)
-            scores = jnp.where(visible(chunk, first, own), scores, MASKED)
+            scores = []
+            for part in range(2):
+                keys = load_chunk(kv_ref, where_ref, 2 * double + part)[:, : 2 * BLK]
+                scores.append(jnp.where(visible(2 * double + part, first, own), dot(keys, wide_q), MASKED))
+            scores = jnp.concatenate(scores, axis=0)
             fresh = jnp.maximum(top, jnp.max(scores, axis=0, keepdims=True))
             expo = jnp.exp(scores - fresh)
             shrink = jnp.exp(top - fresh)
             total = total * shrink + jnp.sum(expo, axis=0, keepdims=True)
-            acc_ref[...] = acc_ref[...] * shrink + dot(vt_ref[chunk], expo.astype(bf16))
+            vals = jnp.concatenate([load_chunk(kv_ref, where_ref, 2 * double + part)[:, BLK:] for part in range(2)], axis=0)
+            acc_ref[...] = acc_ref[...] * shrink + outer(vals, expo.astype(bf16))
             return fresh, total
 
         top, total = lax.fori_loop(
-            low_ref[slot],
-            high_ref[slot] + 1,
+            low_ref[slot] // 2,
+            high_ref[slot] // 2 + 1,
             step,
             (jnp.full((1, WIDE), MASKED, f32), jnp.zeros((1, WIDE), f32)),
         )
@@ -158,12 +155,12 @@
         scaled = acc_ref[...] / total
         pieces = []
         for head in range(PER):
-            row = DH * V_ORDER.index(head) - DH
+            row = DH * V_ORDER.index(head)
             pieces.append(scaled[row : row + DH, BLK * head : BLK * head + BLK])
-        kept = jnp.concatenate(pieces, axis=0)
-        wide_ref[slot] = kept
-        out_ref[slot] = kept.astype(bf16)
-        return _
+        whole = jnp.concatenate(pieces, axis=0)
+        wide_ref[slot] = whole
+        out_ref[slot] = whole.astype(bf16)
+        return kept
 
     lax.fori_loop(0, q_ref.shape[0], one_slot, 0)
 
@@ -190,8 +187,7 @@
         out_specs=(whole_vmem(),) * 3,
         scratch_shapes=[
             *survey_scratch(blocks),
-            pltpu.VMEM((blocks // 2, HW, CHUNK), bf16),
-            pltpu.VMEM((HW, WIDE), f32),
+            pltpu.VMEM((2 * BLK, WIDE), f32),
         ],
         compiler_params=pltpu.CompilerParams(vmem_limit_bytes=(6 << 20) + kv.size // 5 * 16),
         name="attend_forward",
@@ -201,7 +197,7 @@
 def backward_kernel(
     deal_ref, lengths_ref, q_ref, kv_ref, lse_ref, do_ref, wide_ref,
     dq_ref, dkv_ref, where_ref, text_ref, low_ref, high_ref, first_ref, qt_ref, qm_ref, dot_ref, dom_ref, delta_ref, acc_ref, dk_acc, dv_acc,
-    packed_ref, out_sem,
+    packed_ref, count_ref, list_ref, out_sem,
 ):
     survey(deal_ref, lengths_ref, where_ref, text_ref, low_ref, high_ref, first_ref)
     slots = q_ref.shape[0]
@@ -237,6 +233,24 @@
 
     lax.fori_loop(0, slots, ready, 0)
 
+    def clear(chunk, kept):
+        count_ref[chunk] = 0
+        return kept
+
+    lax.fori_loop(0, chunks, clear, 0)
+
+    def enlist(slot, kept):
+        def seen(chunk, kept):
+            count = count_ref[chunk]
+            list_ref[chunk * slots + count] = slot
+            count_ref[chunk] = count + 1
+            return kept
+
+        lax.fori_loop(low_ref[slot], high_ref[slot] + 1, seen, 0)
+        return kept
+
+    lax.fori_loop(0, slots, enlist, 0)
+
     def written(chunk, i):
         return pltpu.make_async_copy(
             packed_ref.at[chunk % 2, i], dkv_ref.at[where_ref[2 * chunk + i]], out_sem.at[chunk % 2, i]
@@ -250,23 +264,23 @@
         dk_acc[...] = jnp.zeros_like(dk_acc)
         dv_acc[...] = jnp.zeros_like(dv_acc)
 
-        def one_slot(slot, kept):
-            @pl.when((low_ref[slot] <= chunk) & (chunk <= high_ref[slot]))
-            def _():
-                own = text_ref[slot] * BLK + lax.broadcasted_iota(jnp.int32, (1, BLK), 1)
-                scores = dot(keys, qt_ref[slot])
-                probs = jnp.where(
-                    visible(chunk, first_ref[slot], own), jnp.exp(scores - lse_ref[slot]), 0.0
-                )
-                dprobs = dot(vals, dot_ref[slot])
-                dscores = (probs * (dprobs - delta_ref[slot])).astype(bf16)
-                dv_acc[...] += dot(probs.astype(bf16), dom_ref[slot])
-                dk_acc[...] += dot(dscores, qm_ref[slot])
-                acc_ref[slot] += dot(keys_t, dscores)
-
+        def one_slot(i, kept):
+            for half in range(2):
+                attend(list_ref[chunk * slots + 2 * i + half])
             return kept
 
-        lax.fori_loop(0, slots, one_slot, 0)
+        def attend(slot):
+            own = text_ref[slot] * BLK + lax.broadcasted_iota(jnp.int32, (1, BLK), 1)
+            scores = dot(keys, qt_ref[slot])
+            dprobs = dot(vals, dot_ref[slot])
+            probs = jnp.where(visible(chunk, first_ref[slot], own), jnp.exp(scores - lse_ref[slot]), 0.0)
+            dscores = (probs * (dprobs - delta_ref[slot])).astype(bf16)
+            dv_acc[...] += dot(probs.astype(bf16), dom_ref[slot])
+            dk_acc[...] += dot(dscores, qm_ref[slot])
+            acc_ref[slot] += dot(keys_t, dscores)
+
+        lax.fori_loop(0, count_ref[chunk] // 2, one_slot, 0)
+        pl.when(count_ref[chunk] % 2 == 1)(lambda: attend(list_ref[chunk * slots + count_ref[chunk] - 1]))
         packed = jnp.concatenate(
             [
                 dk_acc[:, :BLK],
@@ -325,6 +339,8 @@
             pltpu.VMEM((CHUNK, 2 * BLK), f32),
             pltpu.VMEM((CHUNK, 2 * BLK), f32),
             pltpu.VMEM((2, 2, BLK, 2 * HW), bf16),
+            pltpu.SMEM((kv.shape[0] // 2,), jnp.int32),
+            pltpu.SMEM((kv.shape[0] // 2 * slots,), jnp.int32),
             pltpu.SemaphoreType.DMA((2, 2)),
         ],
         compiler_params=pltpu.CompilerParams(

time: 297 us -> 286 us (0.963)
  Pallas kernels: 281 us -> 271 us
    pallas_call x1, Pallas kernels: 47.6 us -> 39.3 us  [dense(): pl.pallas_call(dense_kernel, out_shape=(jax.ShapeDtypeStruct(full, f32),...]
    pallas_call x1, Pallas kernels: 104 us -> 98.8 us  [scatter(): pl.pallas_call(scatter_kernel, out_shape=(jax.ShapeDtypeStruct(full, f32)...]
    pallas_call x1, Pallas kernels: 34.1 us -> 38.4 us  [attend_backward(): pl.pallas_call(backward_kernel, out_shape=(jax.ShapeDtypeStruct((slots, B...]
  transfers between devices with their start and end apart: 5 -> 5, of which waited for: 0 -> 0; matrix products, arithmetic and copies ran while one was open for 0% -> 0% of each run, Pallas kernels for 19% -> 21%
where the time goes in v4:
time: 286 us; the launch traced here: 289 us
  Pallas kernels  271 us (95%)
  local copies, waits for them, and re-layouts  11.5 us (4%)
  starting transfers between devices  5.6 us (2%)
    pallas_call x1, Pallas kernels, scatter(): pl.pallas_call(scatter_kernel, out_shape=(jax.ShapeDtypeStruct(full, f32)...  98.8 us
    pallas_call x1, Pallas kernels, gather(): pl.pallas_call(gather_kernel, out_shape=(jax.ShapeDtypeStruct((8, GROUPS,...  61.3 us
    pallas_call x1, Pallas kernels, dense(): pl.pallas_call(dense_kernel, out_shape=(jax.ShapeDtypeStruct(full, f32),...  39.3 us
    pallas_call x1, Pallas kernels, attend_backward(): pl.pallas_call(backward_kernel, out_shape=(jax.ShapeDtypeStruct((slots, B...  38.4 us
    pallas_call x1, Pallas kernels, attend_forward(): pl.pallas_call(forward_kernel, out_shape=(jax.ShapeDtypeStruct((slots, HW...  22.6 us
    pallas_call x1, Pallas kernels, lay_out(): pl.pallas_call(layout_kernel, grid=(PARTS,), out_shape=(jax.ShapeDtypeStr...  10.5 us
    unnamed x39, local copies, waits for them, and re-layouts  10.1 us
  transfers between devices with their start and end apart: 5, of which 0 were waited for; matrix products, arithmetic and copies ran while one was open for 0% of the time, Pallas kernels for 21%

profile of v4, /device:TPU:0, one launch (start us, length us, event | category | flops | bytes accessed | tf_op | source)
XLA Modules:
  0.0 289.1 jit_solution(16684778775539149265)
XLA Ops:
  0.7 1.4 constant_dynamic-slice_fusion
  2.1 61.3 %gather.1 = (bf16[8,4,256,384]{3,2,1,0:T(8,128)(2,1)}, bf16[4,256,256]{2,1,0:T(8,128)(2,1)}, bf16[4,256,768]{2,1,0:T(8,128)(2,1)}, f32[16,768]{1,0:T(8,128)}, bf...) custom-call(bf16[256,768]{1,0:T(8,128)(2,1)} %tokens_any.1, bf16[384,768]{1,0:T(8,128)(2,1)} %query_any.1, ...), custom_call_target="tpu_custom_call" | custom-call | tf_op jit(solution)/shard_map/gather/pallas_call | solution.py:609
  63.4 1.6 collective-permute-start.1
  65.0 0.6 collective-permute-start
  65.5 2.8 copy-done
  68.3 1.0 copy-done.3
  69.4 22.6 %attend_forward.1 = (bf16[8,192,128]{2,1,0:T(8,128)(2,1)S(1)}, f32[8,192,128]{2,1,0:T(8,128)S(1)}, f32[8,1,384]{2,1,0:T(1,128)S(1)}) custom-call(s32[64]{0:T(128)S(1)} %copy-done.13, s32[4]{0:T(128)S(1)} %copy-done.14, bf16[8,128,256]{2,1,0:T(8,128)(2,1)S(1)} %bitcast.12, bf16[64,128,384]{2,1,0:T(8,128)(2,1)S(1)} %bitcast.11), custom_call_target="tpu_custom_call" | custom-call | tf_op jit(solution)/shard_map/attend_forward/pallas_call | solution.py:179
  92.1 39.3 %dense.1 = (f32[256,768]{1,0:T(8,128)S(1)}, bf16[448,768]{1,0:T(8,128)(2,1)S(1)}, f32[256,768]{1,0:T(8,128)S(1)}, bf16[8,192,128]{2,1,0:T(8,128)(2,1)S(1)}, bf16...) custom-call(bf16[8,192,128]{2,1,0:T(8,128)(2,1)S(1)} %get-tuple-elem, ...), custom_call_target="tpu_custom_call" | custom-call | tf_op jit(solution)/shard_map/dense/pallas_call | solution.py:907
  131.5 1.0 copy-done.6
  132.4 0.9 copy-done.7
  133.3 0.9 copy-done.8
  134.2 0.6 copy-done.12
  134.8 0.3 collective-permute-start.2
  135.1 1.6 collective-permute-start.3
  136.7 1.6 collective-permute-start.4
  138.3 38.4 %attend_backward.1 = (bf16[8,128,256]{2,1,0:T(8,128)(2,1)S(1)}, bf16[64,128,384]{2,1,0:T(8,128)(2,1)}) custom-call(s32[64]{0:T(128)S(1)} %copy-done.13, s32[4]{0:T(128)S(1)} %copy-done.14, bf16[8,128,256]{2,1,0:T(8,128)(2,1)S(1)} %bitcast.13, bf16[64,128,384]{2,1,0:T(8,128)(2,1)} %bitcast.10, f32[8,1,384]{2,1,0:T(1,128)S(1)} %get-tuple-element.63.lse_ref, ...), custom_call_target="tpu_custom_call" | custom-call | tf_op jit(solution)/shard_map/attend_backward/pallas_call | solution.py:323
  176.7 0.0 copy-start.9
  176.8 0.8 copy-done.9
  177.6 0.7 copy-done.18
  178.3 0.2 copy-done.15
  178.5 0.3 copy-done.16
  178.8 98.8 %scatter.1 = (f32[256,768]{1,0:T(8,128)}, bf16[2,2,4,216,768]{4,3,2,1,0:T(8,128)(2,1)}, bf16[2,4,192,256]{3,2,1,0:T(8,128)(2,1)}, bf16[2,4,192,384]{3,2,1,0:T(8,128)(2,1)}, f32[24,768]{1,0:T(8,128)}) custom-call(bf16[8,4,256,384]{3,2,1,0:T(8,128)(2,1)} %bitcast.15, bf16[4,256,256]{2,1,0:T(8,128)(2,1)} %bitcast.14, ...), custom_call_target="tpu_custom_call" | custom-call | tf_op jit(solution)/shard_map/scatter/pallas_call | solution.py:1379
  277.7 10.5 %lay_out.1 = (f32[384,3072]{1,0:T(8,128)}, f32[2,768,768]{2,1,0:T(8,128)}, f32[2,192,768]{2,1,0:T(8,128)}, f32[2,192,768]{2,1,0:T(8,128)}, f32[2,192,768]{2,1,0:...) custom-call(bf16[2,8,216,768]{3,2,1,0:T(8,128)(2,1)} %bitcast.16, ...), custom_call_target="tpu_custom_call" | custom-call | tf_op jit(solution)/shard_map/lay_out/pallas_call | solution.py:1501
  288.2 0.9 copy.37
  (32 shorter events, 0.1 us)
Async XLA Ops:
  0.7 64.3 %copy-start.10 = (bf16[256,768]{1,0:T(8,128)(2,1)S(1)}, bf16[256,768]{1,0:T(8,128)(2,1)}, u32[]{:S(2)}) copy-start(bf16[256,768]{1,0:T(8,128)(2,1)} %cot_ref.1) | copy-start | bytes 1179652
  0.7 64.9 %copy-start.13 = (s32[64]{0:T(128)S(1)}, s32[64]{0:T(128)}, u32[]{:S(2)}) copy-start(s32[64]{0:T(128)} %deal_ref.3) | copy-start | bytes 772
  0.7 64.9 %copy-start.14 = (s32[4]{0:T(128)S(1)}, s32[4]{0:T(128)}, u32[]{:S(2)}) copy-start(s32[4]{0:T(128)} %lengths_ref.3) | copy-start | bytes 52
  63.4 28.6 %collective-permute-start.1 = (bf16[384,768]{1,0:T(8,128)(2,1)S(1)}, bf16[384,768]{1,0:T(8,128)(2,1)S(1)}, u32[]{:S(2)}, u32[]{:S(2)}) collective-permute-start(bf16[384,768]{1,0:T(8,128)(2,1)S(1)} %get-tuple-element.68), channel_id=1, source_target_pairs={{0,1},{1,0},{2,3},{3,2},{4,5},{5,4},{6,7},{7,6},{8,9},{9,8},{10,11... | collective-permute-start | bytes 1769480 | tf_op jit(solution)/shard_map/ppermute | solution.py:1565
  65.0 27.1 %collective-permute-start = (bf16[256,768]{1,0:T(8,128)(2,1)S(1)}, bf16[256,768]{1,0:T(8,128)(2,1)S(1)}, u32[]{:S(2)}, u32[]{:S(2)}) collective-permute-start(bf16[256,768]{1,0:T(8,128)(2,1)S(1)} %copy-done.10), channel_id=1, source_target_pairs={{0,1},{1,0},{2,3},{3,2},{4,5},{5,4},{6,7},{7,6},{8,9},{9,8},{10,11... | collective-permute-start | bytes 1179656 | tf_op jit(solution)/shard_map/ppermute | solution.py:1566
  65.5 2.8 copy-start
  68.3 1.0 copy-start.3
  69.4 22.7 %copy-start.1 = (bf16[256,768]{1,0:T(8,128)(2,1)S(1)}, bf16[256,768]{1,0:T(8,128)(2,1)}, u32[]{:S(2)}) copy-start(bf16[256,768]{1,0:T(8,128)(2,1)} %tokens_any.1) | copy-start | bytes 1179652
  69.4 22.7 %copy-start.2 = (bf16[1536,768]{1,0:T(8,128)(2,1)S(1)}, bf16[1536,768]{1,0:T(8,128)(2,1)}, u32[]{:S(2)}) copy-start(bf16[1536,768]{1,0:T(8,128)(2,1)} %down_any.1) | copy-start | bytes 7077892
  69.4 22.7 %copy-start.5 = (bf16[768,768]{1,0:T(8,128)(2,1)S(1)}, bf16[768,768]{1,0:T(8,128)(2,1)}, u32[]{:S(2)}) copy-start(bf16[768,768]{1,0:T(8,128)(2,1)} %get-tuple-element.67.wo_ref) | copy-start | bytes 3538948
  69.4 22.7 %copy-start.11 = (f32[16,768]{1,0:T(8,128)S(1)}, f32[16,768]{1,0:T(8,128)}, u32[]{:S(2)}) copy-start(f32[16,768]{1,0:T(8,128)} %get-tuple-element.66.small_ref) | copy-start | bytes 147460
  92.1 46.2 %copy-start.4 = (bf16[4,256,256]{2,1,0:T(8,128)(2,1)S(1)}, bf16[4,256,256]{2,1,0:T(8,128)(2,1)}, u32[]{:S(2)}) copy-start(bf16[4,256,256]{2,1,0:T(8,128)(2,1)} %get-tuple-element.60) | copy-start | bytes 1572868
  131.5 1.0 copy-start.6
  132.4 0.9 copy-start.7
  133.3 0.9 copy-start.8
  134.2 0.6 copy-start.12
  134.8 42.8 %collective-permute-start.2 = (bf16[4,168,768]{2,1,0:T(8,128)(2,1)S(1)}, bf16[4,168,768]{2,1,0:T(8,128)(2,1)S(1)}, u32[]{:S(2)}, u32[]{:S(2)}) collective-permute-start(bf16[4,168,768]{2,1,0:T(8,128)(2,1)S(1)} %get-tuple-element.77), channel_id=1, source_target_pairs={{0,4},{4,0},{1,5},{5,1},{2,6},{6,2},{3,7},{7,3},{8,12},{12,8},{9,1... | collective-permute-start | bytes 3096584 | tf_op jit(solution)/shard_map/ppermute | solution.py:1571
  135.1 42.4 %collective-permute-start.3 = (bf16[448,768]{1,0:T(8,128)(2,1)S(1)}, bf16[448,768]{1,0:T(8,128)(2,1)S(1)}, u32[]{:S(2)}, u32[]{:S(2)}) collective-permute-start(bf16[448,768]{1,0:T(8,128)(2,1)S(1)} %get-tuple-element.78), channel_id=1, source_target_pairs={{0,1},{1,0},{2,3},{3,2},{4,5},{5,4},{6,7},{7,6},{8,9},{9,8},{10,11... | collective-permute-start | bytes 2064392 | tf_op jit(solution)/shard_map/ppermute | solution.py:1572
  136.7 40.8 %collective-permute-start.4 = (bf16[4,48,768]{2,1,0:T(8,128)(2,1)S(1)}, bf16[4,48,768]{2,1,0:T(8,128)(2,1)S(1)}, u32[]{:S(2)}, u32[]{:S(2)}) collective-permute-start(bf16[4,48,768]{2,1,0:T(8,128)(2,1)S(1)} %get-tuple-element.79), channel_id=1, source_target_pairs={{0,5},{1,4},{4,1},{5,0},{2,7},{3,6},{6,3},{7,2},{8,13},{9,12},{12,... | collective-permute-start | bytes 884744 | tf_op jit(solution)/shard_map/ppermute | solution.py:1573
  176.7 0.8 copy-start.9
  177.5 0.7 copy-start.18
  177.5 1.0 copy-start.15
  177.6 1.3 copy-start.16
  277.7 10.6 %copy-start.17 = (f32[256,768]{1,0:T(8,128)S(1)}, f32[256,768]{1,0:T(8,128)}, u32[]{:S(2)}) copy-start(f32[256,768]{1,0:T(8,128)} %get-tuple-element.123) | copy-start | bytes 2359300

commit v5 on v4

--- a/solution.py
+++ b/solution.py
@@ -16,6 +16,7 @@
 HW = PER * DH
 WIDE = PER * BLK
 CHUNK = 2 * BLK
+DEPTH = 8
 EPS = 1e-05
 SCALE = 0.125
 MASKED = -1e30
@@ -253,7 +254,7 @@
 
     def written(chunk, i):
         return pltpu.make_async_copy(
-            packed_ref.at[chunk % 2, i], dkv_ref.at[where_ref[2 * chunk + i]], out_sem.at[chunk % 2, i]
+            packed_ref.at[chunk % DEPTH, i], dkv_ref.at[where_ref[2 * chunk + i]], out_sem.at[chunk % DEPTH, i]
         )
 
     def one_chunk(chunk, kept):
@@ -290,20 +291,20 @@
             axis=1,
         ).astype(bf16)
 
-        @pl.when(chunk >= 2)
+        @pl.when(chunk >= DEPTH)
         def _():
             for i in range(2):
-                written(chunk - 2, i).wait()
+                written(chunk - DEPTH, i).wait()
 
         for i in range(2):
-            packed_ref[chunk % 2, i] = packed[BLK * i : BLK * i + BLK]
+            packed_ref[chunk % DEPTH, i] = packed[BLK * i : BLK * i + BLK]
             written(chunk, i).start()
         return kept
 
     lax.fori_loop(0, chunks, one_chunk, 0)
-    for last in range(2):
+    for last in range(DEPTH):
         for i in range(2):
-            written(chunks - 2 + last, i).wait()
+            written(chunks - DEPTH + last, i).wait()
 
     def finish(slot, _):
         total = acc_ref[slot]
@@ -338,10 +339,10 @@
             pltpu.VMEM((slots, HW, WIDE), f32),
             pltpu.VMEM((CHUNK, 2 * BLK), f32),
             pltpu.VMEM((CHUNK, 2 * BLK), f32),
-            pltpu.VMEM((2, 2, BLK, 2 * HW), bf16),
+            pltpu.VMEM((DEPTH, 2, BLK, 2 * HW), bf16),
             pltpu.SMEM((kv.shape[0] // 2,), jnp.int32),
             pltpu.SMEM((kv.shape[0] // 2 * slots,), jnp.int32),
-            pltpu.SemaphoreType.DMA((2, 2)),
+            pltpu.SemaphoreType.DMA((DEPTH, 2)),
         ],
         compiler_params=pltpu.CompilerParams(
             vmem_limit_bytes=max(48 << 20, (17 << 20) + kv.size * 2)
@@ -466,12 +467,16 @@
         load.start()
     greet(g, r, core, x, False)
 
-    def along(source, away, sem):
-        return send(lined.at[source], lined.at[source], sem, z_recv.at[source], g=g + away)
+    def half_of(source, part):
+        return lined.at[source, pl.ds(BLK * part, BLK)]
+
+    def along(source, part, away, sem):
+        return send(half_of(source, part), half_of(source, part), sem, z_recv.at[source, part], g=g + away)
 
     lined[g] = tokens_ref[...]
-    pl.when(g > 0)(lambda: along(g, -1, z_own.at[0]).start())
-    pl.when(g < GROUPS - 1)(lambda: along(g, 1, z_own.at[1]).start())
+    for part in range(2):
+        pl.when(g > 0)(lambda: along(g, part, -1, z_own.at[0, part]).start())
+        pl.when(g < GROUPS - 1)(lambda: along(g, part, 1, z_own.at[1, part]).start())
 
     for load in loads:
         load.wait()
@@ -507,80 +512,128 @@
 
     own = seat(r, core, x)
 
-    def block(owner, source):
-        return kv_ref.at[owner, source]
-
-    def push(step, kind, what, **device):
-        copy = send(what[0], what[1], kv_send.at[kind, step], kv_recv.at[kind, step], **device)
-        copy.start()
-
-    def settle(step, kind, owner, source):
-        send(block(owner, source), block(owner, source), kv_send.at[kind, step], kv_recv.at[kind, step], x=other).wait_recv()
+    def span(step):
+        return (step, 0, rows) if step < GROUPS - 1 else (GROUPS - 1, BLK * (step - GROUPS + 1), BLK)
+
+    def block(owner, step):
+        nth, low, count = span(step)
+        return kv_ref.at[owner, nearest(g, nth), pl.ds(low, count)]
+
+    def made(step):
+        nth, low, count = span(step)
+        return kvs.at[nth, pl.ds(low, count)]
+
+    def push(step, kind, src, dst, **device):
+        send(src, dst, kv_send.at[kind, step], kv_recv.at[kind, step], **device).start()
+
+    def settle(step, kind, owner):
+        arrived(block(owner, step), kv_send.at[kind, step], kv_recv.at[kind, step], x)
 
     def forward(step):
-        source = nearest(g, step)
-        by_x = block(seat(r, core, other), source)
-        settle(step, 0, seat(r, core, other), source)
+        by_x = block(seat(r, core, other), step)
+        settle(step, 0, seat(r, core, other))
         if step % 2 == 0:
-            push(step, 3, (by_x, by_x), r=1 - r)
-        push(step, 4, (by_x, by_x), core=1 - core)
-        by_y = block(seat(1 - r, core, x), source)
-        settle(step, 1, seat(1 - r, core, x), source)
+            push(step, 3, by_x, by_x, r=1 - r)
+        push(step, 4, by_x, by_x, core=1 - core)
+        by_y = block(seat(1 - r, core, x), step)
+        settle(step, 1, seat(1 - r, core, x))
         if step % 2 == 1:
-            push(step, 3, (by_y, by_y), x=other)
-        push(step, 5, (by_y, by_y), core=1 - core)
+            push(step, 3, by_y, by_y, x=other)
+        push(step, 5, by_y, by_y, core=1 - core)
 
     def forward_far(step):
-        source = nearest(g, step)
-        far = block(seat(1 - r, core, other), source)
-        settle(step, 3, seat(1 - r, core, other), source)
-        push(step, 6, (far, far), core=1 - core)
-
-    for step in range(GROUPS):
-        source = nearest(g, step)
-        if step > 0:
-            send(lined.at[source], lined.at[source], z_send.at[source], z_recv.at[source], x=other).wait_recv()
-            pl.when((source < g) & (g < GROUPS - 1))(lambda: along(source, 1, z_send.at[source]).start())
-            pl.when((source > g) & (g > 0))(lambda: along(source, -1, z_send.at[source]).start())
-        values = lined[source].astype(f32)
+        far = block(seat(1 - r, core, other), step)
+        settle(step, 3, seat(1 - r, core, other))
+        push(step, 6, far, far, core=1 - core)
+
+    def take(nth, part):
+        source = nearest(g, nth)
+        arrived(half_of(source, part), z_send.at[source, part], z_recv.at[source, part], x)
+        pl.when((source < g) & (g < GROUPS - 1))(lambda: along(source, part, 1, z_send.at[source, part]).start())
+        pl.when((source > g) & (g > 0))(lambda: along(source, part, -1, z_send.at[source, part]).start())
+
+    def project(step):
+        nth, low, count = span(step)
+        source = nearest(g, nth)
+        taken = pl.ds(low, count)
+        values = lined[source, taken].astype(f32)
         normed = layer_norm(values, small_out[0:1], small_out[1:2]).astype(bf16)
-        normed_ref[source] = normed
+        normed_ref[source, taken] = normed
         both = dot(normed, wfull[...]) + small_out[12:13, : wfull.shape[1]]
-        q_ref[source] = (both[:, : 2 * BLK] * SCALE).astype(bf16)
-        kvs[step] = both[:, 2 * BLK :].astype(bf16)
-        here = (kvs.at[step], block(own, source))
-        push(step, 0, here, x=other)
-        push(step, 1, here, r=1 - r)
-        push(step, 2, here, core=1 - core)
-        pltpu.make_async_copy(kvs.at[step], block(own, source), kv_local.at[step]).start()
-        if step > 0:
-            forward(step - 1)
-        if step > 1:
-            forward_far(step - 2)
+        kvs[nth, taken] = both[:, 2 * BLK :].astype(bf16)
+        push(step, 0, made(step), block(own, step), x=other)
+        push(step, 1, made(step), block(own, step), r=1 - r)
+        push(step, 2, made(step), block(own, step), core=1 - core)
+        q_ref[source, taken] = (both[:, : 2 * BLK] * SCALE).astype(bf16)
+        pltpu.make_async_copy(made(step), block(own, step), kv_local.at[step]).start()
+
+    at_end = (g == 0) | (g == GROUPS - 1)
+    between = jnp.logical_not(at_end)
+    project(0)
+    take(1, 0)
+    take(1, 1)
+
+    @pl.when(between)
+    def _():
+        take(2, 0)
+        take(2, 1)
+
+    project(1)
+    forward(0)
+
+    @pl.when(at_end)
+    def _():
+        take(2, 0)
+        take(2, 1)
+
+    project(2)
+
+    @pl.when(at_end)
+    def _():
+        forward(1)
+        forward_far(0)
+
+    take(3, 0)
+    pl.when(between)(lambda: take(3, 1))
+    project(3)
+    pl.when(at_end)(lambda: take(3, 1))
+    project(4)
+
+    @pl.when(between)
+    def _():
+        forward(1)
+        forward_far(0)
+
     wo_x.wait_recv()
     wo_y.start()
     wo_s[0].start()
-    forward(GROUPS - 1)
-    forward_far(GROUPS - 2)
-    send(wo_rows(other, 1 - r), wo_rows(other, 1 - r), w_send.at[3], w_recv.at[3], r=1 - r).wait_recv()
+    forward(2)
+    forward_far(1)
+    forward(3)
+    forward_far(2)
+    forward(4)
+    forward_far(3)
+    arrived(wo_rows(other, 1 - r), w_send.at[3], w_recv.at[3], x)
     wo_s[1].start()
-    forward_far(GROUPS - 1)
-
-    for step in range(GROUPS):
-        source = nearest(g, step)
-        pltpu.make_async_copy(kvs.at[step], block(own, source), kv_local.at[step]).wait()
-        settle(step, 2, seat(r, 1 - core, x), source)
-        settle(step, 4, seat(r, 1 - core, other), source)
-        settle(step, 5, seat(1 - r, 1 - core, x), source)
-        settle(step, 6, seat(1 - r, 1 - core, other), source)
+    forward_far(4)
+
+    for step in range(GROUPS + 1):
+        pltpu.make_async_copy(made(step), block(own, step), kv_local.at[step]).wait()
+        settle(step, 2, seat(r, 1 - core, x))
+        settle(step, 4, seat(r, 1 - core, other))
+        settle(step, 5, seat(1 - r, 1 - core, x))
+        settle(step, 6, seat(1 - r, 1 - core, other))
         for kind in range(7):
-            send(kvs.at[step], block(own, source), kv_send.at[kind, step], kv_recv.at[kind, step], x=other).wait_send()
-    pl.when(g > 0)(lambda: along(g, -1, z_own.at[0]).wait_send())
-    pl.when(g < GROUPS - 1)(lambda: along(g, 1, z_own.at[1]).wait_send())
-    for step in range(1, GROUPS):
-        source = nearest(g, step)
-        passed = ((source < g) & (g < GROUPS - 1)) | ((source > g) & (g > 0))
-        pl.when(passed)(lambda: send(lined.at[source], lined.at[source], z_send.at[source], z_recv.at[source], x=other).wait_send())
+            left(made(step), kv_send.at[kind, step], kv_recv.at[kind, step], x)
+    for part in range(2):
+        pl.when(g > 0)(lambda: left(half_of(g, part), z_own.at[0, part], z_recv.at[g, part], x))
+        pl.when(g < GROUPS - 1)(lambda: left(half_of(g, part), z_own.at[1, part], z_recv.at[g, part], x))
+        for nth in range(1, GROUPS):
+            source = nearest(g, nth)
+            passed = ((source < g) & (g < GROUPS - 1)) | ((source > g) & (g > 0))
+            pl.when(passed)(
+                lambda: left(half_of(source, part), z_send.at[source, part], z_recv.at[source, part], x)
+            )
     small_move.wait_send()
     narrow_x.wait_send()
     narrow_s.wait_send()
@@ -625,8 +678,8 @@
             pltpu.VMEM(small, f32),
             pltpu.VMEM(small, f32),
             pltpu.VMEM((GROUPS, rows, 2 * HW), bf16),
-            dma((2,)), dma((GROUPS,)), dma((GROUPS,)), dma((2,)), dma((2,)), dma((2,)),
-            dma((7, GROUPS)), dma((7, GROUPS)), dma((GROUPS,)), dma((8,)), dma((8,)), dma((2,)), dma((3,)),
+            dma((2, 2)), dma((GROUPS, 2)), dma((GROUPS, 2)), dma((2,)), dma((2,)), dma((2,)),
+            dma((7, GROUPS + 1)), dma((7, GROUPS + 1)), dma((GROUPS + 1,)), dma((8,)), dma((8,)), dma((2,)), dma((3,)),
         ],
         compiler_params=pltpu.CompilerParams(
             collective_id=0, has_side_effects=True, vmem_limit_bytes=60 << 20

time: 286 us -> 282 us (0.986); the launches traced: 289 us -> 280 us
  Pallas kernels: 271 us -> 262 us
    pallas_call x1, Pallas kernels: 38.4 us -> 31.9 us  [attend_backward(): pl.pallas_call(backward_kernel, out_shape=(jax.ShapeDtypeStruct((slots, B...]
    pallas_call x1, Pallas kernels: 61.3 us -> 55 us  [gather(): pl.pallas_call(gather_kernel, out_shape=(jax.ShapeDtypeStruct((8, GROUPS,...]
    pallas_call x1, Pallas kernels: 39.3 us -> 43.2 us  [dense(): pl.pallas_call(dense_kernel, out_shape=(jax.ShapeDtypeStruct(full, f32),...]
  transfers between devices with their start and end apart: 5 -> 5, of which waited for: 0 -> 0; matrix products, arithmetic and copies ran while one was open for 0% -> 0% of each run, Pallas kernels for 21% -> 19%
where the time goes in v5:
time: 282 us; the launch traced here: 280 us
  Pallas kernels  262 us (93%)
  local copies, waits for them, and re-layouts  11.5 us (4%)
  starting transfers between devices  5.59 us (2%)
    pallas_call x1, Pallas kernels, scatter(): pl.pallas_call(scatter_kernel, out_shape=(jax.ShapeDtypeStruct(full, f32)...  101 us
    pallas_call x1, Pallas kernels, gather(): pl.pallas_call(gather_kernel, out_shape=(jax.ShapeDtypeStruct((8, GROUPS,...  55 us
    pallas_call x1, Pallas kernels, dense(): pl.pallas_call(dense_kernel, out_shape=(jax.ShapeDtypeStruct(full, f32),...  43.2 us
    pallas_call x1, Pallas kernels, attend_backward(): pl.pallas_call(backward_kernel, out_shape=(jax.ShapeDtypeStruct((slots, B...  31.9 us
    pallas_call x1, Pallas kernels, attend_forward(): pl.pallas_call(forward_kernel, out_shape=(jax.ShapeDtypeStruct((slots, HW...  20 us
    pallas_call x1, Pallas kernels, lay_out(): pl.pallas_call(layout_kernel, grid=(PARTS,), out_shape=(jax.ShapeDtypeStr...  10.5 us
    unnamed x39, local copies, waits for them, and re-layouts  10.1 us
  transfers between devices with their start and end apart: 5, of which 0 were waited for; matrix products, arithmetic and copies ran while one was open for 0% of the time, Pallas kernels for 19%

profile of v5, /device:TPU:0, one launch (start us, length us, event | category | flops | bytes accessed | tf_op | source)
XLA Modules:
  0.0 279.6 jit_solution(14897019688002122811)
XLA Ops:
  0.7 1.4 constant_dynamic-slice_fusion
  2.1 55.0 %gather.1 = (bf16[8,4,256,384]{3,2,1,0:T(8,128)(2,1)}, bf16[4,256,256]{2,1,0:T(8,128)(2,1)}, bf16[4,256,768]{2,1,0:T(8,128)(2,1)}, f32[16,768]{1,0:T(8,128)}, bf...) custom-call(bf16[256,768]{1,0:T(8,128)(2,1)} %tokens_any.1, bf16[384,768]{1,0:T(8,128)(2,1)} %query_any.1, ...), custom_call_target="tpu_custom_call" | custom-call | tf_op jit(solution)/shard_map/gather/pallas_call | solution.py:662
  57.1 0.6 collective-permute-start.1
  57.7 1.5 collective-permute-start
  59.2 2.8 copy-done
  62.0 1.0 copy-done.3
  63.0 20.0 %attend_forward.1 = (bf16[8,192,128]{2,1,0:T(8,128)(2,1)S(1)}, f32[8,192,128]{2,1,0:T(8,128)S(1)}, f32[8,1,384]{2,1,0:T(1,128)S(1)}) custom-call(s32[64]{0:T(128)S(1)} %copy-done.13, s32[4]{0:T(128)S(1)} %copy-done.14, bf16[8,128,256]{2,1,0:T(8,128)(2,1)S(1)} %bitcast.12, bf16[64,128,384]{2,1,0:T(8,128)(2,1)S(1)} %bitcast.11), custom_call_target="tpu_custom_call" | custom-call | tf_op jit(solution)/shard_map/attend_forward/pallas_call | solution.py:180
  83.2 43.2 %dense.1 = (f32[256,768]{1,0:T(8,128)S(1)}, bf16[448,768]{1,0:T(8,128)(2,1)S(1)}, f32[256,768]{1,0:T(8,128)S(1)}, bf16[8,192,128]{2,1,0:T(8,128)(2,1)S(1)}, bf16...) custom-call(bf16[8,192,128]{2,1,0:T(8,128)(2,1)S(1)} %get-tuple-elem, ...), custom_call_target="tpu_custom_call" | custom-call | tf_op jit(solution)/shard_map/dense/pallas_call | solution.py:960
  126.4 1.0 copy-done.6
  127.4 0.9 copy-done.7
  128.2 0.9 copy-done.8
  129.1 0.6 copy-done.12
  129.7 1.7 collective-permute-start.2
  131.4 0.6 collective-permute-start.3
  132.0 1.2 collective-permute-start.4
  133.2 31.9 %attend_backward.1 = (bf16[8,128,256]{2,1,0:T(8,128)(2,1)S(1)}, bf16[64,128,384]{2,1,0:T(8,128)(2,1)}) custom-call(s32[64]{0:T(128)S(1)} %copy-done.13, s32[4]{0:T(128)S(1)} %copy-done.14, bf16[8,128,256]{2,1,0:T(8,128)(2,1)S(1)} %bitcast.13, bf16[64,128,384]{2,1,0:T(8,128)(2,1)} %bitcast.10, f32[8,1,384]{2,1,0:T(1,128)S(1)} %get-tuple-element.63.lse_ref, ...), custom_call_target="tpu_custom_call" | custom-call | tf_op jit(solution)/shard_map/attend_backward/pallas_call | solution.py:324
  165.2 0.0 copy-start.9
  165.2 0.8 copy-done.9
  166.0 0.7 copy-done.18
  166.7 0.2 copy-done.15
  166.9 0.3 copy-done.16
  167.3 100.9 %scatter.1 = (f32[256,768]{1,0:T(8,128)}, bf16[2,2,4,216,768]{4,3,2,1,0:T(8,128)(2,1)}, bf16[2,4,192,256]{3,2,1,0:T(8,128)(2,1)}, bf16[2,4,192,384]{3,2,1,0:T(8,128)(2,1)}, f32[24,768]{1,0:T(8,128)}) custom-call(bf16[8,4,256,384]{3,2,1,0:T(8,128)(2,1)} %bitcast.15, bf16[4,256,256]{2,1,0:T(8,128)(2,1)} %bitcast.14, ...), custom_call_target="tpu_custom_call" | custom-call | tf_op jit(solution)/shard_map/scatter/pallas_call | solution.py:1432
  268.2 10.5 %lay_out.1 = (f32[384,3072]{1,0:T(8,128)}, f32[2,768,768]{2,1,0:T(8,128)}, f32[2,192,768]{2,1,0:T(8,128)}, f32[2,192,768]{2,1,0:T(8,128)}, f32[2,192,768]{2,1,0:...) custom-call(bf16[2,8,216,768]{3,2,1,0:T(8,128)(2,1)} %bitcast.16, ...), custom_call_target="tpu_custom_call" | custom-call | tf_op jit(solution)/shard_map/lay_out/pallas_call | solution.py:1554
  278.8 0.9 copy.37
  (32 shorter events, 0.1 us)
Async XLA Ops:
  0.7 57.0 %copy-start.10 = (bf16[256,768]{1,0:T(8,128)(2,1)S(1)}, bf16[256,768]{1,0:T(8,128)(2,1)}, u32[]{:S(2)}) copy-start(bf16[256,768]{1,0:T(8,128)(2,1)} %cot_ref.1) | copy-start | bytes 1179652
  0.7 58.5 %copy-start.13 = (s32[64]{0:T(128)S(1)}, s32[64]{0:T(128)}, u32[]{:S(2)}) copy-start(s32[64]{0:T(128)} %deal_ref.3) | copy-start | bytes 772
  0.7 58.5 %copy-start.14 = (s32[4]{0:T(128)S(1)}, s32[4]{0:T(128)}, u32[]{:S(2)}) copy-start(s32[4]{0:T(128)} %lengths_ref.3) | copy-start | bytes 52
  57.1 26.0 %collective-permute-start.1 = (bf16[384,768]{1,0:T(8,128)(2,1)S(1)}, bf16[384,768]{1,0:T(8,128)(2,1)S(1)}, u32[]{:S(2)}, u32[]{:S(2)}) collective-permute-start(bf16[384,768]{1,0:T(8,128)(2,1)S(1)} %get-tuple-element.68), channel_id=1, source_target_pairs={{0,1},{1,0},{2,3},{3,2},{4,5},{5,4},{6,7},{7,6},{8,9},{9,8},{10,11... | collective-permute-start | bytes 1769480 | tf_op jit(solution)/shard_map/ppermute | solution.py:1618
  57.7 25.4 %collective-permute-start = (bf16[256,768]{1,0:T(8,128)(2,1)S(1)}, bf16[256,768]{1,0:T(8,128)(2,1)S(1)}, u32[]{:S(2)}, u32[]{:S(2)}) collective-permute-start(bf16[256,768]{1,0:T(8,128)(2,1)S(1)} %copy-done.10), channel_id=1, source_target_pairs={{0,1},{1,0},{2,3},{3,2},{4,5},{5,4},{6,7},{7,6},{8,9},{9,8},{10,11... | collective-permute-start | bytes 1179656 | tf_op jit(solution)/shard_map/ppermute | solution.py:1619
  59.2 2.8 copy-start
  62.0 1.0 copy-start.3
  63.0 20.1 %copy-start.1 = (bf16[256,768]{1,0:T(8,128)(2,1)S(1)}, bf16[256,768]{1,0:T(8,128)(2,1)}, u32[]{:S(2)}) copy-start(bf16[256,768]{1,0:T(8,128)(2,1)} %tokens_any.1) | copy-start | bytes 1179652
  63.0 20.1 %copy-start.2 = (bf16[1536,768]{1,0:T(8,128)(2,1)S(1)}, bf16[1536,768]{1,0:T(8,128)(2,1)}, u32[]{:S(2)}) copy-start(bf16[1536,768]{1,0:T(8,128)(2,1)} %down_any.1) | copy-start | bytes 7077892
  63.0 20.1 %copy-start.5 = (bf16[768,768]{1,0:T(8,128)(2,1)S(1)}, bf16[768,768]{1,0:T(8,128)(2,1)}, u32[]{:S(2)}) copy-start(bf16[768,768]{1,0:T(8,128)(2,1)} %get-tuple-element.67.wo_ref) | copy-start | bytes 3538948
  63.0 20.1 %copy-start.11 = (f32[16,768]{1,0:T(8,128)S(1)}, f32[16,768]{1,0:T(8,128)}, u32[]{:S(2)}) copy-start(f32[16,768]{1,0:T(8,128)} %get-tuple-element.66.small_ref) | copy-start | bytes 147460
  83.1 50.1 %copy-start.4 = (bf16[4,256,256]{2,1,0:T(8,128)(2,1)S(1)}, bf16[4,256,256]{2,1,0:T(8,128)(2,1)}, u32[]{:S(2)}) copy-start(bf16[4,256,256]{2,1,0:T(8,128)(2,1)} %get-tuple-element.60) | copy-start | bytes 1572868
  126.4 1.0 copy-start.6
  127.4 0.9 copy-start.7
  128.2 0.9 copy-start.8
  129.1 0.6 copy-start.12
  129.7 36.3 %collective-permute-start.2 = (bf16[4,168,768]{2,1,0:T(8,128)(2,1)S(1)}, bf16[4,168,768]{2,1,0:T(8,128)(2,1)S(1)}, u32[]{:S(2)}, u32[]{:S(2)}) collective-permute-start(bf16[4,168,768]{2,1,0:T(8,128)(2,1)S(1)} %get-tuple-element.77), channel_id=1, source_target_pairs={{0,4},{4,0},{1,5},{5,1},{2,6},{6,2},{3,7},{7,3},{8,12},{12,8},{9,1... | collective-permute-start | bytes 3096584 | tf_op jit(solution)/shard_map/ppermute | solution.py:1624
  131.4 34.6 %collective-permute-start.3 = (bf16[448,768]{1,0:T(8,128)(2,1)S(1)}, bf16[448,768]{1,0:T(8,128)(2,1)S(1)}, u32[]{:S(2)}, u32[]{:S(2)}) collective-permute-start(bf16[448,768]{1,0:T(8,128)(2,1)S(1)} %get-tuple-element.78), channel_id=1, source_target_pairs={{0,1},{1,0},{2,3},{3,2},{4,5},{5,4},{6,7},{7,6},{8,9},{9,8},{10,11... | collective-permute-start | bytes 2064392 | tf_op jit(solution)/shard_map/ppermute | solution.py:1625
  132.0 34.0 %collective-permute-start.4 = (bf16[4,48,768]{2,1,0:T(8,128)(2,1)S(1)}, bf16[4,48,768]{2,1,0:T(8,128)(2,1)S(1)}, u32[]{:S(2)}, u32[]{:S(2)}) collective-permute-start(bf16[4,48,768]{2,1,0:T(8,128)(2,1)S(1)} %get-tuple-element.79), channel_id=1, source_target_pairs={{0,5},{1,4},{4,1},{5,0},{2,7},{3,6},{6,3},{7,2},{8,13},{9,12},{12,... | collective-permute-start | bytes 884744 | tf_op jit(solution)/shard_map/ppermute | solution.py:1626
  165.2 0.8 copy-start.9
  166.0 0.7 copy-start.18
  166.0 1.0 copy-start.15
  166.0 1.3 copy-start.16
  268.2 10.6 %copy-start.17 = (f32[256,768]{1,0:T(8,128)S(1)}, f32[256,768]{1,0:T(8,128)}, u32[]{:S(2)}) copy-start(f32[256,768]{1,0:T(8,128)} %get-tuple-element.123) | copy-start | bytes 2359300

commit v6 on v5

--- a/solution.py
+++ b/solution.py
@@ -345,7 +345,7 @@
             pltpu.SemaphoreType.DMA((DEPTH, 2)),
         ],
         compiler_params=pltpu.CompilerParams(
-            vmem_limit_bytes=max(48 << 20, (17 << 20) + kv.size * 2)
+            vmem_limit_bytes=max(30 << 20, (17 << 20) + kv.size * 2)
         ),
         name="attend_backward",
     )(deal, lengths, q, kv, lse, grad_t, wide)
@@ -682,7 +682,7 @@
             dma((7, GROUPS + 1)), dma((7, GROUPS + 1)), dma((GROUPS + 1,)), dma((8,)), dma((8,)), dma((2,)), dma((3,)),
         ],
         compiler_params=pltpu.CompilerParams(
-            collective_id=0, has_side_effects=True, vmem_limit_bytes=60 << 20
+            collective_id=0, has_side_effects=True, vmem_limit_bytes=16 << 20
         ),
         name="gather",
     )(tokens, query, key, value, wo, *lines)
@@ -1605,9 +1605,14 @@
     def up_columns(owner):
         return lax.dynamic_slice_in_dim(up_weight, (2 * owner + core) * width, width, 1)
 
+    def stay(*items):
+        return tuple(pltpu.with_memory_space_constraint(item, pltpu.HBM) for item in items)
+
     kv, q, normed, small, wfull, wo = gather(
-        tokens, query_weight, key_weight, value_weight, output_weight,
-        first_gain, first_shift, output_bias, second_gain, second_shift, down_bias, query_bias, value_bias, up_bias,
+        *stay(
+            tokens, query_weight, key_weight, value_weight, output_weight,
+            first_gain, first_shift, output_bias, second_gain, second_shift, down_bias, query_bias, value_bias, up_bias,
+        )
     )
     wide = blocks > 8 * 2 * GROUPS
     if wide:
@@ -1630,7 +1635,7 @@
         dkv = lax.psum_scatter(dkv, "s", scatter_dimension=0, tiled=True)
     dq = dq.reshape(GROUPS, rows, 2 * BLK)
     grad_tokens, big, query_own, kv_own, sums = scatter(
-        dkv, dq, normed, wfull, tokens, grad_middle, small, kept_part, over, x_got, far, sums
+        *stay(dkv, dq, normed, wfull, tokens, grad_middle), small, *stay(kept_part, over, x_got, far), sums
     )
     if wide:
         big, query_own, kv_own, sums = (
@@ -1640,7 +1645,7 @@
     (
         up_own, down_own, wo_own, query_own, key_own, value_own,
         low_gain, low_shift, query_sum, value_sum, out_sum, high_gain, high_shift, up_sum, down_sum, result,
-    ) = lay_out(big.reshape(2, PARTS, UNIT, width), query_own, kv_own, sums, base, x_got)
+    ) = lay_out(big.reshape(2, PARTS, UNIT, width), query_own, kv_own, sums, *stay(base, x_got))
 
     def flat(item):
         return item.reshape(-1, width)

time: 282 us -> 282 us (level); the launches traced: 280 us -> 282 us
  Pallas kernels: 262 us -> 268 us
  local copies, waits for them, and re-layouts: 11.5 us -> 8.12 us
    pallas_call x1, Pallas kernels: 31.9 us -> 41.7 us  [attend_backward(): pl.pallas_call(backward_kernel, out_shape=(jax.ShapeDtypeStruct((slots, B...]
    unnamed x39 -> x37, local copies, waits for them, and re-layouts: 10.1 us -> 6.75 us
    pallas_call x1, Pallas kernels: 101 us -> 97.7 us  [scatter(): pl.pallas_call(scatter_kernel, out_shape=(jax.ShapeDtypeStruct(full, f32)...]
  transfers between devices with their start and end apart: 5 -> 5, of which waited for: 0 -> 0; matrix products, arithmetic and copies ran while one was open for 0% -> 0% of each run, Pallas kernels for 19% -> 23%
where the time goes in v6:
time: 282 us
  Pallas kernels  268 us (95%)
  local copies, waits for them, and re-layouts  8.12 us (3%)
  starting transfers between devices  5.59 us (2%)
    pallas_call x1, Pallas kernels, scatter(): pl.pallas_call(scatter_kernel, out_shape=(jax.ShapeDtypeStruct(full, f32)...  97.7 us
    pallas_call x1, Pallas kernels, gather(): pl.pallas_call(gather_kernel, out_shape=(jax.ShapeDtypeStruct((8, GROUPS,...  52.5 us
    pallas_call x1, Pallas kernels, dense(): pl.pallas_call(dense_kernel, out_shape=(jax.ShapeDtypeStruct(full, f32),...  42.8 us
    pallas_call x1, Pallas kernels, attend_backward(): pl.pallas_call(backward_kernel, out_shape=(jax.ShapeDtypeStruct((slots, B...  41.7 us
    pallas_call x1, Pallas kernels, attend_forward(): pl.pallas_call(forward_kernel, out_shape=(jax.ShapeDtypeStruct((slots, HW...  22.5 us
    pallas_call x1, Pallas kernels, lay_out(): pl.pallas_call(layout_kernel, grid=(PARTS,), out_shape=(jax.ShapeDtypeStr...  10.5 us
    unnamed x37, local copies, waits for them, and re-layouts  6.75 us
  transfers between devices with their start and end apart: 5, of which 0 were waited for; matrix products, arithmetic and copies ran while one was open for 0% of the time, Pallas kernels for 23%

profile of v6, /device:TPU:0, one launch (start us, length us, event | category | flops | bytes accessed | tf_op | source)
XLA Modules:
  0.0 282.5 jit_solution(16160322906807315768)
XLA Ops:
  0.7 1.4 constant_dynamic-slice_fusion
  2.1 52.5 %gather.1 = (bf16[8,4,256,384]{3,2,1,0:T(8,128)(2,1)S(1)}, bf16[4,256,256]{2,1,0:T(8,128)(2,1)S(1)}, bf16[4,256,768]{2,1,0:T(8,128)(2,1)S(1)}, f32[16,768]{1,0:T...) custom-call(bf16[256,768]{1,0:T(8,128)(2,1)} %tokens_any.1, bf16[384,768]{1,0:T(8,128)(2,1)} %query_any.1, ...), custom_call_target="tpu_custom_call" | custom-call | tf_op jit(solution)/shard_map/gather/pallas_call | solution.py:662
  54.6 0.0 copy-start.3
  54.6 1.1 copy-done.3
  55.8 0.5 collective-permute-start.1
  56.3 1.5 collective-permute-start
  57.8 22.5 %attend_forward.1 = (bf16[8,192,128]{2,1,0:T(8,128)(2,1)S(1)}, f32[8,192,128]{2,1,0:T(8,128)S(1)}, f32[8,1,384]{2,1,0:T(1,128)S(1)}) custom-call(s32[64]{0:T(128)S(1)} %copy-done.12, s32[4]{0:T(128)S(1)} %copy-done.13, bf16[8,128,256]{2,1,0:T(8,128)(2,1)S(1)} %bitcast.13, bf16[64,128,384]{2,1,0:T(8,128)(2,1)S(1)} %bitcast.10), custom_call_target="tpu_custom_call" | custom-call | tf_op jit(solution)/shard_map/attend_forward/pallas_call | solution.py:180
  80.3 0.0 collective-permute-done.cot_x_ref
  80.4 42.8 %dense.1 = (f32[256,768]{1,0:T(8,128)S(1)}, bf16[448,768]{1,0:T(8,128)(2,1)S(1)}, f32[256,768]{1,0:T(8,128)S(1)}, bf16[8,192,128]{2,1,0:T(8,128)(2,1)S(1)}, bf16...) custom-call(bf16[8,192,128]{2,1,0:T(8,128)(2,1)S(1)} %get-tuple-elem, ...), custom_call_target="tpu_custom_call" | custom-call | tf_op jit(solution)/shard_map/dense/pallas_call | solution.py:960
  123.2 0.0 copy-start.4
  123.2 0.0 copy-start.7
  123.2 1.4 collective-permute-start.2
  124.7 1.4 collective-permute-start.3
  126.1 0.7 collective-permute-start.4
  126.8 41.7 %attend_backward.1 = (bf16[8,128,256]{2,1,0:T(8,128)(2,1)S(1)}, bf16[64,128,384]{2,1,0:T(8,128)(2,1)S(1)}) custom-call(s32[64]{0:T(128)S(1)} %copy-done.12, s32[4]{0:T(128)S(1)} %copy-done.13, bf16[8,128,256]{2,1,0:T(8,128)(2,1)S(1)} %bitcast.14, bf16[64,128,384]{2,1,0:T(8,128)(2,1)S(1)} %bitcast.11, f32[8,1,384]{2,1,0:T(1,128)S(1)} %get-tuple-element.63.lse_ref, ...), custom_call_target="tpu_custom_call" | custom-call | tf_op jit(solution)/shard_map/attend_backward/pallas_call | solution.py:324
  168.6 2.6 copy-done
  171.2 0.8 copy-done.8
  172.0 0.0 copy-start.15
  172.0 0.7 copy-done.17
  172.7 0.2 copy-done.14
  173.0 0.3 copy-done.15
  173.3 97.7 %scatter.1 = (f32[256,768]{1,0:T(8,128)}, bf16[2,2,4,216,768]{4,3,2,1,0:T(8,128)(2,1)}, bf16[2,4,192,256]{3,2,1,0:T(8,128)(2,1)}, bf16[2,4,192,384]{3,2,1,0:T(8,128)(2,1)}, f32[24,768]{1,0:T(8,128)}) custom-call(bf16[8,4,256,384]{3,2,1,0:T(8,128)(2,1)} %bitcast.12, bf16[4,256,256]{2,1,0:T(8,128)(2,1)} %bitcast.15, bf16[4,256,768]{2,1,0:T(8,128)(2,1)} %copy-done.3, ...), custom_call_target="tpu_custom_call" | custom-call | tf_op jit(solution)/shard_map/scatter/pallas_call | solution.py:1432
  271.0 10.5 %lay_out.1 = (f32[384,3072]{1,0:T(8,128)}, f32[2,768,768]{2,1,0:T(8,128)}, f32[2,192,768]{2,1,0:T(8,128)}, f32[2,192,768]{2,1,0:T(8,128)}, f32[2,192,768]{2,1,0:...) custom-call(bf16[2,8,216,768]{3,2,1,0:T(8,128)(2,1)} %bitcast.16, ...), custom_call_target="tpu_custom_call" | custom-call | tf_op jit(solution)/shard_map/lay_out/pallas_call | solution.py:1554
  281.6 0.9 copy.37
  (30 shorter events, 0.1 us)
Async XLA Ops:
  0.7 55.6 %copy-start.9 = (bf16[256,768]{1,0:T(8,128)(2,1)S(1)}, bf16[256,768]{1,0:T(8,128)(2,1)}, u32[]{:S(2)}) copy-start(bf16[256,768]{1,0:T(8,128)(2,1)} %cot_ref.1) | copy-start | bytes 1179652
  0.7 57.1 %copy-start.12 = (s32[64]{0:T(128)S(1)}, s32[64]{0:T(128)}, u32[]{:S(2)}) copy-start(s32[64]{0:T(128)} %deal_ref.3) | copy-start | bytes 772
  0.7 57.1 %copy-start.13 = (s32[4]{0:T(128)S(1)}, s32[4]{0:T(128)}, u32[]{:S(2)}) copy-start(s32[4]{0:T(128)} %lengths_ref.3) | copy-start | bytes 52
  54.6 1.1 copy-start.3
  55.8 24.6 %copy-start.5 = (bf16[768,640]{1,0:T(8,128)(2,1)}, bf16[768,640]{1,0:T(8,128)(2,1)S(1)}, u32[]{:S(2)}) copy-start(bf16[768,640]{1,0:T(8,128)(2,1)S(1)} %get-tuple-element.74.wfull_any) | copy-start | bytes 2949124
  55.8 24.6 %copy-start.10 = (f32[16,768]{1,0:T(8,128)}, f32[16,768]{1,0:T(8,128)S(1)}, u32[]{:S(2)}) copy-start(f32[16,768]{1,0:T(8,128)S(1)} %get-tuple-element.66.small_ref) | copy-start | bytes 147460
  55.8 24.6 %collective-permute-start.1 = (bf16[384,768]{1,0:T(8,128)(2,1)S(1)}, bf16[384,768]{1,0:T(8,128)(2,1)S(1)}, u32[]{:S(2)}, u32[]{:S(2)}) collective-permute-start(bf16[384,768]{1,0:T(8,128)(2,1)S(1)} %get-tuple-element.68), channel_id=1, source_target_pairs={{0,1},{1,0},{2,3},{3,2},{4,5},{5,4},{6,7},{7,6},{8,9},{9,8},{10,11... | collective-permute-start | bytes 1769480 | tf_op jit(solution)/shard_map/ppermute | solution.py:1623
  56.3 24.0 %collective-permute-start = (bf16[256,768]{1,0:T(8,128)(2,1)S(1)}, bf16[256,768]{1,0:T(8,128)(2,1)S(1)}, u32[]{:S(2)}, u32[]{:S(2)}) collective-permute-start(bf16[256,768]{1,0:T(8,128)(2,1)S(1)} %copy-done.9), channel_id=1, source_target_pairs={{0,1},{1,0},{2,3},{3,2},{4,5},{5,4},{6,7},{7,6},{8,9},{9,8},{10,11... | collective-permute-start | bytes 1179656 | tf_op jit(solution)/shard_map/ppermute | solution.py:1624
  57.8 22.5 %copy-start.1 = (bf16[256,768]{1,0:T(8,128)(2,1)S(1)}, bf16[256,768]{1,0:T(8,128)(2,1)}, u32[]{:S(2)}) copy-start(bf16[256,768]{1,0:T(8,128)(2,1)} %tokens_any.1) | copy-start | bytes 1179652
  57.8 22.5 %copy-start.2 = (bf16[1536,768]{1,0:T(8,128)(2,1)S(1)}, bf16[1536,768]{1,0:T(8,128)(2,1)}, u32[]{:S(2)}) copy-start(bf16[1536,768]{1,0:T(8,128)(2,1)} %down_any.1) | copy-start | bytes 7077892
  123.2 45.3 %copy-start.4 = (bf16[4,168,768]{2,1,0:T(8,128)(2,1)}, bf16[4,168,768]{2,1,0:T(8,128)(2,1)S(1)}, u32[]{:S(2)}) copy-start(bf16[4,168,768]{2,1,0:T(8,128)(2,1)S(1)} %get-tuple-element.76.keep_any) | copy-start | bytes 3096580
  123.2 45.3 %copy-start.6 = (f32[256,768]{1,0:T(8,128)}, f32[256,768]{1,0:T(8,128)S(1)}, u32[]{:S(2)}) copy-start(f32[256,768]{1,0:T(8,128)S(1)} %get-tuple-element.85.base_ref) | copy-start | bytes 2359300
  123.2 45.3 %copy-start.7 = (f32[256,768]{1,0:T(8,128)}, f32[256,768]{1,0:T(8,128)S(1)}, u32[]{:S(2)}) copy-start(f32[256,768]{1,0:T(8,128)S(1)} %get-tuple-element.75.mgrad_any) | copy-start | bytes 2359300
  123.2 45.3 %copy-start.11 = (f32[16,768]{1,0:T(8,128)}, f32[16,768]{1,0:T(8,128)S(1)}, u32[]{:S(2)}) copy-start(f32[16,768]{1,0:T(8,128)S(1)} %get-tuple-element.80.sums_in) | copy-start | bytes 147460
  123.2 48.8 %collective-permute-start.2 = (bf16[4,168,768]{2,1,0:T(8,128)(2,1)S(1)}, bf16[4,168,768]{2,1,0:T(8,128)(2,1)S(1)}, u32[]{:S(2)}, u32[]{:S(2)}) collective-permute-start(bf16[4,168,768]{2,1,0:T(8,128)(2,1)S(1)} %get-tuple-element.77), channel_id=1, source_target_pairs={{0,4},{4,0},{1,5},{5,1},{2,6},{6,2},{3,7},{7,3},{8,12},{12,8},{9,1... | collective-permute-start | bytes 3096584 | tf_op jit(solution)/shard_map/ppermute | solution.py:1629
  124.7 47.3 %collective-permute-start.3 = (bf16[448,768]{1,0:T(8,128)(2,1)S(1)}, bf16[448,768]{1,0:T(8,128)(2,1)S(1)}, u32[]{:S(2)}, u32[]{:S(2)}) collective-permute-start(bf16[448,768]{1,0:T(8,128)(2,1)S(1)} %get-tuple-element.78), channel_id=1, source_target_pairs={{0,1},{1,0},{2,3},{3,2},{4,5},{5,4},{6,7},{7,6},{8,9},{9,8},{10,11... | collective-permute-start | bytes 2064392 | tf_op jit(solution)/shard_map/ppermute | solution.py:1630
  126.1 45.9 %collective-permute-start.4 = (bf16[4,48,768]{2,1,0:T(8,128)(2,1)S(1)}, bf16[4,48,768]{2,1,0:T(8,128)(2,1)S(1)}, u32[]{:S(2)}, u32[]{:S(2)}) collective-permute-start(bf16[4,48,768]{2,1,0:T(8,128)(2,1)S(1)} %get-tuple-element.79), channel_id=1, source_target_pairs={{0,5},{1,4},{4,1},{5,0},{2,7},{3,6},{6,3},{7,2},{8,13},{9,12},{12,... | collective-permute-start | bytes 884744 | tf_op jit(solution)/shard_map/ppermute | solution.py:1631
  168.6 2.6 copy-start
  171.2 0.8 copy-start.8
  172.0 0.7 copy-start.17
  172.0 0.9 copy-start.14
  172.0 1.3 copy-start.15
  271.0 10.6 %copy-start.16 = (f32[256,768]{1,0:T(8,128)S(1)}, f32[256,768]{1,0:T(8,128)}, u32[]{:S(2)}) copy-start(f32[256,768]{1,0:T(8,128)} %get-tuple-element.123) | copy-start | bytes 2359300

commit v7 on v6

--- a/solution.py
+++ b/solution.py
@@ -345,7 +345,7 @@
             pltpu.SemaphoreType.DMA((DEPTH, 2)),
         ],
         compiler_params=pltpu.CompilerParams(
-            vmem_limit_bytes=max(30 << 20, (17 << 20) + kv.size * 2)
+            vmem_limit_bytes=max(46 << 20, (17 << 20) + kv.size * 2)
         ),
         name="attend_backward",
     )(deal, lengths, q, kv, lse, grad_t, wide)
@@ -699,7 +699,7 @@
 
 
 def dense_kernel(
-    out_t_ref, tokens_ref, cot_ref, cot_x_ref, small_ref, wo_ref, up_mine, up_other, down_any,
+    out_t_ref, tokens_ref, cot_ref, small_ref, wo_ref, up_mine, up_other, down_any,
     base_ref, x_give_ref, middle_grad_ref, grad_t_ref, keep_ref, give_ref, far_ref, sums_ref,
     down_ref, up_ref, attn_in, attn_t, cots, h2s, mid_ref, n2_ref, scales, part_y, part_d, in_y, in_d, pass_y, pass_d,
     x_y, x_d, hids, dus, branch_ref, grad_out, wo_keep, wo_give, wo_in, wo_pass, wo_x,
@@ -741,10 +741,8 @@
             begin(out_t_ref.at[2 * to + b], attn_in.at[g, b], a_send.at[b, away], a_recv.at[b, g], g=to)
         attn_in[g, b] = out_t_ref[2 * g + b]
         cots[b, 0] = cot_ref[rows_of(b)]
-        cots[b, 2] = cot_x_ref[rows_of(b)]
-    cot_moves = [
-        begin(cots.at[:, 2 * i], cots.at[:, 2 * i + 1], c_send.at[i], c_recv.at[i], core=sib) for i in range(2)
-    ]
+    cot_x = begin(cots.at[:, 0], cots.at[:, 2], c_send.at[2], c_recv.at[2], x=other)
+    cot_moves = [begin(cots.at[:, 0], cots.at[:, 1], c_send.at[0], c_recv.at[0], core=sib)]
     sums_ref[...] = jnp.zeros_like(sums_ref)
     sums_ref[5:6] = jnp.sum(cot_ref[...].astype(f32), axis=0, keepdims=True)
     h2_moves = []
@@ -848,6 +846,8 @@
     for load in loads:
         load.wait()
     near = [near_pair(0), None]
+    cot_x.wait_recv()
+    cot_moves.append(begin(cots.at[:, 2], cots.at[:, 3], c_send.at[1], c_recv.at[1], core=sib))
     passed = [pass_on(0), None]
     near[1] = near_pair(1)
     far = [far_pair(0, passed[0]), None]
@@ -950,7 +950,7 @@
         move.wait_send()
 
 
-def dense(out_t, tokens, cot, cot_x, small, wo, up_mine, up_other, down):
+def dense(out_t, tokens, cot, small, wo, up_mine, up_other, down):
     rows, width = tokens.shape
     dma = pltpu.SemaphoreType.DMA
     full = (rows, width)
@@ -969,7 +969,7 @@
             jax.ShapeDtypeStruct((GROUPS, 48, width), bf16),
             jax.ShapeDtypeStruct(small.shape, f32),
         ),
-        in_specs=[whole_vmem()] * 6 + [anywhere()] * 3,
+        in_specs=[whole_vmem()] * 5 + [anywhere()] * 3,
         out_specs=(whole_vmem(),) * 8,
         scratch_shapes=[
             pltpu.VMEM((width, width), bf16),
@@ -998,14 +998,14 @@
             pltpu.VMEM((2, *fourth), bf16),
             pltpu.VMEM(fourth, bf16),
             pltpu.VMEM(fourth, bf16),
-            dma((3,)), dma((2, GROUPS)), dma((2, GROUPS)), dma((2,)), dma((2,)), dma((2, 3)), dma((2, 3)),
+            dma((3,)), dma((2, GROUPS)), dma((2, GROUPS)), dma((3,)), dma((3,)), dma((2, 3)), dma((2, 3)),
             dma((2, 2)), dma((2, 2)), dma((2, 3)), dma((2, 3)), dma((2, GROUPS)), dma((2, GROUPS)), dma((2,)), dma((2,)),
         ],
         compiler_params=pltpu.CompilerParams(
             collective_id=1, has_side_effects=True, vmem_limit_bytes=40 << 20
         ),
         name="dense",
-    )(out_t, tokens, cot, cot_x, small, wo, up_mine, up_other, down)
+    )(out_t, tokens, cot, small, wo, up_mine, up_other, down)
 
 
 FARTHEST = ((3, 2, 1, 0), (3, 0, 2, 1), (0, 3, 1, 2), (0, 1, 2, 3))
@@ -1619,12 +1619,11 @@
         kv = lax.all_gather(kv, "s", axis=0, tiled=True)
     kv = kv.reshape(blocks, BLK, 2 * HW)
     q = q.reshape(2 * GROUPS, BLK, 2 * BLK)
-    cot_x, up_other, kv = lax.optimization_barrier((cotangent, up_columns(1 - x), kv))
+    up_other, kv = lax.optimization_barrier((up_columns(1 - x), kv))
     up_other = lax.ppermute(up_other, "x", swap)
-    cot_x = lax.ppermute(cot_x, "x", swap)
     out_t, kept, lse = attend_forward(deal, doc_lengths, q, kv)
     base, x_give, grad_middle, grad_t, kept_part, over, far, sums = dense(
-        out_t, tokens, cotangent, cot_x, small, wo, up_columns(x), up_other, down_weight
+        out_t, tokens, cotangent, small, wo, up_columns(x), up_other, down_weight
     )
     over = lax.ppermute(over, "r", swap)
     x_got = lax.ppermute(x_give, "x", swap)

time: 282 us -> 272 us (0.965); the launches traced: 282 us -> 276 us
  Pallas kernels: 268 us -> 258 us
  starting transfers between devices: 5.59 us -> 8.58 us
    pallas_call x1, Pallas kernels: 41.7 us -> 26.2 us  [attend_backward(): pl.pallas_call(backward_kernel, out_shape=(jax.ShapeDtypeStruct((slots, B...]
    pallas_call x1, Pallas kernels: 97.7 us -> 106 us  [scatter(): pl.pallas_call(scatter_kernel, out_shape=(jax.ShapeDtypeStruct(full, f32)...]
    pallas_call x1, Pallas kernels: 22.5 us -> 14.9 us  [attend_forward(): pl.pallas_call(forward_kernel, out_shape=(jax.ShapeDtypeStruct((slots, HW...]
    pallas_call x1, Pallas kernels: 42.8 us -> 47.6 us  [dense(): pl.pallas_call(dense_kernel, out_shape=(jax.ShapeDtypeStruct(full, f32),...]
    ppermute x1, starting transfers between devices: 1.44 us -> 5.38 us  [shards(): over = lax.ppermute(over, 'r', swap)]
  transfers between devices with their start and end apart: 5 -> 4, of which waited for: 0 -> 1; matrix products, arithmetic and copies ran while one was open for 0% -> 0% of each run, Pallas kernels for 23% -> 15%
where the time goes in v7:
time: 272 us; the launch traced here: 276 us
  Pallas kernels  258 us (95%)
  local copies, waits for them, and re-layouts  8.77 us (3%)
  starting transfers between devices  8.58 us (3%)
    pallas_call x1, Pallas kernels, scatter(): pl.pallas_call(scatter_kernel, out_shape=(jax.ShapeDtypeStruct(full, f32)...  106 us
    pallas_call x1, Pallas kernels, gather(): pl.pallas_call(gather_kernel, out_shape=(jax.ShapeDtypeStruct((8, GROUPS,...  52.5 us
    pallas_call x1, Pallas kernels, dense(): pl.pallas_call(dense_kernel, out_shape=(jax.ShapeDtypeStruct(full, f32),...  47.6 us
    pallas_call x1, Pallas kernels, attend_backward(): pl.pallas_call(backward_kernel, out_shape=(jax.ShapeDtypeStruct((slots, B...  26.2 us
    pallas_call x1, Pallas kernels, attend_forward(): pl.pallas_call(forward_kernel, out_shape=(jax.ShapeDtypeStruct((slots, HW...  14.9 us
    pallas_call x1, Pallas kernels, lay_out(): pl.pallas_call(layout_kernel, grid=(PARTS,), out_shape=(jax.ShapeDtypeStr...  10.5 us
    unnamed x37, local copies, waits for them, and re-layouts  7.43 us
  transfers between devices with their start and end apart: 4, of which 1 were waited for; matrix products, arithmetic and copies ran while one was open for 0% of the time, Pallas kernels for 15%

profile of v7, /device:TPU:0, one launch (start us, length us, event | category | flops | bytes accessed | tf_op | source)
XLA Modules:
  0.0 276.2 jit_solution(15303837734011490268)
XLA Ops:
  0.7 1.3 constant_dynamic-slice_fusion
  2.0 52.5 %gather.1 = (bf16[8,4,256,384]{3,2,1,0:T(8,128)(2,1)S(1)}, bf16[4,256,256]{2,1,0:T(8,128)(2,1)S(1)}, bf16[4,256,768]{2,1,0:T(8,128)(2,1)S(1)}, f32[16,768]{1,0:T...) custom-call(bf16[256,768]{1,0:T(8,128)(2,1)} %tokens_any.1, bf16[384,768]{1,0:T(8,128)(2,1)} %query_any.1, ...), custom_call_target="tpu_custom_call" | custom-call | tf_op jit(solution)/shard_map/gather/pallas_call | solution.py:662
  54.6 0.0 copy-start.3
  54.6 1.1 copy-done.3
  55.7 0.9 copy-done.5
  56.7 0.6 collective-permute-start
  57.2 0.0 copy-start.9
  57.2 14.9 %attend_forward.1 = (bf16[8,192,128]{2,1,0:T(8,128)(2,1)S(1)}, f32[8,192,128]{2,1,0:T(8,128)S(1)}, f32[8,1,384]{2,1,0:T(1,128)S(1)}) custom-call(s32[64]{0:T(128)S(1)} %copy-done.12, s32[4]{0:T(128)S(1)} %copy-done.13, bf16[8,128,256]{2,1,0:T(8,128)(2,1)S(1)} %bitcast.12, bf16[64,128,384]{2,1,0:T(8,128)(2,1)S(1)} %bitcast.10), custom_call_target="tpu_custom_call" | custom-call | tf_op jit(solution)/shard_map/attend_forward/pallas_call | solution.py:180
  72.1 0.1 collective-permute-done.up_other
  72.3 47.6 %dense.1 = (f32[256,768]{1,0:T(8,128)S(1)}, bf16[448,768]{1,0:T(8,128)(2,1)S(1)}, f32[256,768]{1,0:T(8,128)S(1)}, bf16[8,192,128]{2,1,0:T(8,128)(2,1)S(1)}, bf16...) custom-call(bf16[8,192,128]{2,1,0:T(8,128)(2,1)S(1)} %get-tuple-elem, ...), custom_call_target="tpu_custom_call" | custom-call | tf_op jit(solution)/shard_map/dense/pallas_call | solution.py:960
  119.9 0.9 copy-done.6
  120.8 0.9 copy-done.7
  121.7 0.6 copy-done.11
  122.3 5.4 %collective-permute-start.1 = (bf16[4,168,768]{2,1,0:T(8,128)(2,1)S(1)}, bf16[4,168,768]{2,1,0:T(8,128)(2,1)S(1)}, u32[]{:S(2)}, u32[]{:S(2)}) collective-permute-start(bf16[4,168,768]{2,1,0:T(8,128)(2,1)S(1)} %get-tuple-element.75), channel_id=1, source_target_pairs={{0,4},{4,0},{1,5},{5,1},{2,6},{6,2},{3,7},{7,3},{8,12},{12,8},{9,1... | collective-permute-start | bytes 3096584 | tf_op jit(solution)/shard_map/ppermute | solution.py:1628
  127.7 2.6 collective-permute-start.2
  130.3 26.2 %attend_backward.1 = (bf16[8,128,256]{2,1,0:T(8,128)(2,1)S(1)}, bf16[64,128,384]{2,1,0:T(8,128)(2,1)}) custom-call(s32[64]{0:T(128)S(1)} %copy-done.12, s32[4]{0:T(128)S(1)} %copy-done.13, bf16[8,128,256]{2,1,0:T(8,128)(2,1)S(1)} %bitcast.13, bf16[64,128,384]{2,1,0:T(8,128)(2,1)} %bitcast.11, f32[8,1,384]{2,1,0:T(1,128)S(1)} %get-tuple-element.62.lse_ref, ...), custom_call_target="tpu_custom_call" | custom-call | tf_op jit(solution)/shard_map/attend_backward/pallas_call | solution.py:324
  156.5 0.8 copy-done.8
  157.3 0.0 copy-start.15
  157.4 0.7 copy-done.17
  158.0 0.2 copy-done.14
  158.3 0.3 copy-done.15
  158.6 106.1 %scatter.1 = (f32[256,768]{1,0:T(8,128)}, bf16[2,2,4,216,768]{4,3,2,1,0:T(8,128)(2,1)}, bf16[2,4,192,256]{3,2,1,0:T(8,128)(2,1)}, bf16[2,4,192,384]{3,2,1,0:T(8,128)(2,1)}, f32[24,768]{1,0:T(8,128)}) custom-call(bf16[8,4,256,384]{3,2,1,0:T(8,128)(2,1)} %bitcast.15, bf16[4,256,256]{2,1,0:T(8,128)(2,1)} %bitcast.14, bf16[4,256,768]{2,1,0:T(8,128)(2,1)} %copy-done.3, ...), custom_call_target="tpu_custom_call" | custom-call | tf_op jit(solution)/shard_map/scatter/pallas_call | solution.py:1432
  264.7 10.5 %lay_out.1 = (f32[384,3072]{1,0:T(8,128)}, f32[2,768,768]{2,1,0:T(8,128)}, f32[2,192,768]{2,1,0:T(8,128)}, f32[2,192,768]{2,1,0:T(8,128)}, f32[2,192,768]{2,1,0:...) custom-call(bf16[2,8,216,768]{3,2,1,0:T(8,128)(2,1)} %bitcast.16, ...), custom_call_target="tpu_custom_call" | custom-call | tf_op jit(solution)/shard_map/lay_out/pallas_call | solution.py:1554
  275.3 0.9 copy.37
  (28 shorter events, 0.1 us)
Async XLA Ops:
  0.7 56.5 %copy-start.12 = (s32[64]{0:T(128)S(1)}, s32[64]{0:T(128)}, u32[]{:S(2)}) copy-start(s32[64]{0:T(128)} %deal_ref.3) | copy-start | bytes 772
  0.7 56.5 %copy-start.13 = (s32[4]{0:T(128)S(1)}, s32[4]{0:T(128)}, u32[]{:S(2)}) copy-start(s32[4]{0:T(128)} %lengths_ref.3) | copy-start | bytes 52
  54.6 1.1 copy-start.3
  55.7 0.9 copy-start.5
  56.6 15.4 %copy-start = (bf16[8,4,256,384]{3,2,1,0:T(8,128)(2,1)}, bf16[8,4,256,384]{3,2,1,0:T(8,128)(2,1)S(1)}, u32[]{:S(2)}) copy-start(bf16[8,4,256,384]{3,2,1,0:T(8,128)(2,1)S(1)} %get-tuple-element.60) | copy-start | bytes 18874372
  56.6 15.6 %copy-start.10 = (f32[16,768]{1,0:T(8,128)}, f32[16,768]{1,0:T(8,128)S(1)}, u32[]{:S(2)}) copy-start(f32[16,768]{1,0:T(8,128)S(1)} %get-tuple-element.64.small_ref) | copy-start | bytes 147460
  56.7 15.6 %collective-permute-start = (bf16[384,768]{1,0:T(8,128)(2,1)S(1)}, bf16[384,768]{1,0:T(8,128)(2,1)S(1)}, u32[]{:S(2)}, u32[]{:S(2)}) collective-permute-start(bf16[384,768]{1,0:T(8,128)(2,1)S(1)} %get-tuple-element.66), channel_id=1, source_target_pairs={{0,1},{1,0},{2,3},{3,2},{4,5},{5,4},{6,7},{7,6},{8,9},{9,8},{10,11... | collective-permute-start | bytes 1769480 | tf_op jit(solution)/shard_map/ppermute | solution.py:1623
  57.2 15.0 %copy-start.1 = (bf16[256,768]{1,0:T(8,128)(2,1)S(1)}, bf16[256,768]{1,0:T(8,128)(2,1)}, u32[]{:S(2)}) copy-start(bf16[256,768]{1,0:T(8,128)(2,1)} %tokens_any.1) | copy-start | bytes 1179652
  57.2 15.0 %copy-start.2 = (bf16[1536,768]{1,0:T(8,128)(2,1)S(1)}, bf16[1536,768]{1,0:T(8,128)(2,1)}, u32[]{:S(2)}) copy-start(bf16[1536,768]{1,0:T(8,128)(2,1)} %down_any.1) | copy-start | bytes 7077892
  57.2 15.0 %copy-start.9 = (bf16[256,768]{1,0:T(8,128)(2,1)S(1)}, bf16[256,768]{1,0:T(8,128)(2,1)}, u32[]{:S(2)}) copy-start(bf16[256,768]{1,0:T(8,128)(2,1)} %cot_ref.1) | copy-start | bytes 1179652
  119.9 0.9 copy-start.6
  120.8 0.9 copy-start.7
  121.7 0.6 copy-start.11
  122.3 34.2 %copy-start.4 = (bf16[4,168,768]{2,1,0:T(8,128)(2,1)}, bf16[4,168,768]{2,1,0:T(8,128)(2,1)S(1)}, u32[]{:S(2)}) copy-start(bf16[4,168,768]{2,1,0:T(8,128)(2,1)S(1)} %get-tuple-element.74.keep_any) | copy-start | bytes 3096580
  122.3 35.0 %collective-permute-start.1 = (bf16[4,168,768]{2,1,0:T(8,128)(2,1)S(1)}, bf16[4,168,768]{2,1,0:T(8,128)(2,1)S(1)}, u32[]{:S(2)}, u32[]{:S(2)}) collective-permute-start(bf16[4,168,768]{2,1,0:T(8,128)(2,1)S(1)} %get-tuple-element.75), channel_id=1, source_target_pairs={{0,4},{4,0},{1,5},{5,1},{2,6},{6,2},{3,7},{7,3},{8,12},{12,8},{9,1... | collective-permute-start | bytes 3096584 | tf_op jit(solution)/shard_map/ppermute | solution.py:1628
  127.7 29.6 %collective-permute-start.2 = (bf16[448,768]{1,0:T(8,128)(2,1)S(1)}, bf16[448,768]{1,0:T(8,128)(2,1)S(1)}, u32[]{:S(2)}, u32[]{:S(2)}) collective-permute-start(bf16[448,768]{1,0:T(8,128)(2,1)S(1)} %get-tuple-element.76), channel_id=1, source_target_pairs={{0,1},{1,0},{2,3},{3,2},{4,5},{5,4},{6,7},{7,6},{8,9},{9,8},{10,11... | collective-permute-start | bytes 2064392 | tf_op jit(solution)/shard_map/ppermute | solution.py:1629
  130.3 27.0 %collective-permute-start.3 = (bf16[4,48,768]{2,1,0:T(8,128)(2,1)S(1)}, bf16[4,48,768]{2,1,0:T(8,128)(2,1)S(1)}, u32[]{:S(2)}, u32[]{:S(2)}) collective-permute-start(bf16[4,48,768]{2,1,0:T(8,128)(2,1)S(1)} %get-tuple-element.77), channel_id=1, source_target_pairs={{0,5},{1,4},{4,1},{5,0},{2,7},{3,6},{6,3},{7,2},{8,13},{9,12},{12,... | collective-permute-start | bytes 884744 | tf_op jit(solution)/shard_map/ppermute | solution.py:1630
  156.5 0.8 copy-start.8
  157.3 0.7 copy-start.17
  157.3 0.9 copy-start.14
  157.3 1.3 copy-start.15
  264.7 10.6 %copy-start.16 = (f32[256,768]{1,0:T(8,128)S(1)}, f32[256,768]{1,0:T(8,128)}, u32[]{:S(2)}) copy-start(f32[256,768]{1,0:T(8,128)} %get-tuple-element.121) | copy-start | bytes 2359300

commit v8 on v7

--- a/solution.py
+++ b/solution.py
@@ -1144,18 +1144,15 @@
         pending[:] = [item for item in pending if item is not move]
 
     kv_moves = []
-    for i in range(GROUPS):
-        c = farthest(g, i)
-        for spot in range(4):
-            own = pltpu.make_async_copy(
-                dkv_ref.at[seat(spot // 2, core, spot % 2), c], own_kv.at[i, spot], own_sem.at[i, spot]
+
+    def start_kv():
+        for i in range(GROUPS):
+            c = farthest(g, i)
+            own = pltpu.make_async_copy(dkv_ref.at[:, core, :, c], own_kv.at[i], own_sem.at[i])
+            own.start()
+            kv_moves.append(
+                (own, begin(dkv_ref.at[:, sib, :, c], sib_kv.at[i], k_send.at[i], k_recv.at[i], core=sib))
             )
-            own.start()
-            across = begin(
-                dkv_ref.at[seat(spot // 2, sib, spot % 2), c], sib_kv.at[i, spot],
-                k_send.at[i, spot], k_recv.at[i, spot], core=sib,
-            )
-            kv_moves.append((own, across))
 
     def split(total, keep, give):
         for owner in range(2):
@@ -1189,6 +1186,7 @@
             line_q += scaled(c).astype(f32)
         sums_ref[pl.ds(16 + g, 1), 0:wide_q] = jnp.sum(line_q, axis=0, keepdims=True)
 
+    start_kv()
     sums_ref[...] = jnp.zeros_like(sums_ref)
     sums_ref[0:16] = sums_in[...]
     wg_kv[...] = jnp.zeros_like(wg_kv)
@@ -1241,13 +1239,12 @@
             chain.step(farthest(g, i))
 
     def on_sibling(i):
-        for own, across in kv_moves[4 * i : 4 * i + 4]:
-            own.wait()
-            across.wait_recv()
+        own, across = kv_moves[i]
+        own.wait()
+        across.wait_recv()
 
         def total(row, column):
-            spot = 2 * row + column
-            return own_kv[i, spot].astype(f32) + sib_kv[i, spot].astype(f32)
+            return own_kv[i, row, column].astype(f32) + sib_kv[i, row, column].astype(f32)
 
         for k in range(2):
             give_x[i, k] = (total(k, other) if i % 2 == 0 else total(far_r, k)).astype(bf16)
@@ -1315,19 +1312,20 @@
     q_sum[...] = (q_keep[x] + q_in[x].astype(f32) + q_x[...].astype(f32)).astype(bf16)
     q_over = begin(q_sum, q_y, q_send.at[2], q_recv.at[2], r=far_r)
     pl.when(between)(lambda: steps(chain_a, 0))
+    on_ring_b(1)
     on_second(2)
     on_second(3)
     pl.when(at_end)(lambda: steps(chain_a, 2))
     split(wg_kv, v_keep, v_give)
     v_move = begin(v_give, v_in, v_send.at[0], v_recv.at[0], core=sib)
     s_sib = begin(sums_ref, sums_got.at[0], s_send.at[0], s_recv.at[0], core=sib)
+    on_ring_b(2)
     spread_far(0)
     settled(q_over)
     q_sum[...] = (q_sum[...].astype(f32) + q_y[...].astype(f32)).astype(bf16)
     store(q_sum, q_slot(g), l_sem.at[0])
     ring_q.start()
     begin(q_slot(g), q_slot(g), qs_send.at[0], qs_recv.at[0], core=sib)
-    on_ring_b(1)
     v_move.wait_recv()
     v_pass[...] = (v_keep[other] + v_in[other].astype(f32)).astype(bf16)
     v_across = begin(v_pass, v_x, v_send.at[1], v_recv.at[1], x=other)
@@ -1341,13 +1339,13 @@
     settled(s_x)
     sums_ref[...] += sums_got[1]
     s_y = begin(sums_ref, sums_got.at[2], s_send.at[2], s_recv.at[2], r=far_r)
-    on_ring_b(2)
     pl.when(between)(lambda: steps(chain_a, 2))
     settled(v_over)
     v_sum[...] = (v_sum[...].astype(f32) + v_y[...].astype(f32)).astype(bf16)
     store(v_sum, v_slot(g), l_sem.at[0])
     ring_v.start()
     begin(v_slot(g), v_slot(g), vs_send.at[0], vs_recv.at[0], core=sib)
+    on_ring_b(3)
     settled(s_y)
     sums_ref[...] += sums_got[2]
     for away in range(1, GROUPS):
@@ -1357,7 +1355,6 @@
         )
     spread_far(1)
     on_ring_q(1)
-    on_ring_b(3)
     chain_a.step(g)
 
     loads[7].wait()
@@ -1447,8 +1444,8 @@
             ],
             pltpu.VMEM((48 * GROUPS, width), bf16),
             pltpu.VMEM(far.shape, bf16),
-            pltpu.VMEM((GROUPS, 4, *kv_block), bf16),
-            pltpu.VMEM((GROUPS, 4, *kv_block), bf16),
+            pltpu.VMEM((GROUPS, 2, 2, *kv_block), bf16),
+            pltpu.VMEM((GROUPS, 2, 2, *kv_block), bf16),
             pltpu.VMEM((GROUPS, 2, *kv_block), f32),
             pltpu.VMEM((GROUPS, 2, *kv_block), bf16),
             pltpu.VMEM((GROUPS, 2, *kv_block), bf16),
@@ -1471,7 +1468,7 @@
             pltpu.VMEM((8, width), f32),
             pltpu.VMEM((len(AROUND) + GROUPS - 1, 8, width), f32),
             dma((9,)),
-            dma((GROUPS, 4)), dma((GROUPS, 4)), dma((GROUPS, 4)), dma((GROUPS,)), dma((GROUPS,)), dma((GROUPS,)), dma((GROUPS,)),
+            dma((GROUPS,)), dma((GROUPS,)), dma((GROUPS,)), dma((GROUPS,)), dma((GROUPS,)), dma((GROUPS,)), dma((GROUPS,)),
             dma((GROUPS,)), dma((2, GROUPS)),
             dma((GROUPS,)), dma((2, GROUPS)), dma((2,)), dma((GROUPS,)), dma((GROUPS,)),
             dma((GROUPS,)), dma((GROUPS,)), dma((2, GROUPS)), dma((2, GROUPS)),
@@ -1632,6 +1629,7 @@
     dkv = dkv.reshape(-1, GROUPS, rows, 2 * HW)
     if wide:
         dkv = lax.psum_scatter(dkv, "s", scatter_dimension=0, tiled=True)
+    dkv = dkv.reshape(2, 2, 2, GROUPS, rows, 2 * HW)
     dq = dq.reshape(GROUPS, rows, 2 * BLK)
     grad_tokens, big, query_own, kv_own, sums = scatter(
         *stay(dkv, dq, normed, wfull, tokens, grad_middle), small, *stay(kept_part, over, x_got, far), sums

time: 272 us -> 265 us (0.974); the launches traced: 276 us -> 264 us
  Pallas kernels: 258 us -> 250 us
  starting transfers between devices: 8.58 us -> 4.04 us
    pallas_call x1, Pallas kernels: 106 us -> 92.4 us  [scatter(): pl.pallas_call(scatter_kernel, out_shape=(jax.ShapeDtypeStruct(full, f32)...]
    pallas_call x1, Pallas kernels: 26.2 us -> 30.7 us  [attend_backward(): pl.pallas_call(backward_kernel, out_shape=(jax.ShapeDtypeStruct((slots, B...]
    ppermute x1, starting transfers between devices: 5.38 us -> 1.85 us  [shards(): over = lax.ppermute(over, 'r', swap)]
    pallas_call x1, Pallas kernels: 14.9 us -> 18.3 us  [attend_forward(): pl.pallas_call(forward_kernel, out_shape=(jax.ShapeDtypeStruct((slots, HW...]
  transfers between devices with their start and end apart: 4 -> 4, of which waited for: 1 -> 0; matrix products, arithmetic and copies ran while one was open for 0% -> 0% of each run, Pallas kernels for 15% -> 19%
where the time goes in v8:
time: 265 us; the launch traced here: 264 us
  Pallas kernels  250 us (94%)
  local copies, waits for them, and re-layouts  8.77 us (3%)
  starting transfers between devices  4.04 us (2%)
    pallas_call x1, Pallas kernels, scatter(): pl.pallas_call(scatter_kernel, out_shape=(jax.ShapeDtypeStruct(full, f32)...  92.4 us
    pallas_call x1, Pallas kernels, gather(): pl.pallas_call(gather_kernel, out_shape=(jax.ShapeDtypeStruct((8, GROUPS,...  52.5 us
    pallas_call x1, Pallas kernels, dense(): pl.pallas_call(dense_kernel, out_shape=(jax.ShapeDtypeStruct(full, f32),...  45.8 us
    pallas_call x1, Pallas kernels, attend_backward(): pl.pallas_call(backward_kernel, out_shape=(jax.ShapeDtypeStruct((slots, B...  30.7 us
    pallas_call x1, Pallas kernels, attend_forward(): pl.pallas_call(forward_kernel, out_shape=(jax.ShapeDtypeStruct((slots, HW...  18.3 us
    pallas_call x1, Pallas kernels, lay_out(): pl.pallas_call(layout_kernel, grid=(PARTS,), out_shape=(jax.ShapeDtypeStr...  10.5 us
    unnamed x37, local copies, waits for them, and re-layouts  7.43 us
  transfers between devices with their start and end apart: 4, of which 0 were waited for; matrix products, arithmetic and copies ran while one was open for 0% of the time, Pallas kernels for 19%

profile of v8, /device:TPU:0, one launch (start us, length us, event | category | flops | bytes accessed | tf_op | source)
XLA Modules:
  0.0 264.0 jit_solution(5731900591210410323)
XLA Ops:
  0.7 1.3 constant_dynamic-slice_fusion
  2.0 52.5 %gather.1 = (bf16[8,4,256,384]{3,2,1,0:T(8,128)(2,1)S(1)}, bf16[4,256,256]{2,1,0:T(8,128)(2,1)S(1)}, bf16[4,256,768]{2,1,0:T(8,128)(2,1)S(1)}, f32[16,768]{1,0:T...) custom-call(bf16[256,768]{1,0:T(8,128)(2,1)} %tokens_any.1, bf16[384,768]{1,0:T(8,128)(2,1)} %query_any.1, ...), custom_call_target="tpu_custom_call" | custom-call | tf_op jit(solution)/shard_map/gather/pallas_call | solution.py:662
  54.6 0.0 copy-start.3
  54.6 1.1 copy-done.3
  55.7 0.9 copy-done.5
  56.7 0.6 collective-permute-start
  57.2 0.0 copy-start.9
  57.2 18.3 %attend_forward.1 = (bf16[8,192,128]{2,1,0:T(8,128)(2,1)S(1)}, f32[8,192,128]{2,1,0:T(8,128)S(1)}, f32[8,1,384]{2,1,0:T(1,128)S(1)}) custom-call(s32[64]{0:T(128)S(1)} %copy-done.12, s32[4]{0:T(128)S(1)} %copy-done.13, bf16[8,128,256]{2,1,0:T(8,128)(2,1)S(1)} %bitcast.12, bf16[64,128,384]{2,1,0:T(8,128)(2,1)S(1)} %bitcast.10), custom_call_target="tpu_custom_call" | custom-call | tf_op jit(solution)/shard_map/attend_forward/pallas_call | solution.py:180
  75.6 45.8 %dense.1 = (f32[256,768]{1,0:T(8,128)S(1)}, bf16[448,768]{1,0:T(8,128)(2,1)S(1)}, f32[256,768]{1,0:T(8,128)S(1)}, bf16[8,192,128]{2,1,0:T(8,128)(2,1)S(1)}, bf16...) custom-call(bf16[8,192,128]{2,1,0:T(8,128)(2,1)S(1)} %get-tuple-elem, ...), custom_call_target="tpu_custom_call" | custom-call | tf_op jit(solution)/shard_map/dense/pallas_call | solution.py:960
  121.4 0.9 copy-done.6
  122.3 0.9 copy-done.7
  123.2 0.6 copy-done.11
  123.8 1.9 collective-permute-start.1
  125.6 0.2 collective-permute-start.2
  125.8 1.5 collective-permute-start.3
  127.3 30.7 %attend_backward.1 = (bf16[8,128,256]{2,1,0:T(8,128)(2,1)S(1)}, bf16[64,128,384]{2,1,0:T(8,128)(2,1)}) custom-call(s32[64]{0:T(128)S(1)} %copy-done.12, s32[4]{0:T(128)S(1)} %copy-done.13, bf16[8,128,256]{2,1,0:T(8,128)(2,1)S(1)} %bitcast.13, bf16[64,128,384]{2,1,0:T(8,128)(2,1)} %bitcast.11, f32[8,1,384]{2,1,0:T(1,128)S(1)} %get-tuple-element.62.lse_ref, ...), custom_call_target="tpu_custom_call" | custom-call | tf_op jit(solution)/shard_map/attend_backward/pallas_call | solution.py:324
  158.0 0.0 copy-start.8
  158.0 0.8 copy-done.8
  158.8 0.7 copy-done.17
  159.5 0.2 copy-done.14
  159.7 0.3 copy-done.15
  160.1 92.4 %scatter.1 = (f32[256,768]{1,0:T(8,128)}, bf16[2,2,4,216,768]{4,3,2,1,0:T(8,128)(2,1)}, bf16[2,4,192,256]{3,2,1,0:T(8,128)(2,1)}, bf16[2,4,192,384]{3,2,1,0:T(8,128)(2,1)}, f32[24,768]{1,0:T(8,128)}) custom-call(bf16[2,2,2,4,256,384]{5,4,3,2,1,0:T(8,128)(2,1)} %bitcast.15, bf16[4,256,256]{2,1,0:T(8,128)(2,1)} %bitcast.14, bf16[4,256,768]{2,1,0:T(8,128)(2,1)} %copy-done.3, ...), custom_call_target="tpu_custom_call" | custom-call | tf_op jit(solution)/shard_map/scatter/pallas_call | solution.py:1429
  252.5 10.5 %lay_out.1 = (f32[384,3072]{1,0:T(8,128)}, f32[2,768,768]{2,1,0:T(8,128)}, f32[2,192,768]{2,1,0:T(8,128)}, f32[2,192,768]{2,1,0:T(8,128)}, f32[2,192,768]{2,1,0:...) custom-call(bf16[2,8,216,768]{3,2,1,0:T(8,128)(2,1)} %bitcast.16, ...), custom_call_target="tpu_custom_call" | custom-call | tf_op jit(solution)/shard_map/lay_out/pallas_call | solution.py:1551
  263.1 0.9 copy.37
  (28 shorter events, 0.1 us)
Async XLA Ops:
  0.7 56.5 %copy-start.12 = (s32[64]{0:T(128)S(1)}, s32[64]{0:T(128)}, u32[]{:S(2)}) copy-start(s32[64]{0:T(128)} %deal_ref.3) | copy-start | bytes 772
  0.7 56.5 %copy-start.13 = (s32[4]{0:T(128)S(1)}, s32[4]{0:T(128)}, u32[]{:S(2)}) copy-start(s32[4]{0:T(128)} %lengths_ref.3) | copy-start | bytes 52
  54.6 1.1 copy-start.3
  55.7 0.9 copy-start.5
  56.6 18.9 %copy-start = (bf16[8,4,256,384]{3,2,1,0:T(8,128)(2,1)}, bf16[8,4,256,384]{3,2,1,0:T(8,128)(2,1)S(1)}, u32[]{:S(2)}) copy-start(bf16[8,4,256,384]{3,2,1,0:T(8,128)(2,1)S(1)} %get-tuple-element.60) | copy-start | bytes 18874372
  56.6 18.9 %copy-start.10 = (f32[16,768]{1,0:T(8,128)}, f32[16,768]{1,0:T(8,128)S(1)}, u32[]{:S(2)}) copy-start(f32[16,768]{1,0:T(8,128)S(1)} %get-tuple-element.64.small_ref) | copy-start | bytes 147460
  56.7 18.9 %collective-permute-start = (bf16[384,768]{1,0:T(8,128)(2,1)S(1)}, bf16[384,768]{1,0:T(8,128)(2,1)S(1)}, u32[]{:S(2)}, u32[]{:S(2)}) collective-permute-start(bf16[384,768]{1,0:T(8,128)(2,1)S(1)} %get-tuple-element.66), channel_id=1, source_target_pairs={{0,1},{1,0},{2,3},{3,2},{4,5},{5,4},{6,7},{7,6},{8,9},{9,8},{10,11... | collective-permute-start | bytes 1769480 | tf_op jit(solution)/shard_map/ppermute | solution.py:1620
  57.2 18.4 %copy-start.1 = (bf16[256,768]{1,0:T(8,128)(2,1)S(1)}, bf16[256,768]{1,0:T(8,128)(2,1)}, u32[]{:S(2)}) copy-start(bf16[256,768]{1,0:T(8,128)(2,1)} %tokens_any.1) | copy-start | bytes 1179652
  57.2 18.4 %copy-start.2 = (bf16[1536,768]{1,0:T(8,128)(2,1)S(1)}, bf16[1536,768]{1,0:T(8,128)(2,1)}, u32[]{:S(2)}) copy-start(bf16[1536,768]{1,0:T(8,128)(2,1)} %down_any.1) | copy-start | bytes 7077892
  57.2 18.4 %copy-start.9 = (bf16[256,768]{1,0:T(8,128)(2,1)S(1)}, bf16[256,768]{1,0:T(8,128)(2,1)}, u32[]{:S(2)}) copy-start(bf16[256,768]{1,0:T(8,128)(2,1)} %cot_ref.1) | copy-start | bytes 1179652
  121.4 0.9 copy-start.6
  122.3 0.9 copy-start.7
  123.2 0.6 copy-start.11
  123.8 34.2 %copy-start.4 = (bf16[4,168,768]{2,1,0:T(8,128)(2,1)}, bf16[4,168,768]{2,1,0:T(8,128)(2,1)S(1)}, u32[]{:S(2)}) copy-start(bf16[4,168,768]{2,1,0:T(8,128)(2,1)S(1)} %get-tuple-element.74.keep_any) | copy-start | bytes 3096580
  123.8 35.0 %collective-permute-start.1 = (bf16[4,168,768]{2,1,0:T(8,128)(2,1)S(1)}, bf16[4,168,768]{2,1,0:T(8,128)(2,1)S(1)}, u32[]{:S(2)}, u32[]{:S(2)}) collective-permute-start(bf16[4,168,768]{2,1,0:T(8,128)(2,1)S(1)} %get-tuple-element.75), channel_id=1, source_target_pairs={{0,4},{4,0},{1,5},{5,1},{2,6},{6,2},{3,7},{7,3},{8,12},{12,8},{9,1... | collective-permute-start | bytes 3096584 | tf_op jit(solution)/shard_map/ppermute | solution.py:1625
  125.6 33.2 %collective-permute-start.2 = (bf16[448,768]{1,0:T(8,128)(2,1)S(1)}, bf16[448,768]{1,0:T(8,128)(2,1)S(1)}, u32[]{:S(2)}, u32[]{:S(2)}) collective-permute-start(bf16[448,768]{1,0:T(8,128)(2,1)S(1)} %get-tuple-element.76), channel_id=1, source_target_pairs={{0,1},{1,0},{2,3},{3,2},{4,5},{5,4},{6,7},{7,6},{8,9},{9,8},{10,11... | collective-permute-start | bytes 2064392 | tf_op jit(solution)/shard_map/ppermute | solution.py:1626
  125.8 33.0 %collective-permute-start.3 = (bf16[4,48,768]{2,1,0:T(8,128)(2,1)S(1)}, bf16[4,48,768]{2,1,0:T(8,128)(2,1)S(1)}, u32[]{:S(2)}, u32[]{:S(2)}) collective-permute-start(bf16[4,48,768]{2,1,0:T(8,128)(2,1)S(1)} %get-tuple-element.77), channel_id=1, source_target_pairs={{0,5},{1,4},{4,1},{5,0},{2,7},{3,6},{6,3},{7,2},{8,13},{9,12},{12,... | collective-permute-start | bytes 884744 | tf_op jit(solution)/shard_map/ppermute | solution.py:1627
  158.0 0.8 copy-start.8
  158.8 0.7 copy-start.17
  158.8 0.9 copy-start.14
  158.8 1.3 copy-start.15
  252.5 10.6 %copy-start.16 = (f32[256,768]{1,0:T(8,128)S(1)}, f32[256,768]{1,0:T(8,128)}, u32[]{:S(2)}) copy-start(f32[256,768]{1,0:T(8,128)} %get-tuple-element.121) | copy-start | bytes 2359300

commit v9 on v8

--- a/solution.py
+++ b/solution.py
@@ -1002,7 +1002,7 @@
             dma((2, 2)), dma((2, 2)), dma((2, 3)), dma((2, 3)), dma((2, GROUPS)), dma((2, GROUPS)), dma((2,)), dma((2,)),
         ],
         compiler_params=pltpu.CompilerParams(
-            collective_id=1, has_side_effects=True, vmem_limit_bytes=40 << 20
+            collective_id=1, has_side_effects=True, vmem_limit_bytes=46 << 20
         ),
         name="dense",
     )(out_t, tokens, cot, small, wo, up_mine, up_other, down)

time: 265 us -> 270 us (1.019)
  Pallas kernels: 250 us -> 257 us
    pallas_call x1, Pallas kernels: 92.4 us -> 97.3 us  [scatter(): pl.pallas_call(scatter_kernel, out_shape=(jax.ShapeDtypeStruct(full, f32)...]
  transfers between devices with their start and end apart: 4 -> 4, of which waited for: 0 -> 0; matrix products, arithmetic and copies ran while one was open for 0% -> 0% of each run, Pallas kernels for 19% -> 18%
where the time goes in v9:
time: 270 us; the launch traced here: 269 us
  Pallas kernels  257 us (95%)
  local copies, waits for them, and re-layouts  7.4 us (3%)
  starting transfers between devices  4.24 us (2%)
    pallas_call x1, Pallas kernels, scatter(): pl.pallas_call(scatter_kernel, out_shape=(jax.ShapeDtypeStruct(full, f32)...  97.3 us
    pallas_call x1, Pallas kernels, gather(): pl.pallas_call(gather_kernel, out_shape=(jax.ShapeDtypeStruct((8, GROUPS,...  52.5 us
    pallas_call x1, Pallas kernels, dense(): pl.pallas_call(dense_kernel, out_shape=(jax.ShapeDtypeStruct(full, f32),...  48.3 us
    pallas_call x1, Pallas kernels, attend_backward(): pl.pallas_call(backward_kernel, out_shape=(jax.ShapeDtypeStruct((slots, B...  29.8 us
    pallas_call x1, Pallas kernels, attend_forward(): pl.pallas_call(forward_kernel, out_shape=(jax.ShapeDtypeStruct((slots, HW...  18.3 us
    pallas_call x1, Pallas kernels, lay_out(): pl.pallas_call(layout_kernel, grid=(PARTS,), out_shape=(jax.ShapeDtypeStr...  10.5 us
    unnamed x37, local copies, waits for them, and re-layouts  6.06 us
  transfers between devices with their start and end apart: 4, of which 0 were waited for; matrix products, arithmetic and copies ran while one was open for 0% of the time, Pallas kernels for 18%

profile of v9, /device:TPU:0, one launch (start us, length us, event | category | flops | bytes accessed | tf_op | source)
XLA Modules:
  0.0 269.4 jit_solution(1949633692719862666)
XLA Ops:
  0.7 1.3 constant_dynamic-slice_fusion
  2.0 52.5 %gather.1 = (bf16[8,4,256,384]{3,2,1,0:T(8,128)(2,1)S(1)}, bf16[4,256,256]{2,1,0:T(8,128)(2,1)S(1)}, bf16[4,256,768]{2,1,0:T(8,128)(2,1)S(1)}, f32[16,768]{1,0:T...) custom-call(bf16[256,768]{1,0:T(8,128)(2,1)} %tokens_any.1, bf16[384,768]{1,0:T(8,128)(2,1)} %query_any.1, ...), custom_call_target="tpu_custom_call" | custom-call | tf_op jit(solution)/shard_map/gather/pallas_call | solution.py:662
  54.6 0.0 copy-start.2
  54.6 1.1 copy-done.2
  55.7 1.0 copy-done.3
  56.7 0.9 copy-done.5
  57.7 0.6 collective-permute-start
  58.2 18.3 %attend_forward.1 = (bf16[8,192,128]{2,1,0:T(8,128)(2,1)S(1)}, f32[8,192,128]{2,1,0:T(8,128)S(1)}, f32[8,1,384]{2,1,0:T(1,128)S(1)}) custom-call(s32[64]{0:T(128)S(1)} %copy-done.12, s32[4]{0:T(128)S(1)} %copy-done.13, bf16[8,128,256]{2,1,0:T(8,128)(2,1)S(1)} %bitcast.12, bf16[64,128,384]{2,1,0:T(8,128)(2,1)S(1)} %bitcast.10), custom_call_target="tpu_custom_call" | custom-call | tf_op jit(solution)/shard_map/attend_forward/pallas_call | solution.py:180
  76.6 48.3 %dense.1 = (f32[256,768]{1,0:T(8,128)S(1)}, bf16[448,768]{1,0:T(8,128)(2,1)S(1)}, f32[256,768]{1,0:T(8,128)S(1)}, bf16[8,192,128]{2,1,0:T(8,128)(2,1)S(1)}, bf16...) custom-call(bf16[8,192,128]{2,1,0:T(8,128)(2,1)S(1)} %get-tuple-elem, ...), custom_call_target="tpu_custom_call" | custom-call | tf_op jit(solution)/shard_map/dense/pallas_call | solution.py:960
  124.9 0.0 copy-start.4
  124.9 0.0 copy-start.7
  125.0 0.1 collective-permute-start.1
  125.0 2.2 collective-permute-start.2
  127.3 1.4 collective-permute-start.3
  128.7 29.8 %attend_backward.1 = (bf16[8,128,256]{2,1,0:T(8,128)(2,1)S(1)}, bf16[64,128,384]{2,1,0:T(8,128)(2,1)}) custom-call(s32[64]{0:T(128)S(1)} %copy-done.12, s32[4]{0:T(128)S(1)} %copy-done.13, bf16[8,128,256]{2,1,0:T(8,128)(2,1)S(1)} %bitcast.13, bf16[64,128,384]{2,1,0:T(8,128)(2,1)} %bitcast.11, f32[8,1,384]{2,1,0:T(1,128)S(1)} %get-tuple-element.62.lse_ref, ...), custom_call_target="tpu_custom_call" | custom-call | tf_op jit(solution)/shard_map/attend_backward/pallas_call | solution.py:324
  158.5 0.0 copy-start.8
  158.5 0.8 copy-done.8
  159.4 0.0 copy-start.15
  159.4 0.7 copy-done.17
  160.0 0.2 copy-done.14
  160.3 0.3 copy-done.15
  160.6 97.3 %scatter.1 = (f32[256,768]{1,0:T(8,128)}, bf16[2,2,4,216,768]{4,3,2,1,0:T(8,128)(2,1)}, bf16[2,4,192,256]{3,2,1,0:T(8,128)(2,1)}, bf16[2,4,192,384]{3,2,1,0:T(8,128)(2,1)}, f32[24,768]{1,0:T(8,128)}) custom-call(bf16[2,2,2,4,256,384]{5,4,3,2,1,0:T(8,128)(2,1)} %bitcast.15, bf16[4,256,256]{2,1,0:T(8,128)(2,1)} %bitcast.14, bf16[4,256,768]{2,1,0:T(8,128)(2,1)} %copy-done.2, ...), custom_call_target="tpu_custom_call" | custom-call | tf_op jit(solution)/shard_map/scatter/pallas_call | solution.py:1429
  257.9 10.5 %lay_out.1 = (f32[384,3072]{1,0:T(8,128)}, f32[2,768,768]{2,1,0:T(8,128)}, f32[2,192,768]{2,1,0:T(8,128)}, f32[2,192,768]{2,1,0:T(8,128)}, f32[2,192,768]{2,1,0:...) custom-call(bf16[2,8,216,768]{3,2,1,0:T(8,128)(2,1)} %bitcast.16, ...), custom_call_target="tpu_custom_call" | custom-call | tf_op jit(solution)/shard_map/lay_out/pallas_call | solution.py:1551
  268.5 0.9 copy.37
  (28 shorter events, 0.1 us)
Async XLA Ops:
  0.7 57.6 %copy-start.12 = (s32[64]{0:T(128)S(1)}, s32[64]{0:T(128)}, u32[]{:S(2)}) copy-start(s32[64]{0:T(128)} %deal_ref.3) | copy-start | bytes 772
  0.7 57.5 %copy-start.13 = (s32[4]{0:T(128)S(1)}, s32[4]{0:T(128)}, u32[]{:S(2)}) copy-start(s32[4]{0:T(128)} %lengths_ref.3) | copy-start | bytes 52
  54.6 1.1 copy-start.2
  55.7 1.0 copy-start.3
  56.7 0.9 copy-start.5
  57.7 18.9 %copy-start = (bf16[8,4,256,384]{3,2,1,0:T(8,128)(2,1)}, bf16[8,4,256,384]{3,2,1,0:T(8,128)(2,1)S(1)}, u32[]{:S(2)}) copy-start(bf16[8,4,256,384]{3,2,1,0:T(8,128)(2,1)S(1)} %get-tuple-element.60) | copy-start | bytes 18874372
  57.7 18.9 %copy-start.10 = (f32[16,768]{1,0:T(8,128)}, f32[16,768]{1,0:T(8,128)S(1)}, u32[]{:S(2)}) copy-start(f32[16,768]{1,0:T(8,128)S(1)} %get-tuple-element.64.small_ref) | copy-start | bytes 147460
  57.7 18.9 %collective-permute-start = (bf16[384,768]{1,0:T(8,128)(2,1)S(1)}, bf16[384,768]{1,0:T(8,128)(2,1)S(1)}, u32[]{:S(2)}, u32[]{:S(2)}) collective-permute-start(bf16[384,768]{1,0:T(8,128)(2,1)S(1)} %get-tuple-element.66), channel_id=1, source_target_pairs={{0,1},{1,0},{2,3},{3,2},{4,5},{5,4},{6,7},{7,6},{8,9},{9,8},{10,11... | collective-permute-start | bytes 1769480 | tf_op jit(solution)/shard_map/ppermute | solution.py:1620
  58.2 18.4 %copy-start.1 = (bf16[256,768]{1,0:T(8,128)(2,1)S(1)}, bf16[256,768]{1,0:T(8,128)(2,1)}, u32[]{:S(2)}) copy-start(bf16[256,768]{1,0:T(8,128)(2,1)} %tokens_any.1) | copy-start | bytes 1179652
  58.2 18.4 %copy-start.9 = (bf16[256,768]{1,0:T(8,128)(2,1)S(1)}, bf16[256,768]{1,0:T(8,128)(2,1)}, u32[]{:S(2)}) copy-start(bf16[256,768]{1,0:T(8,128)(2,1)} %cot_ref.1) | copy-start | bytes 1179652
  124.9 33.6 %copy-start.4 = (bf16[4,168,768]{2,1,0:T(8,128)(2,1)}, bf16[4,168,768]{2,1,0:T(8,128)(2,1)S(1)}, u32[]{:S(2)}) copy-start(bf16[4,168,768]{2,1,0:T(8,128)(2,1)S(1)} %get-tuple-element.74.keep_any) | copy-start | bytes 3096580
  124.9 33.6 %copy-start.6 = (f32[256,768]{1,0:T(8,128)}, f32[256,768]{1,0:T(8,128)S(1)}, u32[]{:S(2)}) copy-start(f32[256,768]{1,0:T(8,128)S(1)} %get-tuple-element.83.base_ref) | copy-start | bytes 2359300
  124.9 33.6 %copy-start.7 = (f32[256,768]{1,0:T(8,128)}, f32[256,768]{1,0:T(8,128)S(1)}, u32[]{:S(2)}) copy-start(f32[256,768]{1,0:T(8,128)S(1)} %get-tuple-element.73.mgrad_any) | copy-start | bytes 2359300
  124.9 33.6 %copy-start.11 = (f32[16,768]{1,0:T(8,128)}, f32[16,768]{1,0:T(8,128)S(1)}, u32[]{:S(2)}) copy-start(f32[16,768]{1,0:T(8,128)S(1)} %get-tuple-element.78.sums_in) | copy-start | bytes 147460
  125.0 34.4 %collective-permute-start.1 = (bf16[4,168,768]{2,1,0:T(8,128)(2,1)S(1)}, bf16[4,168,768]{2,1,0:T(8,128)(2,1)S(1)}, u32[]{:S(2)}, u32[]{:S(2)}) collective-permute-start(bf16[4,168,768]{2,1,0:T(8,128)(2,1)S(1)} %get-tuple-element.75), channel_id=1, source_target_pairs={{0,4},{4,0},{1,5},{5,1},{2,6},{6,2},{3,7},{7,3},{8,12},{12,8},{9,1... | collective-permute-start | bytes 3096584 | tf_op jit(solution)/shard_map/ppermute | solution.py:1625
  125.0 34.3 %collective-permute-start.2 = (bf16[448,768]{1,0:T(8,128)(2,1)S(1)}, bf16[448,768]{1,0:T(8,128)(2,1)S(1)}, u32[]{:S(2)}, u32[]{:S(2)}) collective-permute-start(bf16[448,768]{1,0:T(8,128)(2,1)S(1)} %get-tuple-element.76), channel_id=1, source_target_pairs={{0,1},{1,0},{2,3},{3,2},{4,5},{5,4},{6,7},{7,6},{8,9},{9,8},{10,11... | collective-permute-start | bytes 2064392 | tf_op jit(solution)/shard_map/ppermute | solution.py:1626
  127.3 32.1 %collective-permute-start.3 = (bf16[4,48,768]{2,1,0:T(8,128)(2,1)S(1)}, bf16[4,48,768]{2,1,0:T(8,128)(2,1)S(1)}, u32[]{:S(2)}, u32[]{:S(2)}) collective-permute-start(bf16[4,48,768]{2,1,0:T(8,128)(2,1)S(1)} %get-tuple-element.77), channel_id=1, source_target_pairs={{0,5},{1,4},{4,1},{5,0},{2,7},{3,6},{6,3},{7,2},{8,13},{9,12},{12,... | collective-permute-start | bytes 884744 | tf_op jit(solution)/shard_map/ppermute | solution.py:1627
  158.5 0.8 copy-start.8
  159.3 0.7 copy-start.17
  159.3 0.9 copy-start.14
  159.4 1.3 copy-start.15
  257.9 10.6 %copy-start.16 = (f32[256,768]{1,0:T(8,128)S(1)}, f32[256,768]{1,0:T(8,128)}, u32[]{:S(2)}) copy-start(f32[256,768]{1,0:T(8,128)} %get-tuple-element.121) | copy-start | bytes 2359300

commit v10 on v9

--- a/solution.py
+++ b/solution.py
@@ -1477,7 +1477,7 @@
             dma((6,)), dma((6,)), dma((10,)), dma((10,)), dma((1,)),
         ],
         compiler_params=pltpu.CompilerParams(
-            collective_id=2, has_side_effects=True, vmem_limit_bytes=54 << 20
+            collective_id=2, has_side_effects=True, vmem_limit_bytes=47 << 20
         ),
         name="scatter",
     )(dkv, dq, normed, wfull, tokens, mgrad, keep, over, near, far, small, sums)
@@ -1578,7 +1578,7 @@
             spec((base.shape[0] // PARTS, width), lambda p: (p, 0)),
         ),
         compiler_params=pltpu.CompilerParams(
-            vmem_limit_bytes=VMEM_LIMIT, dimension_semantics=("arbitrary",)
+            vmem_limit_bytes=50 << 20, dimension_semantics=("arbitrary",)
         ),
         name="lay_out",
     )(big, query, kv, sums, base, got)
@@ -1632,7 +1632,7 @@
     dkv = dkv.reshape(2, 2, 2, GROUPS, rows, 2 * HW)
     dq = dq.reshape(GROUPS, rows, 2 * BLK)
     grad_tokens, big, query_own, kv_own, sums = scatter(
-        *stay(dkv, dq, normed, wfull, tokens, grad_middle), small, *stay(kept_part, over, x_got, far), sums
+        *stay(dkv), dq, *stay(normed, wfull, tokens, grad_middle), small, *stay(kept_part), over, x_got, far, sums
     )
     if wide:
         big, query_own, kv_own, sums = (

time: 270 us -> 266 us (0.985); the launches traced: 269 us -> 261 us
  Pallas kernels: 257 us -> 251 us
    pallas_call x1, Pallas kernels: 97.3 us -> 89.8 us  [scatter(): pl.pallas_call(scatter_kernel, out_shape=(jax.ShapeDtypeStruct(full, f32)...]
    pallas_call x1, Pallas kernels: 18.3 us -> 21.1 us  [attend_forward(): pl.pallas_call(forward_kernel, out_shape=(jax.ShapeDtypeStruct((slots, HW...]
    unnamed x37 -> x25, local copies, waits for them, and re-layouts: 6.06 us -> 4.02 us
  transfers between devices with their start and end apart: 4 -> 4, of which waited for: 0 -> 0; matrix products, arithmetic and copies ran while one was open for 0% -> 0% of each run, Pallas kernels for 18% -> 20%
where the time goes in v10:
time: 266 us; the launch traced here: 261 us
  Pallas kernels  251 us (94%)
  local copies, waits for them, and re-layouts  5.35 us (2%)
  starting transfers between devices  4.1 us (2%)
    pallas_call x1, Pallas kernels, scatter(): pl.pallas_call(scatter_kernel, out_shape=(jax.ShapeDtypeStruct(full, f32)...  89.8 us
    pallas_call x1, Pallas kernels, gather(): pl.pallas_call(gather_kernel, out_shape=(jax.ShapeDtypeStruct((8, GROUPS,...  52.5 us
    pallas_call x1, Pallas kernels, dense(): pl.pallas_call(dense_kernel, out_shape=(jax.ShapeDtypeStruct(full, f32),...  46.3 us
    pallas_call x1, Pallas kernels, attend_backward(): pl.pallas_call(backward_kernel, out_shape=(jax.ShapeDtypeStruct((slots, B...  31.3 us
    pallas_call x1, Pallas kernels, attend_forward(): pl.pallas_call(forward_kernel, out_shape=(jax.ShapeDtypeStruct((slots, HW...  21.1 us
    pallas_call x1, Pallas kernels, lay_out(): pl.pallas_call(layout_kernel, grid=(PARTS,), out_shape=(jax.ShapeDtypeStr...  9.72 us
  transfers between devices with their start and end apart: 4, of which 0 were waited for; matrix products, arithmetic and copies ran while one was open for 0% of the time, Pallas kernels for 20%

profile of v10, /device:TPU:0, one launch (start us, length us, event | category | flops | bytes accessed | tf_op | source)
XLA Modules:
  0.0 261.1 jit_solution(1557970235429838677)
XLA Ops:
  0.7 1.3 constant_dynamic-slice_fusion
  2.0 52.5 %gather.1 = (bf16[8,4,256,384]{3,2,1,0:T(8,128)(2,1)S(1)}, bf16[4,256,256]{2,1,0:T(8,128)(2,1)S(1)}, bf16[4,256,768]{2,1,0:T(8,128)(2,1)S(1)}, f32[16,768]{1,0:T...) custom-call(bf16[256,768]{1,0:T(8,128)(2,1)} %tokens_any.1, bf16[384,768]{1,0:T(8,128)(2,1)} %query_any.1, ...), custom_call_target="tpu_custom_call" | custom-call | tf_op jit(solution)/shard_map/gather/pallas_call | solution.py:662
  54.6 0.0 copy-start.3
  54.6 1.1 copy-done.3
  55.7 1.0 copy-done.4
  56.7 0.9 copy-done.6
  57.7 0.6 collective-permute-start
  58.2 0.0 copy-done.11
  58.2 21.1 %attend_forward.1 = (bf16[8,192,128]{2,1,0:T(8,128)(2,1)S(1)}, f32[8,192,128]{2,1,0:T(8,128)S(1)}, f32[8,1,384]{2,1,0:T(1,128)S(1)}) custom-call(s32[64]{0:T(128)S(1)} %copy-done.10, s32[4]{0:T(128)S(1)} %copy-done.11, bf16[8,128,256]{2,1,0:T(8,128)(2,1)S(1)} %bitcast.12, bf16[64,128,384]{2,1,0:T(8,128)(2,1)S(1)} %bitcast.10), custom_call_target="tpu_custom_call" | custom-call | tf_op jit(solution)/shard_map/attend_forward/pallas_call | solution.py:180
  79.3 0.0 collective-permute-done.up_other
  79.4 46.3 %dense.1 = (f32[256,768]{1,0:T(8,128)S(1)}, bf16[448,768]{1,0:T(8,128)(2,1)S(1)}, f32[256,768]{1,0:T(8,128)S(1)}, bf16[8,192,128]{2,1,0:T(8,128)(2,1)S(1)}, bf16...) custom-call(bf16[8,192,128]{2,1,0:T(8,128)(2,1)S(1)} %get-tuple-elem, ...), custom_call_target="tpu_custom_call" | custom-call | tf_op jit(solution)/shard_map/dense/pallas_call | solution.py:960
  125.7 0.0 copy-start.5
  125.7 0.0 copy-start.8
  125.7 1.6 collective-permute-start.1
  127.3 0.0 collective-permute-start.2
  127.3 1.9 collective-permute-start.3
  129.3 31.3 %attend_backward.1 = (bf16[8,128,256]{2,1,0:T(8,128)(2,1)S(1)}, bf16[64,128,384]{2,1,0:T(8,128)(2,1)}) custom-call(s32[64]{0:T(128)S(1)} %copy-done.10, s32[4]{0:T(128)S(1)} %copy-done.11, bf16[8,128,256]{2,1,0:T(8,128)(2,1)S(1)} %bitcast.13, bf16[64,128,384]{2,1,0:T(8,128)(2,1)} %bitcast.11, f32[8,1,384]{2,1,0:T(1,128)S(1)} %get-tuple-element.62.lse_ref, ...), custom_call_target="tpu_custom_call" | custom-call | tf_op jit(solution)/shard_map/attend_backward/pallas_call | solution.py:324
  160.6 0.0 collective-permute-done.3.far_any
  160.6 0.0 collective-permute-done.2.near_any.got_ref
  160.6 0.0 collective-permute-done.1.over_any
  160.7 89.8 %scatter.1 = (f32[256,768]{1,0:T(8,128)S(1)}, bf16[2,2,4,216,768]{4,3,2,1,0:T(8,128)(2,1)}, bf16[2,4,192,256]{3,2,1,0:T(8,128)(2,1)S(1)}, bf16[2,4,192,384]{3,2,1,0:T(8,128)(2,1)S(1)}, f32[24,768]{1,0:T(8,128)S(1)}) custom-call(bf16[2,2,2,4,256,384]{5,4,3,2,1,0:T(8,128)(2,1)} %bitcast.15, bf16[4,256,256]{2,1,0:T(8,128)(2,1)S(1)} %bitcast.14, ...), custom_call_target="tpu_custom_call" | custom-call | tf_op jit(solution)/shard_map/scatter/pallas_call | solution.py:1429
  250.5 0.0 copy-done.2
  250.5 9.7 %lay_out.1 = (f32[384,3072]{1,0:T(8,128)}, f32[2,768,768]{2,1,0:T(8,128)}, f32[2,192,768]{2,1,0:T(8,128)}, f32[2,192,768]{2,1,0:T(8,128)}, f32[2,192,768]{2,1,0:...) custom-call(bf16[2,8,216,768]{3,2,1,0:T(8,128)(2,1)} %bitcast.16, ...), custom_call_target="tpu_custom_call" | custom-call | tf_op jit(solution)/shard_map/lay_out/pallas_call | solution.py:1551
  260.2 0.9 copy.37
  (16 shorter events, 0.0 us)
Async XLA Ops:
  0.7 57.6 %copy-start.10 = (s32[64]{0:T(128)S(1)}, s32[64]{0:T(128)}, u32[]{:S(2)}) copy-start(s32[64]{0:T(128)} %deal_ref.3) | copy-start | bytes 772
  0.7 57.5 %copy-start.11 = (s32[4]{0:T(128)S(1)}, s32[4]{0:T(128)}, u32[]{:S(2)}) copy-start(s32[4]{0:T(128)} %lengths_ref.3) | copy-start | bytes 52
  54.6 1.1 copy-start.3
  55.7 1.0 copy-start.4
  56.7 0.9 copy-start.6
  57.7 21.7 %copy-start = (bf16[8,4,256,384]{3,2,1,0:T(8,128)(2,1)}, bf16[8,4,256,384]{3,2,1,0:T(8,128)(2,1)S(1)}, u32[]{:S(2)}) copy-start(bf16[8,4,256,384]{3,2,1,0:T(8,128)(2,1)S(1)} %get-tuple-element.60) | copy-start | bytes 18874372
  57.7 21.7 %collective-permute-start = (bf16[384,768]{1,0:T(8,128)(2,1)S(1)}, bf16[384,768]{1,0:T(8,128)(2,1)S(1)}, u32[]{:S(2)}, u32[]{:S(2)}) collective-permute-start(bf16[384,768]{1,0:T(8,128)(2,1)S(1)} %get-tuple-element.66), channel_id=1, source_target_pairs={{0,1},{1,0},{2,3},{3,2},{4,5},{5,4},{6,7},{7,6},{8,9},{9,8},{10,11... | collective-permute-start | bytes 1769480 | tf_op jit(solution)/shard_map/ppermute | solution.py:1620
  58.2 21.1 %copy-start.1 = (bf16[256,768]{1,0:T(8,128)(2,1)S(1)}, bf16[256,768]{1,0:T(8,128)(2,1)}, u32[]{:S(2)}) copy-start(bf16[256,768]{1,0:T(8,128)(2,1)} %tokens_any.1) | copy-start | bytes 1179652
  58.2 21.1 %copy-start.9 = (bf16[256,768]{1,0:T(8,128)(2,1)S(1)}, bf16[256,768]{1,0:T(8,128)(2,1)}, u32[]{:S(2)}) copy-start(bf16[256,768]{1,0:T(8,128)(2,1)} %cot_ref.1) | copy-start | bytes 1179652
  125.7 34.9 %copy-start.5 = (bf16[4,168,768]{2,1,0:T(8,128)(2,1)}, bf16[4,168,768]{2,1,0:T(8,128)(2,1)S(1)}, u32[]{:S(2)}) copy-start(bf16[4,168,768]{2,1,0:T(8,128)(2,1)S(1)} %get-tuple-element.74.keep_any) | copy-start | bytes 3096580
  125.7 34.9 %copy-start.7 = (f32[256,768]{1,0:T(8,128)}, f32[256,768]{1,0:T(8,128)S(1)}, u32[]{:S(2)}) copy-start(f32[256,768]{1,0:T(8,128)S(1)} %get-tuple-element.83.base_ref) | copy-start | bytes 2359300
  125.7 34.9 %copy-start.8 = (f32[256,768]{1,0:T(8,128)}, f32[256,768]{1,0:T(8,128)S(1)}, u32[]{:S(2)}) copy-start(f32[256,768]{1,0:T(8,128)S(1)} %get-tuple-element.73.mgrad_any) | copy-start | bytes 2359300
  125.7 34.9 %collective-permute-start.1 = (bf16[4,168,768]{2,1,0:T(8,128)(2,1)S(1)}, bf16[4,168,768]{2,1,0:T(8,128)(2,1)S(1)}, u32[]{:S(2)}, u32[]{:S(2)}) collective-permute-start(bf16[4,168,768]{2,1,0:T(8,128)(2,1)S(1)} %get-tuple-element.75), channel_id=1, source_target_pairs={{0,4},{4,0},{1,5},{5,1},{2,6},{6,2},{3,7},{7,3},{8,12},{12,8},{9,1... | collective-permute-start | bytes 3096584 | tf_op jit(solution)/shard_map/ppermute | solution.py:1625
  127.3 33.3 %collective-permute-start.2 = (bf16[448,768]{1,0:T(8,128)(2,1)S(1)}, bf16[448,768]{1,0:T(8,128)(2,1)S(1)}, u32[]{:S(2)}, u32[]{:S(2)}) collective-permute-start(bf16[448,768]{1,0:T(8,128)(2,1)S(1)} %get-tuple-element.76), channel_id=1, source_target_pairs={{0,1},{1,0},{2,3},{3,2},{4,5},{5,4},{6,7},{7,6},{8,9},{9,8},{10,11... | collective-permute-start | bytes 2064392 | tf_op jit(solution)/shard_map/ppermute | solution.py:1626
  127.3 33.3 %collective-permute-start.3 = (bf16[4,48,768]{2,1,0:T(8,128)(2,1)S(1)}, bf16[4,48,768]{2,1,0:T(8,128)(2,1)S(1)}, u32[]{:S(2)}, u32[]{:S(2)}) collective-permute-start(bf16[4,48,768]{2,1,0:T(8,128)(2,1)S(1)} %get-tuple-element.77), channel_id=1, source_target_pairs={{0,5},{1,4},{4,1},{5,0},{2,7},{3,6},{6,3},{7,2},{8,13},{9,12},{12,... | collective-permute-start | bytes 884744 | tf_op jit(solution)/shard_map/ppermute | solution.py:1627
  160.6 89.8 %copy-start.2 = (bf16[448,768]{1,0:T(8,128)(2,1)}, bf16[448,768]{1,0:T(8,128)(2,1)S(1)}, u32[]{:S(2)}) copy-start(bf16[448,768]{1,0:T(8,128)(2,1)S(1)} %collective-permute-done.2.near_any.got_ref) | copy-start | bytes 2064388
